TPU v7x, 32 devices: a whole 2x2x4 slice. The times are simulated.
32 devices in a mesh: wide: 8 (over z, y), narrow: 4 (over x, core).
Axes of the slice: x: 2, y: 2, z: 4, core: 2. Of those that a mesh axis runs over, the one named last changes fastest.
Arguments:
- charges: bfloat16 [4, 192, 64, 64], P('narrow', 'wide'), may hold values from -6 to 6
- leaf_row_basis: bfloat16 [4, 192, 64, 64], P('narrow', 'wide'), may hold values from -0.75 to 0.75
- leaf_column_basis: bfloat16 [4, 192, 64, 64], P('narrow', 'wide'), may hold values from -0.75 to 0.75
- near_blocks: bfloat16 [4, 192, 8, 64, 64], P('narrow', 'wide'), may hold values from -0.75 to 0.75
- near_src: int32 [4, 192, 8], P('narrow', 'wide'), may hold values from 0 to 191, as said below
- near_count: int32 [4, 192], P('narrow', 'wide'), may hold values from 2 to 8, as said below
- leaf_coupling: bfloat16 [4, 192, 6, 64, 64], P('narrow', 'wide'), may hold values from -0.75 to 0.75
- far_src: int32 [4, 192, 6], P('narrow', 'wide'), may hold values from 0 to 191, as said below
- up_leaf: bfloat16 [4, 192, 64, 64], P('narrow', 'wide'), may hold values from -0.375 to 0.375
- column_transfer_leaf: bfloat16 [4, 192, 64, 64], P('narrow', 'wide'), may hold values from -0.75 to 0.75
- mid_coupling: bfloat16 [4, 48, 6, 64, 64], P('narrow', 'wide'), may hold values from -0.75 to 0.75
- mid_src: int32 [4, 48, 6], P('narrow', 'wide'), may hold values from 0 to 47, as said below
- up_mid: bfloat16 [4, 48, 64, 64], P('narrow', 'wide'), may hold values from -0.3125 to 0.3125
- down_mid: bfloat16 [4, 48, 64, 64], P('narrow', 'wide'), may hold values from -0.75 to 0.75
- up_top: bfloat16 [4, 8, 64, 64], P('narrow', 'wide'), may hold values from -0.25 to 0.25
- down_top: bfloat16 [4, 8, 64, 64], P('narrow', 'wide'), may hold values from -0.75 to 0.75
- top_coupling: bfloat16 [4, 4, 64, 64], P('narrow'), may hold values from -0.75 to 0.75
Outputs:
- sensitivity: bfloat16 [4, 192, 64, 64], P('narrow', 'wide')
Inputs may be any that keep to these rules, and one draw needn't show every extreme that they name: near_src[g, i, 0] is i itself, and every entry differs from i by at most 8; some entry differs by exactly 8. Leaf i uses the first near_count[g, i] slots of its near-field list. `far_src`: every entry differs from its leaf i by 2 to 8. `mid_src`: every entry differs from its mid-level cluster m by 2 to 6.
All inputs are finite; a program needn't handle non-finite values.
Results may differ from a plain program's by a relative error of at most 0.009.
Values may be sent and summed in bfloat16 or wider, within the bound.
No kernel may reach another device: no remote copies, remote signals or barrier semaphores. Data moves between devices by JAX's collectives and lax.ppermute only.
A program may use at most 64 MiB of HBM per device.

v0:
```python
import jax
import jax.numpy as jnp
from jax import lax
from jax.sharding import PartitionSpec as P


def padded_2(cells, sides, width):
    for axis, dim in sides:
        count = lax.axis_size(axis)
        ends = count - 1
        head = lax.slice_in_dim(cells, 0, width, axis=dim)
        tail = lax.slice_in_dim(cells, cells.shape[dim] - width, cells.shape[dim], axis=dim)
        cells = jnp.concatenate(
            [
                lax.ppermute(tail, axis, [(i, (i + 1) % count) for i in range(ends)]),
                cells,
                lax.ppermute(head, axis, [((i + 1) % count, i) for i in range(ends)]),
            ],
            axis=dim,
        )
    return cells


def on_device(
    charges,
    leaf_row_basis,
    leaf_column_basis,
    near_blocks,
    near_src,
    near_count,
    leaf_coupling,
    far_src,
    up_leaf,
    column_transfer_leaf,
    mid_coupling,
    mid_src,
    up_mid,
    down_mid,
    up_top,
    down_top,
    top_coupling,
):
    leaf_count = charges.shape[1]
    leaf_size = charges.shape[2]
    mid_count = leaf_count // 4
    slot_count = near_src.shape[2]
    position = lax.axis_index("wide")
    my_group = lax.axis_index("narrow")
    group_count = lax.axis_size("narrow")
    rank_size = leaf_row_basis.shape[3]
    rhs_size = charges.shape[3]
    skeleton_leaf = jnp.einsum(
        "mwl,mwv->mlv", leaf_row_basis[0], charges[0], preferred_element_type=jnp.float32
    ).astype(jnp.bfloat16)
    skel_mid = jnp.einsum(
        "mqab,mqac->mbc",
        up_leaf[0].reshape(mid_count, 4, rank_size, rank_size),
        skeleton_leaf.reshape(mid_count, 4, rank_size, rhs_size),
        preferred_element_type=jnp.float32,
    ).astype(jnp.bfloat16)
    skel_dev = jnp.einsum(
        "mab,mac->bc", up_mid[0], skel_mid, preferred_element_type=jnp.float32
    ).astype(jnp.bfloat16)
    dev_term = jnp.einsum("ab,ac->bc", up_top[0, 0], skel_dev, preferred_element_type=jnp.float32)
    group_total = lax.psum(dev_term, "wide").astype(jnp.bfloat16)
    every_group = lax.all_gather(group_total[None], "narrow", axis=0, tiled=True)
    charge_cols = leaf_size * rhs_size
    skel_cols = rank_size * rhs_size
    packed = jnp.concatenate(
        [
            charges[0].reshape(leaf_count, charge_cols),
            skeleton_leaf.reshape(leaf_count, skel_cols),
            skel_mid.reshape(leaf_count, skel_cols // 4),
        ],
        axis=1,
    )
    received = padded_2(packed[None], (("wide", 1),), leaf_count)[0]
    padded = received[:, :charge_cols].reshape(3 * leaf_count, leaf_size, rhs_size)
    leaf_padded = received[:, charge_cols : charge_cols + skel_cols].reshape(
        3 * leaf_count, rank_size, rhs_size
    )
    mid_padded = received[:, charge_cols + skel_cols :].reshape(3 * mid_count, rank_size, rhs_size)
    first_leaf = position * leaf_count - leaf_count
    other_groups = jnp.arange(group_count, dtype=jnp.int32) != my_group
    masked_groups = jnp.where(other_groups[:, None, None], every_group, jnp.zeros((), jnp.bfloat16))
    top_part = jnp.einsum(
        "hab,hac->bc", top_coupling[0], masked_groups, preferred_element_type=jnp.float32
    ).astype(jnp.bfloat16)
    down_dev = jnp.dot(down_top[0, 0], top_part, preferred_element_type=jnp.float32).astype(
        jnp.bfloat16
    )
    mid_gathered = jnp.take(mid_padded, mid_src[0] - (position * mid_count - mid_count), axis=0)
    middle_downward_pass = (
        jnp.einsum(
            "jkab,jkac->jbc", mid_coupling[0], mid_gathered, preferred_element_type=jnp.float32
        )
        + jnp.einsum("jab,bc->jac", down_mid[0], down_dev, preferred_element_type=jnp.float32)
    ).astype(jnp.bfloat16)
    leaf_gathered = jnp.take(leaf_padded, far_src[0] - first_leaf, axis=0)
    leaf_downward_pass = (
        jnp.einsum(
            "tkab,tkac->tbc", leaf_coupling[0], leaf_gathered, preferred_element_type=jnp.float32
        )
        + jnp.einsum(
            "ruy,ryv->ruv",
            column_transfer_leaf[0],
            jnp.repeat(middle_downward_pass, 4, axis=0),
            preferred_element_type=jnp.float32,
        )
    ).astype(jnp.bfloat16)
    gathered = jnp.take(padded, near_src[0] - first_leaf, axis=0)
    live_slot = jnp.arange(slot_count, dtype=jnp.int32)[None, :] < near_count[0][:, None]
    gathered = jnp.where(live_slot[:, :, None, None], gathered, jnp.zeros((), jnp.bfloat16))
    near_part = jnp.einsum(
        "tkab,tkac->tbc", near_blocks[0], gathered, preferred_element_type=jnp.float32
    )
    far_field_part = jnp.einsum(
        "eiu,eug->eig", leaf_column_basis[0], leaf_downward_pass, preferred_element_type=jnp.float32
    )
    return (near_part + far_field_part).astype(jnp.bfloat16)[None]


def solution(mesh):
    return jax.shard_map(
        on_device,
        mesh=mesh,
        in_specs=(
            P("narrow", "wide", None, None),
            P("narrow", "wide", None, None),
            P("narrow", "wide", None, None),
            P("narrow", "wide", None, None, None),
            P("narrow", "wide", None),
            P("narrow", "wide"),
            P("narrow", "wide", None, None, None),
            P("narrow", "wide", None),
            P("narrow", "wide", None, None),
            P("narrow", "wide", None, None),
            P("narrow", "wide", None, None, None),
            P("narrow", "wide", None),
            P("narrow", "wide", None, None),
            P("narrow", "wide", None, None),
            P("narrow", "wide", None, None),
            P("narrow", "wide", None, None),
            P("narrow", None, None, None),
        ),
        out_specs=P("narrow", "wide", None, None),
        check_vma=False,
    )
```

profile of v0, /device:TPU:0, one launch (start us, length us, event | category | flops | bytes accessed | tf_op | source)
XLA Modules:
  0.0 113.8 jit_solution(15665633021091207519)
XLA Ops:
  0.0 2.2 %reshape_squeeze.6 = bf16[24,4096]{1,0:T(8,128)(2,1)} reshape(bf16[1,24,64,64]{3,2,1,0:T(8,128)(2,1)} %param.17) | data formatting | bytes 393216 | tf_op jit(solution)/shard_map/reshape;squeeze | solution.py:71
  2.2 1.4 %convolution_convert_fusion = bf16[24,64,64]{2,1,0:T(8,128)(2,1)S(1)} fusion(bf16[1,24,64,64]{3,2,1,0:T(8,128)(2,1)} %param.17, bf16[1,24,64,64]{3,2,1,0:T(8,128)(2,1)} %param.18), kind=kOutput, calls=%fused_computation.22 | convolution fusion | flops 12681216 | bytes 589824 | tf_op jit(solution)/shard_map/mwl,mwv->mlv/dot_general | solution.py:52
  4.7 1.9 %fusion.29 = bf16[6,64,64]{1,2,0:T(8,128)(2,1)} fusion(bf16[6,4,64,64]{3,2,1,0:T(8,128)(2,1)S(1)} %bitcast.130, bf16[6,4,64,64]{3,2,1,0:T(8,128)(2,1)} %bitcast.133), kind=kOutput, calls=%fused_computation.31 | convolution fusion | flops 12607488 | bytes 442368 | tf_op jit(solution)/shard_map/mqab,mqac->mbc/dot_general | solution.py:55
  7.7 1.8 %maximum_bitcast_fusion.1 = bf16[1,24,9216]{2,1,0:T(8,128)(2,1)} fusion(bf16[24,1024]{1,0:T(8,128)(2,1)S(1)} %reshape.138, bf16[24,4096]{1,0:T(8,128)(2,1)} %reshape.136, bf16[24,4096]{1,0:T(8,128)(2,1)} %reshape_squeeze.6), kind=kLoop, calls=%fused_computation.42 | loop fusion | flops 1327104 | bytes 884736 | tf_op jit(solution)/shard_map/broadcast_in_dim | solution.py:77
  9.6 1.3 %collective-permute-start.1 = (bf16[1,24,9216]{2,1,0:T(8,128)(2,1)}, bf16[1,24,9216]{2,1,0:T(8,128)(2,1)}, u32[]{:S(2)}, u32[]{:S(2)}) collective-permute-start(bf16[1,24,9216]{2,1,0:T(8,128)(2,1)} %maximum_bitcast_fusion.1), channel_id=1, source_target_pairs={{4,0},{8,4},{12,8},{16,12},{20,16},{24,20},{28,24},{5,1},{9,5},{13... | collective-permute-start | bytes 1327112 | tf_op jit(solution)/shard_map/ppermute | solution.py:17
  10.8 6.3 %collective-permute-start = (bf16[1,24,9216]{2,1,0:T(8,128)(2,1)}, bf16[1,24,9216]{2,1,0:T(8,128)(2,1)}, u32[]{:S(2)}, u32[]{:S(2)}) collective-permute-start(bf16[1,24,9216]{2,1,0:T(8,128)(2,1)} %maximum_bitcast_fusion.1), channel_id=1, source_target_pairs={{0,4},{4,8},{8,12},{12,16},{16,20},{20,24},{24,28},{1,5},{5,9},{9,... | collective-permute-start | bytes 1327112 | tf_op jit(solution)/shard_map/ppermute | solution.py:15
  17.9 1.3 %convolution_bitcast_fusion.4 = f32[64,64]{0,1:T(8,128)S(1)} fusion(bf16[6,64,64]{1,2,0:T(8,128)(2,1)} %fusion.29, bf16[1,6,64,64]{3,2,1,0:T(8,128)(2,1)} %param.29, bf16[1,1,64,64]{3,2,1,0:T(8,128)(2,1)} %param.31), kind=kOutput, calls=%fused_computation.33 | convolution fusion | flops 3674112 | bytes 122880 | tf_op jit(solution)/shard_map/ab,ac->bc/dot_general | solution.py:64
  19.2 43.5 %psum.7 = bf16[64,64]{0,1:T(8,128)(2,1)S(1)} all-reduce(f32[64,64]{0,1:T(8,128)S(1)} %convolution_bitcast_fusion.4), channel_id=1, replica_groups=mesh['wide'=8,'narrow'=4] {'wide'}, use_global_device_ids=true, to_apply=%region_0.0 | all-reduce | flops 4096 | bytes 24576 | tf_op jit(solution)/shard_map/psum | solution.py:65
  62.8 5.2 %all-gather = bf16[256,64]{1,0:T(8,128)(2,1)S(1)} all-gather(bf16[64,64]{1,0:T(8,128)(2,1)S(1)} %copy.48), channel_id=2, replica_groups=mesh['wide'=8,'narrow'=4] {'narrow'}, dimensions={0}, use_global_device_ids=true | all-gather | bytes 40960 | tf_op jit(solution)/shard_map/all_gather | solution.py:66
  68.2 1.2 %fusion.32 = bf16[64,64,1]{1,0,2:T(8,128)(2,1)S(1)} fusion(bf16[1,4,64,64]{3,2,1,0:T(8,128)(2,1)} %param.33, bf16[4,64,64]{1,2,0:T(8,128)(2,1)S(1)} %copy.49, pred[4]{0:T(512)(128)(4,1)S(1)} %iota_compare_fusion.1, bf16[1,1,64,64]{3,2,1,0:T(8,128)(2,1)} %param.32), kind=kOutput, calls=%fused_computation.38 | convolution fusion | flops 2646016 | bytes 81924 | tf_op jit(solution)/shard_map/dot_general | solution.py:89
  69.5 1.4 %maximum_bitcast_fusion = bf16[72,9216]{1,0:T(8,128)(2,1)S(1)} fusion(bf16[1,24,9216]{2,1,0:T(8,128)(2,1)} %collective-permute-done.1, bf16[1,24,9216]{2,1,0:T(8,128)(2,1)} %maximum_bitcast_fusion.1, bf16[1,24,9216]{2,1,0:T(8,128)(2,1)} %collective-permute-done), kind=kLoop, calls=%fused_computation.15 | loop fusion | flops 3981312 | bytes 2654208 | tf_op jit(solution)/shard_map/squeeze | solution.py:77
  73.8 1.5 %gather_fusion.2 = bf16[36,64,64]{2,1,0:T(8,128)(2,1)} fusion(bf16[18,64,64]{2,1,0:T(8,128)(2,1)S(1)} %reshape.141, s32[1024]{0:T(1024)S(1)} %pad_clamp_fusion), kind=kCustom, calls=%fused_computation.2 | custom fusion | bytes 589968 | tf_op jit(solution)/shard_map/jit(_take)/gather | solution.py:92
  75.3 2.2 %copy.47 = bf16[6,6,64,64]{2,3,1,0:T(8,128)(2,1)} copy(bf16[6,6,64,64]{3,2,1,0:T(8,128)(2,1)} %bitcast.131) | data formatting | bytes 589824 | tf_op jit(solution)/shard_map/jit(_take)/gather | solution.py:92
  77.5 2.9 %reshape.140 = bf16[72,64,64]{2,1,0:T(8,128)(2,1)} reshape(bf16[72,4096]{1,0:T(8,128)(2,1)} %get-tuple-element.7) | data formatting | bytes 1179648 | tf_op jit(solution)/shard_map/reshape | solution.py:79
  80.4 3.7 %gather_fusion.1 = bf16[144,64,64]{2,1,0:T(8,128)(2,1)} fusion(bf16[72,64,64]{2,1,0:T(8,128)(2,1)} %reshape.140, s32[1024]{0:T(1024)S(1)} %pad_clamp_fusion.1), kind=kCustom, calls=%fused_computation.1 | custom fusion | bytes 2359872 | tf_op jit(solution)/shard_map/jit(_take)/gather | solution.py:99
  84.1 4.4 %copy.45 = bf16[24,6,64,64]{2,3,1,0:T(8,128)(2,1)} copy(bf16[24,6,64,64]{3,2,1,0:T(8,128)(2,1)} %bitcast.129) | data formatting | bytes 2359296 | tf_op jit(solution)/shard_map/jit(_take)/gather | solution.py:99
  88.5 2.9 %reshape.139 = bf16[72,64,64]{2,1,0:T(8,128)(2,1)} reshape(bf16[72,4096]{1,0:T(8,128)(2,1)} %get-tuple-element.8) | data formatting | bytes 1179648 | tf_op jit(solution)/shard_map/reshape | solution.py:78
  91.4 4.0 %gather_fusion = bf16[192,64,64]{2,1,0:T(8,128)(2,1)} fusion(bf16[72,64,64]{2,1,0:T(8,128)(2,1)} %reshape.139, s32[1024]{0:T(1024)S(1)} %pad_clamp_fusion.2), kind=kCustom, calls=%fused_computation | custom fusion | bytes 3146496 | tf_op jit(solution)/shard_map/jit(_take)/gather | solution.py:111
  95.4 4.7 %copy.42 = bf16[24,8,64,64]{2,3,1,0:T(8,128)(2,1)} copy(bf16[24,8,64,64]{3,2,1,0:T(8,128)(2,1)} %bitcast.128) | data formatting | bytes 3145728 | tf_op jit(solution)/shard_map/jit(_take)/gather | solution.py:111
  100.1 1.6 %convolution_bitcast_fusion.1 = f32[6,64,64]{1,2,0:T(8,128)S(1)} fusion(bf16[1,6,6,64,64]{4,3,2,1,0:T(8,128)(2,1)} %param.27, bf16[6,6,64,64]{2,3,1,0:T(8,128)(2,1)} %copy.47, pred[6,6]{1,0:T(8,128)(4,1)S(1)} %compare_and_fusion), kind=kOutput, calls=%fused_computation.26 | convolution fusion | flops 19021824 | bytes 688164 | tf_op jit(solution)/shard_map/jkab,jkac->jbc/dot_general | solution.py:94
  102.0 4.3 %fusion.12 = f32[24,64,64]{2,1,0:T(8,128)} fusion(bf16[1,24,6,64,64]{4,3,2,1,0:T(8,128)(2,1)} %param.23, bf16[24,6,64,64]{2,3,1,0:T(8,128)(2,1)} %copy.45, pred[24,6]{1,0:T(8,128)(4,1)S(1)} %copy.43), kind=kOutput, calls=%fused_computation.16 | convolution fusion | flops 76087296 | bytes 2752656 | tf_op jit(solution)/shard_map/tkab,tkac->tbc/dot_general | solution.py:101
  106.4 2.5 %fusion.17 = f32[24,64,64]{2,1,0:T(8,128)} fusion(bf16[1,24,8,64,64]{4,3,2,1,0:T(8,128)(2,1)S(1)} %copy-done, bf16[24,8,64,64]{2,3,1,0:T(8,128)(2,1)S(1)} %copy-done.1, pred[24,8]{1,0:T(8,128)(4,1)S(1)} %copy.37, pred[24,8]{1,0:T(8,128)(4,1)S(1)} %iota_compare_fusion), kind=kOutput, calls=%fused_computation.19 | convolution fusion | flops 102236160 | bytes 3539328 | tf_op jit(solution)/shard_map/tkab,tkac->tbc/dot_general | solution.py:114
  109.0 2.9 %fusion.24 = bf16[1,24,64,64]{2,3,1,0:T(8,128)(2,1)} fusion(f32[24,64,64]{2,1,0:T(8,128)} %fusion.17, f32[24,64,64]{2,1,0:T(8,128)} %fusion.12, bf16[24,64,64]{1,2,0:T(8,128)(2,1)S(1)} %bitcast.132, bf16[1,24,64,64]{3,2,1,0:T(8,128)(2,1)} %param.19, bf16[1,24,64,64]{3,2,1,0:T(8,128)(2,1)} %param.26), kind=kOutput, calls=%fused_computation.23 | convolution fusion | flops 25559040 | bytes 1572864 | tf_op jit(solution)/shard_map/eiu,eug->eig/dot_general | solution.py:117
  111.9 1.9 %copy.50 = bf16[1,24,64,64]{3,2,1,0:T(8,128)(2,1)} copy(bf16[1,24,64,64]{2,3,1,0:T(8,128)(2,1)} %fusion.24) | data formatting | bytes 393216 | tf_op jit(solution)/shard_map/broadcast_in_dim | solution.py:120
  (45 shorter events, 6.4 us)
Async XLA Ops:
  0.0 106.4 %copy-start = (bf16[1,24,8,64,64]{4,3,2,1,0:T(8,128)(2,1)S(1)}, bf16[1,24,8,64,64]{4,3,2,1,0:T(8,128)(2,1)}, u32[]{:S(2)}) copy-start(bf16[1,24,8,64,64]{4,3,2,1,0:T(8,128)(2,1)} %param.20) | copy-start | bytes 4718596
  0.0 17.2 %copy-start.3 = (s32[1,24,8]{1,2,0:T(8,128)S(1)}, s32[1,24,8]{1,2,0:T(8,128)}, u32[]{:S(2)}) copy-start(s32[1,24,8]{1,2,0:T(8,128)} %param.21) | copy-start | bytes 2308
  0.0 17.3 %copy-start.4 = (s32[1,6,6]{2,0,1:T(1,128)S(1)}, s32[1,6,6]{2,0,1:T(1,128)}, u32[]{:S(2)}) copy-start(s32[1,6,6]{2,0,1:T(1,128)} %param.28) | copy-start | bytes 436
  0.0 17.4 %copy-start.5 = (s32[1,24,6]{1,0,2:T(1,128)S(1)}, s32[1,24,6]{1,0,2:T(1,128)}, u32[]{:S(2)}) copy-start(s32[1,24,6]{1,0,2:T(1,128)} %param.24) | copy-start | bytes 1732
  2.2 67.2 %copy-start.6 = (s32[1,24]{1,0:T(1,128)S(1)}, s32[1,24]{1,0:T(1,128)}, u32[]{:S(2)}) copy-start(s32[1,24]{1,0:T(1,128)} %param.22) | copy-start | bytes 292
  9.6 59.9 %collective-permute-start.1 = (bf16[1,24,9216]{2,1,0:T(8,128)(2,1)}, bf16[1,24,9216]{2,1,0:T(8,128)(2,1)}, u32[]{:S(2)}, u32[]{:S(2)}) collective-permute-start(bf16[1,24,9216]{2,1,0:T(8,128)(2,1)} %maximum_bitcast_fusion.1), channel_id=1, source_target_pairs={{4,0},{8,4},{12,8},{16,12},{20,16},{24,20},{28,24},{5,1},{9,5},{13... | collective-permute-start | bytes 1327112 | tf_op jit(solution)/shard_map/ppermute | solution.py:17
  10.8 58.6 %collective-permute-start = (bf16[1,24,9216]{2,1,0:T(8,128)(2,1)}, bf16[1,24,9216]{2,1,0:T(8,128)(2,1)}, u32[]{:S(2)}, u32[]{:S(2)}) collective-permute-start(bf16[1,24,9216]{2,1,0:T(8,128)(2,1)} %maximum_bitcast_fusion.1), channel_id=1, source_target_pairs={{0,4},{4,8},{8,12},{12,16},{16,20},{20,24},{24,28},{1,5},{5,9},{9,... | collective-permute-start | bytes 1327112 | tf_op jit(solution)/shard_map/ppermute | solution.py:15
  95.4 6.3 %copy-start.2 = (bf16[1,6,64,64]{3,2,1,0:T(8,128)(2,1)S(1)}, bf16[1,6,64,64]{3,2,1,0:T(8,128)(2,1)}, u32[]{:S(2)}) copy-start(bf16[1,6,64,64]{3,2,1,0:T(8,128)(2,1)} %param.30) | copy-start | bytes 147460
  102.0 4.4 %copy-start.1 = (bf16[24,8,64,64]{2,3,1,0:T(8,128)(2,1)S(1)}, bf16[24,8,64,64]{2,3,1,0:T(8,128)(2,1)}, u32[]{:S(2)}) copy-start(bf16[24,8,64,64]{2,3,1,0:T(8,128)(2,1)} %copy.42) | copy-start | bytes 4718596
where the time goes:
time: 115 us; the launch traced here: 114 us
  blocking collectives  48.8 us (42%)
  local copies, waits for them, and re-layouts  36.4 us (32%)
  matrix products  17.5 us (15%)
  starting transfers between devices  7.6 us (7%)
  other arithmetic  3.34 us (3%)
    psum x1, blocking collectives, on_device(): group_total = lax.psum(dev_term, 'wide').astype(jnp.bfloat16)  43.5 us
    gather x2, local copies, waits for them, and re-layouts, on_device(): gathered = jnp.take(padded, near_src[0] - first_leaf, axis=0)  8.69 us
    gather x2, local copies, waits for them, and re-layouts, on_device(): leaf_gathered = jnp.take(leaf_padded, far_src[0] - first_leaf, axis=0)  8.07 us
    ppermute x1, starting transfers between devices, padded_2(): lax.ppermute(tail, axis, [(i, (i + 1) % count) for i in range(ends)])  6.32 us
    all_gather x1, blocking collectives, on_device(): lax.all_gather(group_total[None], 'narrow', axis=0, tiled=True)  5.24 us
    dot_general x1, matrix products, on_device(): jnp.einsum('tkab,tkac->tbc', leaf_coupling[0], leaf_gathered, preferred_e...  4.34 us
    gather x2, local copies, waits for them, and re-layouts, on_device(): jnp.take(mid_padded, mid_src[0] - (position * mid_count - mid_count), axi...  3.66 us
    reshape x1, local copies, waits for them, and re-layouts, on_device(): received[:, :charge_cols].reshape(3 * leaf_count, leaf_size, rhs_size)  2.93 us
  transfers between devices with their start and end apart: 2, of which 0 were waited for; matrix products, arithmetic and copies ran while one was open for 3% of the time, Pallas kernels for 0%

commit v1 on v0

v1 whole, which is shorter than its diff:
```python
import functools

import jax
import jax.numpy as jnp
from jax import lax
from jax.experimental import pallas as pl
from jax.experimental.pallas import tpu as pltpu
from jax.sharding import PartitionSpec as P

REACH = 8
MREACH = 6
F32 = jnp.float32
BF16 = jnp.bfloat16
NN = (((1,), (0,)), ((), ()))
NT = (((1,), (1,)), ((), ()))


def nn(a, b):
    return lax.dot_general(a, b, NN, preferred_element_type=F32)


def nt(a, b):
    return lax.dot_general(a, b, NT, preferred_element_type=F32)


def pack(a, b):
    return jnp.concatenate([a, b], axis=1)


def up_kernel(c_ref, r_ref, ul_ref, um_ref, ut_ref, ct_ref, st_ref, mt_ref, hl_ref, hr_ref, dt_ref):
    n = c_ref.shape[0]
    mids = um_ref.shape[0]
    w = c_ref.shape[1]
    eye = (
        lax.broadcasted_iota(jnp.int32, (w, w), 0) == lax.broadcasted_iota(jnp.int32, (w, w), 1)
    ).astype(F32).astype(BF16)
    dev = None
    for m in range(mids):
        acc = None
        for q in range(4):
            i = 4 * m + q
            ct = nt(eye, c_ref[i]).astype(BF16)
            ct_ref[i] = ct
            st = nn(ct, r_ref[i]).astype(BF16)
            st_ref[i] = st
            part = nn(st, ul_ref[i])
            acc = part if acc is None else acc + part
        mt = acc.astype(BF16)
        mt_ref[m] = mt
        part = nn(mt, um_ref[m])
        dev = part if dev is None else dev + part
    term = nn(dev.astype(BF16), ut_ref[0])
    h = term.shape[0] // 2
    dt_ref[...] = pack(term[:h], term[h:]).astype(BF16)
    half = REACH // 2
    for k in range(half):
        hl_ref[k] = pack(ct_ref[2 * k], ct_ref[2 * k + 1])
        hl_ref[half + k] = pack(st_ref[2 * k], st_ref[2 * k + 1])
        e = n - REACH + 2 * k
        hr_ref[k] = pack(ct_ref[e], ct_ref[e + 1])
        hr_ref[half + k] = pack(st_ref[e], st_ref[e + 1])
    for k in range(MREACH // 2):
        hl_ref[2 * half + k] = pack(mt_ref[2 * k], mt_ref[2 * k + 1])
        e = mids - MREACH + 2 * k
        hr_ref[2 * half + k] = pack(mt_ref[e], mt_ref[e + 1])


def unpack(ref, k, tab, at):
    both = ref[k]
    h = both.shape[1] // 2
    tab[at] = both[:, :h]
    tab[at + 1] = both[:, h:]


def far_kernel(
    ni_ref, fi_ref, mi_ref, ct_ref, st_ref, mt_ref, fl_ref, fr_ref, nb_ref, lc_ref, mc_ref,
    near_ref, lp_ref, mp_ref, ctab, stab, mtab,
):
    n = ct_ref.shape[0]
    mids = mt_ref.shape[0]
    half = REACH // 2
    for i in range(n):
        ctab[REACH + i] = ct_ref[i]
        stab[REACH + i] = st_ref[i]
    for i in range(mids):
        mtab[MREACH + i] = mt_ref[i]
    ctab[n + 2 * REACH] = jnp.zeros(ctab.shape[1:], BF16)
    for k in range(half):
        unpack(fl_ref, k, ctab, 2 * k)
        unpack(fl_ref, half + k, stab, 2 * k)
        unpack(fr_ref, k, ctab, n + REACH + 2 * k)
        unpack(fr_ref, half + k, stab, n + REACH + 2 * k)
    for k in range(MREACH // 2):
        unpack(fl_ref, 2 * half + k, mtab, 2 * k)
        unpack(fr_ref, 2 * half + k, mtab, mids + MREACH + 2 * k)

    @pl.loop(0, n)
    def _(i):
        acc = None
        for k in range(nb_ref.shape[1]):
            part = nn(ctab[ni_ref[i, k]], nb_ref[i, k])
            acc = part if acc is None else acc + part
        near_ref[i] = jnp.transpose(acc)
        acc = None
        for k in range(lc_ref.shape[1]):
            part = nn(stab[fi_ref[i, k]], lc_ref[i, k])
            acc = part if acc is None else acc + part
        lp_ref[i] = acc

    for j in range(mids):
        acc = None
        for k in range(mc_ref.shape[1]):
            part = nn(mtab[mi_ref[j, k]], mc_ref[j, k])
            acc = part if acc is None else acc + part
        mp_ref[j] = acc


def down_kernel(hs_ref, g_ref, tc_ref, dtop_ref, dm_ref, tl_ref, cb_ref, near_ref, lp_ref, mp_ref, out_ref):
    mids = dm_ref.shape[0]
    acc = None
    for k in range(g_ref.shape[0]):
        g = g_ref[k]
        h = g.shape[1] // 2
        gt = jnp.concatenate([g[:, :h], g[:, h:]], axis=0)
        part = nn(gt, tc_ref[hs_ref[k]])
        acc = part if acc is None else acc + part
    dd = nt(acc.astype(BF16), dtop_ref[0]).astype(BF16)
    for m in range(mids):
        md = (mp_ref[m] + nt(dd, dm_ref[m])).astype(BF16)
        for q in range(4):
            i = 4 * m + q
            ld = (lp_ref[i] + nt(md, tl_ref[i])).astype(BF16)
            out_ref[i] = (near_ref[i] + nt(cb_ref[i], ld)).astype(BF16)


def swap(pairs_of, count):
    return [(i, pairs_of(i)) for i in range(count)]


def on_device(
    charges, leaf_row_basis, leaf_column_basis, near_blocks, near_src, near_count, leaf_coupling, far_src,
    up_leaf, column_transfer_leaf, mid_coupling, mid_src, up_mid, down_mid, up_top, down_top, top_coupling,
):
    n, w, v = charges.shape[1:]
    r = leaf_row_basis.shape[3]
    mids = up_mid.shape[1]
    wide, narrow = lax.axis_size("wide"), lax.axis_size("narrow")
    both = ("wide", "narrow")
    total = wide * narrow
    pos = lax.axis_index("wide")
    me = lax.axis_index("narrow")
    pairs = REACH + MREACH // 2

    def shp(*s, t=BF16):
        return jax.ShapeDtypeStruct(s, t)

    ct, st, mt, hl, hr, term = pl.pallas_call(
        up_kernel,
        out_shape=[shp(n, v, w), shp(n, v, r), shp(mids, v, r), shp(pairs, v, 2 * r), shp(pairs, v, 2 * r), shp(v // 2, 2 * r)],
        compiler_params=pltpu.CompilerParams(vmem_limit_bytes=16 << 20),
        name="up",
    )(charges[0], leaf_row_basis[0], up_leaf[0], up_mid[0], up_top[0])

    from_left = lax.ppermute(hr, "wide", [(i, i + 1) for i in range(wide - 1)])
    from_right = lax.ppermute(hl, "wide", [(i + 1, i) for i in range(wide - 1)])

    def xor(x, dw, dn):
        return lax.ppermute(x, both, [(i * narrow + j, (i ^ dw) * narrow + (j ^ dn)) for i in range(wide) for j in range(narrow)])

    f = term.astype(F32)
    own = f + xor(term, 1, 0).astype(F32)
    other = xor(term, 0, 2).astype(F32) + xor(term, 1, 2).astype(F32)
    have = jnp.stack([own, other]).astype(BF16)
    bit = 2
    while bit < wide:
        got = have.astype(F32) + xor(have, bit, 0).astype(F32)
        if 2 * bit < wide:
            got = got + xor(have, 2 * bit, 0).astype(F32) + xor(have, 3 * bit, 0).astype(F32)
        have = got.astype(BF16)
        bit *= 4
    over = xor(have, 0, 1)
    groups = jnp.concatenate([have[1:], over], axis=0)
    hs = jnp.stack([me ^ 2, me ^ 1, me ^ 3]).astype(jnp.int32)

    live = jnp.arange(near_src.shape[2], dtype=jnp.int32)[None, :] < near_count[0][:, None]
    ni = jnp.where(live, near_src[0] - (pos * n - REACH), n + 2 * REACH)
    fi = far_src[0] - (pos * n - REACH)
    mi = mid_src[0] - (pos * mids - MREACH)

    smem = pl.BlockSpec(memory_space=pltpu.SMEM)
    vm = pl.BlockSpec(memory_space=pltpu.VMEM)
    near, lp, mp = pl.pallas_call(
        far_kernel,
        in_specs=[smem] * 3 + [vm] * 8,
        out_shape=[shp(n, w, v, t=F32), shp(n, v, r, t=F32), shp(mids, v, r, t=F32)],
        scratch_shapes=[
            pltpu.VMEM((n + 2 * REACH + 1, v, w), BF16),
            pltpu.VMEM((n + 2 * REACH, v, r), BF16),
            pltpu.VMEM((mids + 2 * MREACH, v, r), BF16),
        ],
        compiler_params=pltpu.CompilerParams(vmem_limit_bytes=32 << 20),
        name="far",
    )(ni, fi, mi, ct, st, mt, from_left, from_right, near_blocks[0], leaf_coupling[0], mid_coupling[0])

    out = pl.pallas_call(
        down_kernel,
        in_specs=[smem] + [vm] * 9,
        out_shape=shp(n, w, v),
        compiler_params=pltpu.CompilerParams(vmem_limit_bytes=16 << 20),
        name="down",
    )(hs, groups, top_coupling[0], down_top[0], down_mid[0], column_transfer_leaf[0], leaf_column_basis[0], near, lp, mp)
    return out[None]


def solution(mesh):
    leaf = P("narrow", "wide", None, None)
    block = P("narrow", "wide", None, None, None)
    lists = P("narrow", "wide", None)
    return jax.shard_map(
        on_device,
        mesh=mesh,
        in_specs=(
            leaf, leaf, leaf, block, lists, P("narrow", "wide"), block, lists,
            leaf, leaf, block, lists, leaf, leaf, leaf, leaf, P("narrow", None, None, None),
        ),
        out_specs=leaf,
        check_vma=False,
    )
```

time: 115 us -> 50.7 us (0.44)
  blocking collectives: 48.8 us -> 0 us
  local copies, waits for them, and re-layouts: 36.4 us -> 10.8 us
  matrix products: 17.5 us -> 0 us
  Pallas kernels: 0 us -> 15.7 us
  starting transfers between devices: 7.6 us -> 16.1 us
  waiting for transfers between devices: 0.01 us -> 5.95 us
  other arithmetic: 3.34 us -> 1.53 us
    psum x1 -> x0, blocking collectives: 43.5 us -> none  [on_device(): group_total = lax.psum(dev_term, 'wide').astype(jnp.bfloat16)]
    gather x6 -> x0, local copies, waits for them, and re-layouts: 20.4 us -> none  [the longest x2 8.69 us: on_device(): gathered = jnp.take(padded, near_src[0] - first_leaf, axis=0)]
    dot_general x9 -> x0, matrix products: 17.5 us -> none  [the longest x1 4.34 us: on_device(): jnp.einsum('tkab,tkac->tbc', leaf_coupling[0], leaf_gathered, preferred_e...]
    pallas_call x0 -> x3, Pallas kernels: none -> 15.7 us  [the longest x1 8.45 us: on_device(): pl.pallas_call(far_kernel, in_specs=[smem] * 3 + [vm] * 8, out_shape=[shp...]
    unnamed x14 -> x28, local copies, waits for them, and re-layouts: 0.03 us -> 10.8 us
    ppermute x2 -> x9, starting transfers between devices: 7.6 us -> 16.1 us  [the longest x7 11 us: xor(): lax.ppermute(x, both, [(i * narrow + j, (i ^ dw) * narrow + (j ^ dn)) for...]
    reshape x5 -> x0, local copies, waits for them, and re-layouts: 8.19 us -> none  [the longest x1 2.93 us: on_device(): received[:, :charge_cols].reshape(3 * leaf_count, leaf_size, rhs_size)]
    ppermute x2 -> x9, waiting for transfers between devices: 0.01 us -> 5.95 us  [the longest x7 5.94 us: xor(): lax.ppermute(x, both, [(i * narrow + j, (i ^ dw) * narrow + (j ^ dn)) for...]
  transfers between devices with their start and end apart: 2 -> 9, of which waited for: 0 -> 3; matrix products, arithmetic and copies ran while one was open for 3% -> 6% of each run, Pallas kernels for 0% -> 0%
where the time goes in v1:
time: 50.7 us; the launch traced here: 50.2 us
  starting transfers between devices  16.1 us (32%)
  Pallas kernels  15.7 us (31%)
  local copies, waits for them, and re-layouts  10.8 us (21%)
  waiting for transfers between devices  5.95 us (12%)
  other arithmetic  1.53 us (3%)
    ppermute x7, starting transfers between devices, xor(): lax.ppermute(x, both, [(i * narrow + j, (i ^ dw) * narrow + (j ^ dn)) for...  11 us
    unnamed x28, local copies, waits for them, and re-layouts  10.8 us
    pallas_call x1, Pallas kernels, on_device(): pl.pallas_call(far_kernel, in_specs=[smem] * 3 + [vm] * 8, out_shape=[shp...  8.45 us
    ppermute x7, waiting for transfers between devices, xor(): lax.ppermute(x, both, [(i * narrow + j, (i ^ dw) * narrow + (j ^ dn)) for...  5.94 us
    pallas_call x1, Pallas kernels, on_device(): pl.pallas_call(up_kernel, out_shape=[shp(n, v, w), shp(n, v, r), shp(mids...  4.22 us
    ppermute x1, starting transfers between devices, on_device(): from_left = lax.ppermute(hr, 'wide', [(i, i + 1) for i in range(wide - 1)])  3.82 us
    pallas_call x1, Pallas kernels, on_device(): pl.pallas_call(down_kernel, in_specs=[smem] + [vm] * 9, out_shape=shp(n,...  3.04 us
    ppermute x1, starting transfers between devices, on_device(): from_right = lax.ppermute(hl, 'wide', [(i + 1, i) for i in range(wide - 1)])  1.29 us
  transfers between devices with their start and end apart: 9, of which 3 were waited for; matrix products, arithmetic and copies ran while one was open for 6% of the time, Pallas kernels for 0%

profile of v1, /device:TPU:0, one launch (start us, length us, event | category | flops | bytes accessed | tf_op | source)
XLA Modules:
  0.0 50.2 jit_solution(6957691405886254888)
XLA Ops:
  0.0 1.0 %copy-done.3 = bf16[1,24,64,64]{3,2,1,0:T(8,128)(2,1)S(1)} copy-done((bf16[1,24,64,64]{3,2,1,0:T(8,128)(2,1)S(1)}, bf16[1,24,64,64]{3,2,1,0:T(8,128)(2,1)}, u32[]{:S(2)}) %copy-start.3) | copy-done | bytes 196632
  1.0 1.0 %copy-done.4 = bf16[1,24,64,64]{3,2,1,0:T(8,128)(2,1)S(1)} copy-done((bf16[1,24,64,64]{3,2,1,0:T(8,128)(2,1)S(1)}, bf16[1,24,64,64]{3,2,1,0:T(8,128)(2,1)}, u32[]{:S(2)}) %copy-start.4) | copy-done | bytes 196632
  2.0 1.0 %copy-done.5 = bf16[1,24,64,64]{3,2,1,0:T(8,128)(2,1)S(1)} copy-done((bf16[1,24,64,64]{3,2,1,0:T(8,128)(2,1)S(1)}, bf16[1,24,64,64]{3,2,1,0:T(8,128)(2,1)}, u32[]{:S(2)}) %copy-start.5) | copy-done | bytes 196632
  3.0 0.9 %copy-done.8 = bf16[1,6,64,64]{3,2,1,0:T(8,128)(2,1)S(1)} copy-done((bf16[1,6,64,64]{3,2,1,0:T(8,128)(2,1)S(1)}, bf16[1,6,64,64]{3,2,1,0:T(8,128)(2,1)}, u32[]{:S(2)}) %copy-start.8) | copy-done | bytes 49176
  3.9 0.7 %copy-done.11 = bf16[1,1,64,64]{3,2,1,0:T(8,128)(2,1)S(1)} copy-done((bf16[1,1,64,64]{3,2,1,0:T(8,128)(2,1)S(1)}, bf16[1,1,64,64]{3,2,1,0:T(8,128)(2,1)}, u32[]{:S(2)}) %copy-start.11) | copy-done | bytes 8216
  4.6 4.2 %up.1 = (bf16[24,64,64]{2,1,0:T(8,128)(2,1)S(1)}, bf16[24,64,64]{2,1,0:T(8,128)(2,1)S(1)}, bf16[6,64,64]{2,1,0:T(8,128)(2,1)S(1)}, bf16[11,64,128]{2,1,0:T(8,128...) custom-call(bf16[24,64,64]{2,1,0:T(8,128)(2,1)S(1)} %bitcast.31, ...), custom_call_target="tpu_custom_call" | custom-call | tf_op jit(solution)/shard_map/up/pallas_call | solution.py:157
  8.8 4.0 %collective-permute-start.2 = (bf16[32,128]{1,0:T(8,128)(2,1)S(1)}, bf16[32,128]{1,0:T(8,128)(2,1)S(1)}, u32[]{:S(2)}, u32[]{:S(2)}) collective-permute-start(bf16[32,128]{1,0:T(8,128)(2,1)S(1)} %get-tuple-element.14), channel_id=1, source_target_pairs={{0,6},{1,7},{2,4},{3,5},{4,2},{5,3},{6,0},{7,1},{8,14},{9,15},{10,... | collective-permute-start | bytes 24584 | tf_op jit(solution)/shard_map/ppermute | solution.py:168
  12.8 0.5 %collective-permute-start.1 = (bf16[32,128]{1,0:T(8,128)(2,1)S(1)}, bf16[32,128]{1,0:T(8,128)(2,1)S(1)}, u32[]{:S(2)}, u32[]{:S(2)}) collective-permute-start(bf16[32,128]{1,0:T(8,128)(2,1)S(1)} %get-tuple-element.14), channel_id=1, source_target_pairs={{0,2},{1,3},{2,0},{3,1},{4,6},{5,7},{6,4},{7,5},{8,10},{9,11},{10,... | collective-permute-start | bytes 24584 | tf_op jit(solution)/shard_map/ppermute | solution.py:168
  13.5 3.8 %collective-permute-start.7 = (bf16[11,64,128]{2,1,0:T(8,128)(2,1)S(1)}, bf16[11,64,128]{2,1,0:T(8,128)(2,1)S(1)}, u32[]{:S(2)}, u32[]{:S(2)}) collective-permute-start(bf16[11,64,128]{2,1,0:T(8,128)(2,1)S(1)} %get-tuple-element.18), channel_id=1, source_target_pairs={{0,4},{4,8},{8,12},{12,16},{16,20},{20,24},{24,28},{1,5},{5,9},{9,... | collective-permute-start | bytes 540680 | tf_op jit(solution)/shard_map/ppermute | solution.py:164
  17.3 1.3 %collective-permute-start.8 = (bf16[11,64,128]{2,1,0:T(8,128)(2,1)S(1)}, bf16[11,64,128]{2,1,0:T(8,128)(2,1)S(1)}, u32[]{:S(2)}, u32[]{:S(2)}) collective-permute-start(bf16[11,64,128]{2,1,0:T(8,128)(2,1)S(1)} %get-tuple-element.19), channel_id=1, source_target_pairs={{4,0},{8,4},{12,8},{16,12},{20,16},{24,20},{28,24},{5,1},{9,5},{13... | collective-permute-start | bytes 540680 | tf_op jit(solution)/shard_map/ppermute | solution.py:165
  18.6 0.8 %copy.18 = s32[1,24,8]{2,1,0:T(8,128)S(1)} copy(s32[1,24,8]{1,2,0:T(8,128)} %param.21) | data formatting | bytes 1536 | tf_op args[4]
  19.4 0.8 %copy.19 = s32[1,24,6]{2,1,0:T(8,128)S(1)} copy(s32[1,24,6]{1,0,2:T(1,128)} %param.24) | data formatting | bytes 1152 | tf_op args[7]
  20.1 0.7 %bitcast_select_fusion.ni_ref = s32[24,8]{1,0:T(8,128)S(1)} fusion(s32[1,24,8]{2,1,0:T(8,128)S(1)} %copy.18, s32[]{:T(128)S(6)} %sub.32, s32[24]{0:T(128)} %bitcast.41), kind=kLoop, calls=%fused_computation.5 | loop fusion | flops 576 | bytes 1636 | tf_op jit(solution)/shard_map/jit(_where)/select_n | solution.py:186
  20.9 4.7 %collective-permute-start.4 = (bf16[2,32,128]{2,1,0:T(8,128)(2,1)S(1)}, bf16[2,32,128]{2,1,0:T(8,128)(2,1)S(1)}, u32[]{:S(2)}, u32[]{:S(2)}) collective-permute-start(bf16[2,32,128]{2,1,0:T(8,128)(2,1)S(1)} %pad_maximum_fusion.1), channel_id=1, source_target_pairs={{0,16},{1,17},{2,18},{3,19},{4,20},{5,21},{6,22},{7,23},{8,24},{9,... | collective-permute-start | bytes 49160 | tf_op jit(solution)/shard_map/ppermute | solution.py:168
  25.6 1.6 %collective-permute-start.3 = (bf16[2,32,128]{2,1,0:T(8,128)(2,1)S(1)}, bf16[2,32,128]{2,1,0:T(8,128)(2,1)S(1)}, u32[]{:S(2)}, u32[]{:S(2)}) collective-permute-start(bf16[2,32,128]{2,1,0:T(8,128)(2,1)S(1)} %pad_maximum_fusion.1), channel_id=1, source_target_pairs={{0,8},{1,9},{2,10},{3,11},{4,12},{5,13},{6,14},{7,15},{8,0},{9,1},... | collective-permute-start | bytes 49160 | tf_op jit(solution)/shard_map/ppermute | solution.py:168
  27.2 0.7 %fusion.2.mi_ref = s32[6,6]{1,0:T(8,128)S(1)} fusion(s32[1,6,6]{2,0,1:T(1,128)} %param.28, s32[]{:T(128)S(6)} %sub.39), kind=kLoop, calls=%fused_computation.11 | loop fusion | flops 36 | bytes 292 | tf_op jit(solution)/shard_map/sub | solution.py:188
  27.9 1.5 %collective-permute-done.3 = bf16[2,32,128]{2,1,0:T(8,128)(2,1)S(1)} collective-permute-done((bf16[2,32,128]{2,1,0:T(8,128)(2,1)S(1)}, bf16[2,32,128]{2,1,0:T(8,128)(2,1)S(1)}, u32[]{:S(2)}, u32[]{:S(2)}) %collective-permute-start.3) | collective-permute-done | bytes 16416 | tf_op jit(solution)/shard_map/ppermute | solution.py:168
  29.3 3.4 %collective-permute-done.5 = bf16[2,32,128]{2,1,0:T(8,128)(2,1)S(1)} collective-permute-done((bf16[2,32,128]{2,1,0:T(8,128)(2,1)S(1)}, bf16[2,32,128]{2,1,0:T(8,128)(2,1)S(1)}, u32[]{:S(2)}, u32[]{:S(2)}) %collective-permute-start.5) | collective-permute-done | bytes 16416 | tf_op jit(solution)/shard_map/ppermute | solution.py:168
  32.9 1.1 %collective-permute-done.6 = bf16[2,32,128]{2,1,0:T(8,128)(2,1)S(1)} collective-permute-done((bf16[2,32,128]{2,1,0:T(8,128)(2,1)S(1)}, bf16[2,32,128]{2,1,0:T(8,128)(2,1)S(1)}, u32[]{:S(2)}, u32[]{:S(2)}) %collective-permute-start.6) | collective-permute-done | bytes 16416 | tf_op jit(solution)/shard_map/ppermute | solution.py:168
  34.0 1.9 %copy-done = bf16[1,24,8,64,64]{4,3,2,1,0:T(8,128)(2,1)S(1)} copy-done((bf16[1,24,8,64,64]{4,3,2,1,0:T(8,128)(2,1)S(1)}, bf16[1,24,8,64,64]{4,3,2,1,0:T(8,128)(2,1)}, u32[]{:S(2)}) %copy-start) | copy-done | bytes 1572888
  35.9 1.7 %copy-done.1 = bf16[1,24,6,64,64]{4,3,2,1,0:T(8,128)(2,1)S(1)} copy-done((bf16[1,24,6,64,64]{4,3,2,1,0:T(8,128)(2,1)S(1)}, bf16[1,24,6,64,64]{4,3,2,1,0:T(8,128)(2,1)}, u32[]{:S(2)}) %copy-start.1) | copy-done | bytes 1179672
  37.6 1.1 %copy-done.2 = bf16[1,6,6,64,64]{4,3,2,1,0:T(8,128)(2,1)S(1)} copy-done((bf16[1,6,6,64,64]{4,3,2,1,0:T(8,128)(2,1)S(1)}, bf16[1,6,6,64,64]{4,3,2,1,0:T(8,128)(2,1)}, u32[]{:S(2)}) %copy-start.2) | copy-done | bytes 294936
  38.6 8.4 %far.1 = (f32[24,64,64]{2,1,0:T(8,128)S(1)}, f32[24,64,64]{2,1,0:T(8,128)S(1)}, f32[6,64,64]{2,1,0:T(8,128)S(1)}) custom-call(s32[24,8]{1,0:T(8,128)S(1)} %bitcast_select_fusion.ni_ref, s32[24,6]{1,0:T(8,128)S(1)} %subtract_bitcast_fusion.fi_ref, s32[6,6]{1,0:T(8,128)S(1)} %fusion.2.mi_ref, bf16[24,64,64]{2,1,0:T(8,128)(2,1)S(1)} %get-tuple-element.15.ct_ref, ...), custom_call_target="tpu_custom_call" | custom-call | tf_op jit(solution)/shard_map/far/pallas_call | solution.py:192
  47.1 3.0 %down.1 = bf16[24,64,64]{2,1,0:T(8,128)(2,1)} custom-call(s32[3]{0:T(128)S(1)} %pad_add_fusion.hs_ref, bf16[3,32,128]{2,1,0:T(8,128)(2,1)S(1)} %pad_maximum_fusion.g_ref, bf16[4,64,64]{2,1,0:T(8,128)(2,1)S(1)} %bitcast.38, bf16[1,64,64]{2,1,0:T(8,128)(2,1)S(1)} %bitcast.40, bf16[6,64,64]{2,1,0:T(8,128)(2,1)S(1)} %bitcast.37, ...), custom_call_target="tpu_custom_call" | custom-call | tf_op jit(solution)/shard_map/down/pallas_call | solution.py:205
  (35 shorter events, 0.4 us)
Async XLA Ops:
  0.0 1.0 %copy-start.3 = (bf16[1,24,64,64]{3,2,1,0:T(8,128)(2,1)S(1)}, bf16[1,24,64,64]{3,2,1,0:T(8,128)(2,1)}, u32[]{:S(2)}) copy-start(bf16[1,24,64,64]{3,2,1,0:T(8,128)(2,1)} %param.17) | copy-start | bytes 589828
  1.0 1.0 %copy-start.4 = (bf16[1,24,64,64]{3,2,1,0:T(8,128)(2,1)S(1)}, bf16[1,24,64,64]{3,2,1,0:T(8,128)(2,1)}, u32[]{:S(2)}) copy-start(bf16[1,24,64,64]{3,2,1,0:T(8,128)(2,1)} %param.18) | copy-start | bytes 589828
  2.0 1.0 %copy-start.5 = (bf16[1,24,64,64]{3,2,1,0:T(8,128)(2,1)S(1)}, bf16[1,24,64,64]{3,2,1,0:T(8,128)(2,1)}, u32[]{:S(2)}) copy-start(bf16[1,24,64,64]{3,2,1,0:T(8,128)(2,1)} %param.25) | copy-start | bytes 589828
  3.0 0.9 %copy-start.8 = (bf16[1,6,64,64]{3,2,1,0:T(8,128)(2,1)S(1)}, bf16[1,6,64,64]{3,2,1,0:T(8,128)(2,1)}, u32[]{:S(2)}) copy-start(bf16[1,6,64,64]{3,2,1,0:T(8,128)(2,1)} %param.29) | copy-start | bytes 147460
  3.9 0.7 %copy-start.11 = (bf16[1,1,64,64]{3,2,1,0:T(8,128)(2,1)S(1)}, bf16[1,1,64,64]{3,2,1,0:T(8,128)(2,1)}, u32[]{:S(2)}) copy-start(bf16[1,1,64,64]{3,2,1,0:T(8,128)(2,1)} %param.31) | copy-start | bytes 24580
  8.8 12.0 %collective-permute-start.2 = (bf16[32,128]{1,0:T(8,128)(2,1)S(1)}, bf16[32,128]{1,0:T(8,128)(2,1)S(1)}, u32[]{:S(2)}, u32[]{:S(2)}) collective-permute-start(bf16[32,128]{1,0:T(8,128)(2,1)S(1)} %get-tuple-element.14), channel_id=1, source_target_pairs={{0,6},{1,7},{2,4},{3,5},{4,2},{5,3},{6,0},{7,1},{8,14},{9,15},{10,... | collective-permute-start | bytes 24584 | tf_op jit(solution)/shard_map/ppermute | solution.py:168
  12.8 8.1 %collective-permute-start.1 = (bf16[32,128]{1,0:T(8,128)(2,1)S(1)}, bf16[32,128]{1,0:T(8,128)(2,1)S(1)}, u32[]{:S(2)}, u32[]{:S(2)}) collective-permute-start(bf16[32,128]{1,0:T(8,128)(2,1)S(1)} %get-tuple-element.14), channel_id=1, source_target_pairs={{0,2},{1,3},{2,0},{3,1},{4,6},{5,7},{6,4},{7,5},{8,10},{9,11},{10,... | collective-permute-start | bytes 24584 | tf_op jit(solution)/shard_map/ppermute | solution.py:168
  13.4 7.5 %collective-permute-start = (bf16[32,128]{1,0:T(8,128)(2,1)S(1)}, bf16[32,128]{1,0:T(8,128)(2,1)S(1)}, u32[]{:S(2)}, u32[]{:S(2)}) collective-permute-start(bf16[32,128]{1,0:T(8,128)(2,1)S(1)} %get-tuple-element.14), channel_id=1, source_target_pairs={{0,4},{1,5},{2,6},{3,7},{4,0},{5,1},{6,2},{7,3},{8,12},{9,13},{10,... | collective-permute-start | bytes 24584 | tf_op jit(solution)/shard_map/ppermute | solution.py:168
  13.5 20.5 %collective-permute-start.7 = (bf16[11,64,128]{2,1,0:T(8,128)(2,1)S(1)}, bf16[11,64,128]{2,1,0:T(8,128)(2,1)S(1)}, u32[]{:S(2)}, u32[]{:S(2)}) collective-permute-start(bf16[11,64,128]{2,1,0:T(8,128)(2,1)S(1)} %get-tuple-element.18), channel_id=1, source_target_pairs={{0,4},{4,8},{8,12},{12,16},{16,20},{20,24},{24,28},{1,5},{5,9},{9,... | collective-permute-start | bytes 540680 | tf_op jit(solution)/shard_map/ppermute | solution.py:164
  17.3 16.7 %collective-permute-start.8 = (bf16[11,64,128]{2,1,0:T(8,128)(2,1)S(1)}, bf16[11,64,128]{2,1,0:T(8,128)(2,1)S(1)}, u32[]{:S(2)}, u32[]{:S(2)}) collective-permute-start(bf16[11,64,128]{2,1,0:T(8,128)(2,1)S(1)} %get-tuple-element.19), channel_id=1, source_target_pairs={{4,0},{8,4},{12,8},{16,12},{20,16},{24,20},{28,24},{5,1},{9,5},{13... | collective-permute-start | bytes 540680 | tf_op jit(solution)/shard_map/ppermute | solution.py:165
  20.9 6.9 %collective-permute-start.4 = (bf16[2,32,128]{2,1,0:T(8,128)(2,1)S(1)}, bf16[2,32,128]{2,1,0:T(8,128)(2,1)S(1)}, u32[]{:S(2)}, u32[]{:S(2)}) collective-permute-start(bf16[2,32,128]{2,1,0:T(8,128)(2,1)S(1)} %pad_maximum_fusion.1), channel_id=1, source_target_pairs={{0,16},{1,17},{2,18},{3,19},{4,20},{5,21},{6,22},{7,23},{8,24},{9,... | collective-permute-start | bytes 49160 | tf_op jit(solution)/shard_map/ppermute | solution.py:168
  25.6 3.7 %collective-permute-start.3 = (bf16[2,32,128]{2,1,0:T(8,128)(2,1)S(1)}, bf16[2,32,128]{2,1,0:T(8,128)(2,1)S(1)}, u32[]{:S(2)}, u32[]{:S(2)}) collective-permute-start(bf16[2,32,128]{2,1,0:T(8,128)(2,1)S(1)} %pad_maximum_fusion.1), channel_id=1, source_target_pairs={{0,8},{1,9},{2,10},{3,11},{4,12},{5,13},{6,14},{7,15},{8,0},{9,1},... | collective-permute-start | bytes 49160 | tf_op jit(solution)/shard_map/ppermute | solution.py:168
  27.2 5.5 %collective-permute-start.5 = (bf16[2,32,128]{2,1,0:T(8,128)(2,1)S(1)}, bf16[2,32,128]{2,1,0:T(8,128)(2,1)S(1)}, u32[]{:S(2)}, u32[]{:S(2)}) collective-permute-start(bf16[2,32,128]{2,1,0:T(8,128)(2,1)S(1)} %pad_maximum_fusion.1), channel_id=1, source_target_pairs={{0,24},{1,25},{2,26},{3,27},{4,28},{5,29},{6,30},{7,31},{8,16},{9,... | collective-permute-start | bytes 49160 | tf_op jit(solution)/shard_map/ppermute | solution.py:168
  32.7 1.2 %collective-permute-start.6 = (bf16[2,32,128]{2,1,0:T(8,128)(2,1)S(1)}, bf16[2,32,128]{2,1,0:T(8,128)(2,1)S(1)}, u32[]{:S(2)}, u32[]{:S(2)}) collective-permute-start(bf16[2,32,128]{2,1,0:T(8,128)(2,1)S(1)} %add_convert_fusion), channel_id=1, source_target_pairs={{0,1},{1,0},{2,3},{3,2},{4,5},{5,4},{6,7},{7,6},{8,9},{9,8},{10,11... | collective-permute-start | bytes 49160 | tf_op jit(solution)/shard_map/ppermute | solution.py:168
  34.0 1.9 %copy-start = (bf16[1,24,8,64,64]{4,3,2,1,0:T(8,128)(2,1)S(1)}, bf16[1,24,8,64,64]{4,3,2,1,0:T(8,128)(2,1)}, u32[]{:S(2)}) copy-start(bf16[1,24,8,64,64]{4,3,2,1,0:T(8,128)(2,1)} %param.20) | copy-start | bytes 4718596
  35.9 1.7 %copy-start.1 = (bf16[1,24,6,64,64]{4,3,2,1,0:T(8,128)(2,1)S(1)}, bf16[1,24,6,64,64]{4,3,2,1,0:T(8,128)(2,1)}, u32[]{:S(2)}) copy-start(bf16[1,24,6,64,64]{4,3,2,1,0:T(8,128)(2,1)} %param.23) | copy-start | bytes 3538948
  37.6 1.1 %copy-start.2 = (bf16[1,6,6,64,64]{4,3,2,1,0:T(8,128)(2,1)S(1)}, bf16[1,6,6,64,64]{4,3,2,1,0:T(8,128)(2,1)}, u32[]{:S(2)}) copy-start(bf16[1,6,6,64,64]{4,3,2,1,0:T(8,128)(2,1)} %param.27) | copy-start | bytes 884740
  38.6 8.5 %copy-start.6 = (bf16[1,24,64,64]{3,2,1,0:T(8,128)(2,1)S(1)}, bf16[1,24,64,64]{3,2,1,0:T(8,128)(2,1)}, u32[]{:S(2)}) copy-start(bf16[1,24,64,64]{3,2,1,0:T(8,128)(2,1)} %param.26) | copy-start | bytes 589828
  38.6 8.5 %copy-start.7 = (bf16[1,24,64,64]{3,2,1,0:T(8,128)(2,1)S(1)}, bf16[1,24,64,64]{3,2,1,0:T(8,128)(2,1)}, u32[]{:S(2)}) copy-start(bf16[1,24,64,64]{3,2,1,0:T(8,128)(2,1)} %param.19) | copy-start | bytes 589828
  38.6 8.5 %copy-start.9 = (bf16[1,6,64,64]{3,2,1,0:T(8,128)(2,1)S(1)}, bf16[1,6,64,64]{3,2,1,0:T(8,128)(2,1)}, u32[]{:S(2)}) copy-start(bf16[1,6,64,64]{3,2,1,0:T(8,128)(2,1)} %param.30) | copy-start | bytes 147460
  38.6 8.5 %copy-start.10 = (bf16[1,4,64,64]{3,2,1,0:T(8,128)(2,1)S(1)}, bf16[1,4,64,64]{3,2,1,0:T(8,128)(2,1)}, u32[]{:S(2)}) copy-start(bf16[1,4,64,64]{3,2,1,0:T(8,128)(2,1)} %param.33) | copy-start | bytes 98308
  38.6 8.5 %copy-start.12 = (bf16[1,1,64,64]{3,2,1,0:T(8,128)(2,1)S(1)}, bf16[1,1,64,64]{3,2,1,0:T(8,128)(2,1)}, u32[]{:S(2)}) copy-start(bf16[1,1,64,64]{3,2,1,0:T(8,128)(2,1)} %param.32) | copy-start | bytes 24580

commit v2 on v1

v2 whole, which is shorter than its diff:
```python
import functools

import jax
import jax.numpy as jnp
from jax import lax
from jax.experimental import pallas as pl
from jax.experimental.pallas import tpu as pltpu
from jax.sharding import PartitionSpec as P

REACH = 8
MREACH = 6
F32 = jnp.float32
BF16 = jnp.bfloat16
NN = (((1,), (0,)), ((), ()))
NT = (((1,), (1,)), ((), ()))


def nn(a, b):
    return lax.dot_general(a, b, NN, preferred_element_type=F32)


def nt(a, b):
    return lax.dot_general(a, b, NT, preferred_element_type=F32)


def beside(*parts):
    return jnp.concatenate(parts, axis=1)


def rows(ref, *at):
    x = ref[at]
    return x.reshape(-1, x.shape[-1])


def in_hbm(x):
    return pltpu.with_memory_space_constraint(x, pltpu.HBM)


def up_kernel(c_hbm, r_hbm, ul_hbm, um_hbm, ut_hbm, cp_ref, sp_ref, mp_ref, e0_ref, e1_ref, dt_ref,
              c_ref, r_ref, ul_ref, um_ref, ut_ref, sems):
    n, w = c_ref.shape[:2]
    mids = um_ref.shape[0]
    cut = n // 2
    copies = []
    for h in range(2):
        part = pl.ds(h * cut, cut)
        copies.append([
            pltpu.make_async_copy(src.at[part], dst.at[part], sems.at[3 * h + j])
            for j, (src, dst) in enumerate(((c_hbm, c_ref), (r_hbm, r_ref), (ul_hbm, ul_ref)))
        ])
    tail = [pltpu.make_async_copy(um_hbm, um_ref, sems.at[6]), pltpu.make_async_copy(ut_hbm, ut_ref, sems.at[7])]
    for group in copies + [tail]:
        for copy in group:
            copy.start()
    eye = (
        lax.broadcasted_iota(jnp.int32, (w, w), 0) == lax.broadcasted_iota(jnp.int32, (w, w), 1)
    ).astype(F32).astype(BF16)
    zero = jnp.zeros((w, w), BF16)
    zeros = jnp.zeros((w, 2 * w), BF16)
    mid = []
    for m in range(mids):
        for h in range(2):
            if 4 * m == h * cut:
                for copy in copies[h]:
                    copy.wait()
        i = 4 * m
        ct = nt(eye, rows(c_ref, pl.ds(i, 4))).astype(BF16)
        cp_ref[2 * m] = ct[:, : 2 * w]
        cp_ref[2 * m + 1] = ct[:, 2 * w :]
        blocks = jnp.concatenate([
            beside(beside(r_ref[i], zero), zeros),
            beside(beside(zero, r_ref[i + 1]), zeros),
            beside(zeros, beside(r_ref[i + 2], zero)),
            beside(zeros, beside(zero, r_ref[i + 3])),
        ], axis=0)
        st = nn(ct, blocks).astype(BF16)
        sp_ref[2 * m] = st[:, : 2 * w]
        sp_ref[2 * m + 1] = st[:, 2 * w :]
        mid.append(nn(st, rows(ul_ref, pl.ds(i, 4))))
    for m in range(mids // 2):
        mp_ref[m] = beside(mid[2 * m], mid[2 * m + 1]).astype(BF16)
    for copy in tail:
        copy.wait()
    dev = nn(beside(*[mp_ref[m] for m in range(mids // 2)]), rows(um_ref, pl.ds(0, mids)))
    term = nn(dev.astype(BF16), ut_ref[0])
    h = term.shape[0] // 2
    dt_ref[...] = beside(term[:h], term[h:]).astype(BF16)
    odd = lax.axis_index("wide") % 2
    half, mhalf = REACH // 2, MREACH // 2
    for e_ref, right in ((e0_ref, 1 - odd), (e1_ref, odd)):
        at = right * (n // 2 - half)
        mat = right * (mids // 2 - mhalf)
        for k in range(half):
            e_ref[k] = cp_ref[at + k]
            e_ref[half + k] = sp_ref[at + k]
        for k in range(mhalf):
            e_ref[2 * half + k] = mp_ref[mat + k]


def far_kernel(near_hbm, count_hbm, far_hbm, mid_hbm, cp_ref, sp_ref, mp_ref, f0_ref, f1_ref, nb_hbm, lc_hbm, mc_hbm,
               near_ref, lf_ref, mf_ref, ctab, stab, mtab, ni_ref, nc_ref, fi_ref, mi_ref, nb_ref, lc_ref, mc_ref,
               small, big):
    n = nb_ref.shape[0]
    slots, fars, mfars = nb_ref.shape[1], lc_ref.shape[1], mc_ref.shape[1]
    mids = mc_ref.shape[0]
    lists = [
        pltpu.make_async_copy(src, dst, small.at[j])
        for j, (src, dst) in enumerate(((near_hbm, ni_ref), (count_hbm, nc_ref), (far_hbm, fi_ref), (mid_hbm, mi_ref)))
    ]
    for copy in lists:
        copy.start()
    whole = pltpu.make_async_copy(mc_hbm, mc_ref, small.at[4])
    whole.start()
    groups = big.shape[1]
    step = n // groups

    def chunk(g):
        part = pl.ds(g * step, step)
        return (
            pltpu.make_async_copy(nb_hbm.at[part], nb_ref.at[part], big.at[0, g]),
            pltpu.make_async_copy(lc_hbm.at[part], lc_ref.at[part], big.at[1, g]),
        )

    for g in range(groups):
        for copy in chunk(g):
            copy.start()
    w = ctab.shape[1]
    lo = lax.broadcasted_iota(jnp.int32, (w, 2 * w), 1) < w
    odd = lax.axis_index("wide") % 2
    pos = lax.axis_index("wide")

    def double(pair, tab, at):
        turned = jnp.concatenate([pair[:, w:], pair[:, :w]], axis=1)
        tab[at] = jnp.where(lo, pair, turned)
        tab[at + 1] = jnp.where(lo, turned, pair)

    half, mhalf = REACH // 2, MREACH // 2

    @pl.loop(0, n // 2)
    def _(k):
        double(cp_ref[k], ctab, REACH + 2 * k)
        double(sp_ref[k], stab, REACH + 2 * k)

    for k in range(mids // 2):
        double(mp_ref[k], mtab, MREACH + 2 * k)
    ctab[n + 2 * REACH] = jnp.zeros(ctab.shape[1:], BF16)
    for f_ref, right in ((f0_ref, 1 - odd), (f1_ref, odd)):
        at = right * (n + REACH)
        mat = right * (mids + MREACH)

        @pl.loop(0, half)
        def _(k):
            double(f_ref[k], ctab, at + 2 * k)
            double(f_ref[half + k], stab, at + 2 * k)

        for k in range(mhalf):
            double(f_ref[2 * half + k], mtab, mat + 2 * k)
    for copy in lists:
        copy.wait()
    base, mbase = pos * n - REACH, pos * mids - MREACH

    def side(tab, idx):
        return beside(*[jnp.where(lo, tab[idx[k]], tab[idx[k + 1]]) for k in range(0, len(idx), 2)])

    whole.wait()
    for j in range(mids):
        idx = [mi_ref[j, 0, k] - mbase for k in range(mfars)]
        mf_ref[j] = jnp.transpose(nn(side(mtab, idx), rows(mc_ref, j)))

    @pl.loop(0, groups)
    def _(g):
        for copy in chunk(g):
            copy.wait()
        for q in range(step):
            i = g * step + q
            live = nc_ref[0, i]
            idx = [jnp.where(k < live, ni_ref[k, i] - base, n + 2 * REACH) for k in range(slots)]
            near_ref[i] = jnp.transpose(nn(side(ctab, idx), rows(nb_ref, i)))
            idx = [fi_ref[k, 0, i] - base for k in range(fars)]
            lf_ref[i] = jnp.transpose(nn(side(stab, idx), rows(lc_ref, i)))


def down_kernel(own_ref, over_ref, tc_ref, dtop_ref, dm_ref, tl_ref, cb_ref, near_ref, lf_ref, mf_ref, out_ref):
    mids = dm_ref.shape[0]
    me = lax.axis_index("narrow")
    acc = None
    for ref, k, h in ((own_ref, 1, me ^ 2), (over_ref, 0, me ^ 1), (over_ref, 1, me ^ 3)):
        g = ref[k]
        c = g.shape[1] // 2
        gt = jnp.concatenate([g[:, :c], g[:, c:]], axis=0)
        part = nn(gt, tc_ref[h])
        acc = part if acc is None else acc + part
    dd = nt(dtop_ref[0], acc.astype(BF16)).astype(BF16)
    down = nn(rows(dm_ref, pl.ds(0, mids)), dd)
    r = dd.shape[0]
    for m in range(mids):
        md = (mf_ref[m] + down[m * r : (m + 1) * r]).astype(BF16)
        ld = nn(rows(tl_ref, pl.ds(4 * m, 4)), md)
        for q in range(4):
            i = 4 * m + q
            lq = (lf_ref[i] + ld[q * r : (q + 1) * r]).astype(BF16)
            out_ref[i] = (near_ref[i] + nn(cb_ref[i], lq)).astype(BF16)


def on_device(
    charges, leaf_row_basis, leaf_column_basis, near_blocks, near_src, near_count, leaf_coupling, far_src,
    up_leaf, column_transfer_leaf, mid_coupling, mid_src, up_mid, down_mid, up_top, down_top, top_coupling,
):
    n, w, v = charges.shape[1:]
    mids = up_mid.shape[1]
    wide, narrow = lax.axis_size("wide"), lax.axis_size("narrow")
    both = ("wide", "narrow")
    pairs = REACH + MREACH // 2
    slots, fars, mfars = near_src.shape[2], far_src.shape[2], mid_src.shape[2]
    hbm = pl.BlockSpec(memory_space=pltpu.HBM)
    vm = pl.BlockSpec(memory_space=pltpu.VMEM)
    dma = pltpu.SemaphoreType.DMA

    def shp(*s, t=BF16):
        return jax.ShapeDtypeStruct(s, t)

    cp, sp, mp, e0, e1, term = pl.pallas_call(
        up_kernel,
        in_specs=[hbm] * 5,
        out_specs=[vm] * 6,
        out_shape=[shp(n // 2, v, 2 * w), shp(n // 2, v, 2 * w), shp(mids // 2, v, 2 * w),
                   shp(pairs, v, 2 * w), shp(pairs, v, 2 * w), shp(v // 2, 2 * w)],
        scratch_shapes=[
            pltpu.VMEM((n, w, v), BF16), pltpu.VMEM((n, w, v), BF16), pltpu.VMEM((n, w, v), BF16),
            pltpu.VMEM((mids, w, v), BF16), pltpu.VMEM((1, w, v), BF16), dma((8,)),
        ],
        compiler_params=pltpu.CompilerParams(vmem_limit_bytes=16 << 20),
        cost_estimate=pl.CostEstimate(flops=30_000_000, bytes_accessed=4_000_000, transcendentals=0),
        name="up",
    )(*map(in_hbm, (charges[0], leaf_row_basis[0], up_leaf[0], up_mid[0], up_top[0])))

    def xor(x, dw, dn):
        return lax.ppermute(x, both, [(i * narrow + j, (i ^ dw) * narrow + (j ^ dn)) for i in range(wide) for j in range(narrow)])

    f = term.astype(F32)
    own = f + xor(term, 1, 0).astype(F32)
    other = xor(term, 0, 2).astype(F32) + xor(term, 1, 2).astype(F32)
    f0 = lax.ppermute(e0, "wide", [(i, i ^ 1) for i in range(wide)])
    f1 = lax.ppermute(e1, "wide", [(i, ((i + 1) ^ 1) - 1) for i in range(1, wide - 1)])
    have = jnp.stack([own, other]).astype(BF16)
    bit = 2
    while bit < wide:
        got = have.astype(F32) + xor(have, bit, 0).astype(F32)
        if 2 * bit < wide:
            got = got + xor(have, 2 * bit, 0).astype(F32) + xor(have, 3 * bit, 0).astype(F32)
        have = got.astype(BF16)
        bit *= 4
    over = xor(have, 0, 1)

    near_list = jnp.transpose(near_src, (0, 2, 1))[0]
    far_list = jnp.transpose(far_src, (2, 0, 1))
    mid_list = jnp.transpose(mid_src, (1, 0, 2))
    near, lf, mf = pl.pallas_call(
        far_kernel,
        in_specs=[hbm] * 4 + [vm] * 5 + [hbm] * 3,
        out_specs=[vm] * 3,
        out_shape=[shp(n, w, v, t=F32), shp(n, w, v, t=F32), shp(mids, w, v, t=F32)],
        scratch_shapes=[
            pltpu.VMEM((n + 2 * REACH + 1, v, 2 * w), BF16),
            pltpu.VMEM((n + 2 * REACH, v, 2 * w), BF16),
            pltpu.VMEM((mids + 2 * MREACH, v, 2 * w), BF16),
            pltpu.SMEM((slots, n), jnp.int32), pltpu.SMEM((1, n), jnp.int32),
            pltpu.SMEM((fars, 1, n), jnp.int32), pltpu.SMEM((mids, 1, mfars), jnp.int32),
            pltpu.VMEM((n, slots, w, v), BF16), pltpu.VMEM((n, fars, w, v), BF16), pltpu.VMEM((mids, mfars, w, v), BF16),
            dma((5,)), dma((2, mids)),
        ],
        compiler_params=pltpu.CompilerParams(vmem_limit_bytes=24 << 20),
        cost_estimate=pl.CostEstimate(flops=200_000_000, bytes_accessed=12_000_000, transcendentals=0),
        name="far",
    )(*map(in_hbm, (near_list, near_count, far_list, mid_list)), cp, sp, mp, f0, f1,
      *map(in_hbm, (near_blocks[0], leaf_coupling[0], mid_coupling[0])))

    out = pl.pallas_call(
        down_kernel,
        in_specs=[vm] * 10,
        out_shape=shp(n, w, v),
        compiler_params=pltpu.CompilerParams(vmem_limit_bytes=16 << 20),
        cost_estimate=pl.CostEstimate(flops=30_000_000, bytes_accessed=4_000_000, transcendentals=0),
        name="down",
    )(have, over, top_coupling[0], down_top[0], down_mid[0], column_transfer_leaf[0], leaf_column_basis[0], near, lf, mf)
    return out[None]


def solution(mesh):
    leaf = P("narrow", "wide", None, None)
    block = P("narrow", "wide", None, None, None)
    lists = P("narrow", "wide", None)
    return jax.shard_map(
        on_device,
        mesh=mesh,
        in_specs=(
            leaf, leaf, leaf, block, lists, P("narrow", "wide"), block, lists,
            leaf, leaf, block, lists, leaf, leaf, leaf, leaf, P("narrow", None, None, None),
        ),
        out_specs=leaf,
        check_vma=False,
    )
```

time: 50.7 us -> 31.4 us (0.62)
  the two profiles are of different devices: /device:TPU:0 before, /device:TPU:24 now
where the time goes in v2:
time: 31.4 us; the launch traced here: 31.2 us
  starting transfers between devices  11.5 us (37%)
  Pallas kernels  10.2 us (32%)
  waiting for transfers between devices  9.34 us (30%)
    ppermute x7, starting transfers between devices, xor(): lax.ppermute(x, both, [(i * narrow + j, (i ^ dw) * narrow + (j ^ dn)) for...  8.08 us
    pallas_call x1, Pallas kernels, on_device(): pl.pallas_call(far_kernel, in_specs=[hbm] * 4 + [vm] * 5 + [hbm] * 3, out...  5.38 us
    ppermute x1, waiting for transfers between devices, on_device(): f0 = lax.ppermute(e0, 'wide', [(i, i ^ 1) for i in range(wide)])  3.85 us
    ppermute x7, waiting for transfers between devices, xor(): lax.ppermute(x, both, [(i * narrow + j, (i ^ dw) * narrow + (j ^ dn)) for...  3.12 us
    pallas_call x1, Pallas kernels, on_device(): pl.pallas_call(up_kernel, in_specs=[hbm] * 5, out_specs=[vm] * 6, out_sha...  3.04 us
    ppermute x1, waiting for transfers between devices, on_device(): lax.ppermute(e1, 'wide', [(i, (i + 1 ^ 1) - 1) for i in range(1, wide - 1)])  2.38 us
    ppermute x1, starting transfers between devices, on_device(): lax.ppermute(e1, 'wide', [(i, (i + 1 ^ 1) - 1) for i in range(1, wide - 1)])  1.91 us
    pallas_call x1, Pallas kernels, on_device(): pl.pallas_call(down_kernel, in_specs=[vm] * 10, out_shape=shp(n, w, v), c...  1.78 us
  transfers between devices with their start and end apart: 9, of which 5 were waited for; matrix products, arithmetic and copies ran while one was open for 0% of the time, Pallas kernels for 17%

profile of v2, /device:TPU:24, one launch (start us, length us, event | category | flops | bytes accessed | tf_op | source)
XLA Modules:
  0.0 31.2 jit_solution(17035004117661271323)
XLA Ops:
  0.0 3.0 %up.1 = (bf16[12,64,128]{2,1,0:T(8,128)(2,1)S(1)}, bf16[12,64,128]{2,1,0:T(8,128)(2,1)S(1)}, bf16[3,64,128]{2,1,0:T(8,128)(2,1)S(1)}, bf16[11,64,128]{2,1,0:T(8,...) custom-call(bf16[24,64,64]{2,1,0:T(8,128)(2,1)} %bitcast.31, bf16[24,64,64]{2,1,0:T(8,128)(2,1)} %bitcast.32, ...), custom_call_target="tpu_custom_call" | custom-call | flops 30000000 | bytes 4000000 | tf_op jit(solution)/shard_map/up/pallas_call | solution.py:222
  3.0 1.6 %collective-permute-start = (bf16[32,128]{1,0:T(8,128)(2,1)S(1)}, bf16[32,128]{1,0:T(8,128)(2,1)S(1)}, u32[]{:S(2)}, u32[]{:S(2)}) collective-permute-start(bf16[32,128]{1,0:T(8,128)(2,1)S(1)} %get-tuple-element.14), channel_id=1, source_target_pairs={{0,4},{1,5},{2,6},{3,7},{4,0},{5,1},{6,2},{7,3},{8,12},{9,13},{10,... | collective-permute-start | bytes 24584 | tf_op jit(solution)/shard_map/ppermute | solution.py:238
  4.6 1.4 %collective-permute-start.2 = (bf16[32,128]{1,0:T(8,128)(2,1)S(1)}, bf16[32,128]{1,0:T(8,128)(2,1)S(1)}, u32[]{:S(2)}, u32[]{:S(2)}) collective-permute-start(bf16[32,128]{1,0:T(8,128)(2,1)S(1)} %get-tuple-element.14), channel_id=1, source_target_pairs={{0,6},{1,7},{2,4},{3,5},{4,2},{5,3},{6,0},{7,1},{8,14},{9,15},{10,... | collective-permute-start | bytes 24584 | tf_op jit(solution)/shard_map/ppermute | solution.py:238
  6.1 0.5 %collective-permute-start.1 = (bf16[32,128]{1,0:T(8,128)(2,1)S(1)}, bf16[32,128]{1,0:T(8,128)(2,1)S(1)}, u32[]{:S(2)}, u32[]{:S(2)}) collective-permute-start(bf16[32,128]{1,0:T(8,128)(2,1)S(1)} %get-tuple-element.14), channel_id=1, source_target_pairs={{0,2},{1,3},{2,0},{3,1},{4,6},{5,7},{6,4},{7,5},{8,10},{9,11},{10,... | collective-permute-start | bytes 24584 | tf_op jit(solution)/shard_map/ppermute | solution.py:238
  6.6 0.2 collective-permute-done
  6.8 2.4 %collective-permute-done.2 = bf16[32,128]{1,0:T(8,128)(2,1)S(1)} collective-permute-done((bf16[32,128]{1,0:T(8,128)(2,1)S(1)}, bf16[32,128]{1,0:T(8,128)(2,1)S(1)}, u32[]{:S(2)}, u32[]{:S(2)}) %collective-permute-start.2) | collective-permute-done | bytes 8224 | tf_op jit(solution)/shard_map/ppermute | solution.py:238
  9.2 0.5 %collective-permute-done.1 = bf16[32,128]{1,0:T(8,128)(2,1)S(1)} collective-permute-done((bf16[32,128]{1,0:T(8,128)(2,1)S(1)}, bf16[32,128]{1,0:T(8,128)(2,1)S(1)}, u32[]{:S(2)}, u32[]{:S(2)}) %collective-permute-start.1) | collective-permute-done | bytes 8224 | tf_op jit(solution)/shard_map/ppermute | solution.py:238
  9.7 0.4 %collective-permute-start.4 = (bf16[2,32,128]{2,1,0:T(8,128)(2,1)S(1)}, bf16[2,32,128]{2,1,0:T(8,128)(2,1)S(1)}, u32[]{:S(2)}, u32[]{:S(2)}) collective-permute-start(bf16[2,32,128]{2,1,0:T(8,128)(2,1)S(1)} %pad_maximum_fusion), channel_id=1, source_target_pairs={{0,16},{1,17},{2,18},{3,19},{4,20},{5,21},{6,22},{7,23},{8,24},{9,... | collective-permute-start | bytes 49160 | tf_op jit(solution)/shard_map/ppermute | solution.py:238
  10.1 0.4 %collective-permute-start.3 = (bf16[2,32,128]{2,1,0:T(8,128)(2,1)S(1)}, bf16[2,32,128]{2,1,0:T(8,128)(2,1)S(1)}, u32[]{:S(2)}, u32[]{:S(2)}) collective-permute-start(bf16[2,32,128]{2,1,0:T(8,128)(2,1)S(1)} %pad_maximum_fusion), channel_id=1, source_target_pairs={{0,8},{1,9},{2,10},{3,11},{4,12},{5,13},{6,14},{7,15},{8,0},{9,1},... | collective-permute-start | bytes 49160 | tf_op jit(solution)/shard_map/ppermute | solution.py:238
  10.6 3.6 %collective-permute-start.5 = (bf16[2,32,128]{2,1,0:T(8,128)(2,1)S(1)}, bf16[2,32,128]{2,1,0:T(8,128)(2,1)S(1)}, u32[]{:S(2)}, u32[]{:S(2)}) collective-permute-start(bf16[2,32,128]{2,1,0:T(8,128)(2,1)S(1)} %pad_maximum_fusion), channel_id=1, source_target_pairs={{0,24},{1,25},{2,26},{3,27},{4,28},{5,29},{6,30},{7,31},{8,16},{9,... | collective-permute-start | bytes 49160 | tf_op jit(solution)/shard_map/ppermute | solution.py:238
  14.2 1.5 %collective-permute-start.7 = (bf16[11,64,128]{2,1,0:T(8,128)(2,1)S(1)}, bf16[11,64,128]{2,1,0:T(8,128)(2,1)S(1)}, u32[]{:S(2)}, u32[]{:S(2)}) collective-permute-start(bf16[11,64,128]{2,1,0:T(8,128)(2,1)S(1)} %get-tuple-element.18), channel_id=1, source_target_pairs={{0,4},{4,0},{8,12},{12,8},{16,20},{20,16},{24,28},{28,24},{1,5},{5... | collective-permute-start | bytes 540680 | tf_op jit(solution)/shard_map/ppermute | solution.py:243
  15.7 1.9 %collective-permute-start.8 = (bf16[11,64,128]{2,1,0:T(8,128)(2,1)S(1)}, bf16[11,64,128]{2,1,0:T(8,128)(2,1)S(1)}, u32[]{:S(2)}, u32[]{:S(2)}) collective-permute-start(bf16[11,64,128]{2,1,0:T(8,128)(2,1)S(1)} %get-tuple-element.19), channel_id=1, source_target_pairs={{4,8},{8,4},{12,16},{16,12},{20,24},{24,20},{5,9},{9,5},{13,17},{1... | collective-permute-start | bytes 540680 | tf_op jit(solution)/shard_map/ppermute | solution.py:244
  17.6 0.0 collective-permute-done.4
  17.6 0.0 collective-permute-done.3
  17.6 0.0 collective-permute-done.5
  17.7 0.1 collective-permute-start.6
  17.8 3.8 %collective-permute-done.7.f0_ref = bf16[11,64,128]{2,1,0:T(8,128)(2,1)S(1)} collective-permute-done((bf16[11,64,128]{2,1,0:T(8,128)(2,1)S(1)}, bf16[11,64,128]{2,1,0:T(8,128)(2,1)S(1)}, u32[]{:S(2)}, u32[]{:S(2)}) %collective-permute-start.7) | collective-permute-done | bytes 180256 | tf_op jit(solution)/shard_map/ppermute | solution.py:243
  21.6 2.4 %collective-permute-done.8.f1_ref = bf16[11,64,128]{2,1,0:T(8,128)(2,1)S(1)} collective-permute-done((bf16[11,64,128]{2,1,0:T(8,128)(2,1)S(1)}, bf16[11,64,128]{2,1,0:T(8,128)(2,1)S(1)}, u32[]{:S(2)}, u32[]{:S(2)}) %collective-permute-start.8) | collective-permute-done | bytes 180256 | tf_op jit(solution)/shard_map/ppermute | solution.py:244
  24.0 0.0 copy-start.4
  24.0 5.4 %far.1 = (f32[24,64,64]{2,1,0:T(8,128)S(1)}, f32[24,64,64]{2,1,0:T(8,128)S(1)}, f32[6,64,64]{2,1,0:T(8,128)S(1)}) custom-call(s32[8,24]{1,0:T(8,128)} %bitcast.36, s32[1,24]{1,0:T(1,128)} %count_hbm.1, s32[6,1,24]{2,1,0:T(1,128)} %bitcast.37, s32[6,1,6]{2,1,0:T(1,128)} %bitcast.38, bf16[12,64,128]{2,1,0:T(8,128)(2,1)S(1)} %get-tuple-element.15.cp_ref, ...), custom_call_target="tpu_custom_call" | custom-call | flops 200000000 | bytes 12000000 | tf_op jit(solution)/shard_map/far/pallas_call | solution.py:258
  29.4 0.0 collective-permute-done.6.over_ref
  29.4 0.0 copy-done
  29.4 0.0 copy-done.1
  29.5 1.8 %down.1 = bf16[24,64,64]{2,1,0:T(8,128)(2,1)} custom-call(bf16[2,32,128]{2,1,0:T(8,128)(2,1)S(1)} %add_convert_fusion.own_ref, bf16[2,32,128]{2,1,0:T(8,128)(2,1)S(1)} %collective-permute-done.6.over_ref, bf16[4,64,64]{2,1,0:T(8,128)(2,1)S(1)} %bitcast.26, bf16[1,64,64]{2,1,0:T(8,128)(2,1)S(1)} %bitcast.27, bf16[6,64,64]{2,1,0:T(8,128)(2,1)S(1)} %bitcast.25, ...), custom_call_target="tpu_custom_call" | custom-call | flops 30000000 | bytes 4000000 | tf_op jit(solution)/shard_map/down/pallas_call | solution.py:278
  (11 shorter events, 0.0 us)
Async XLA Ops:
  3.0 3.7 %collective-permute-start = (bf16[32,128]{1,0:T(8,128)(2,1)S(1)}, bf16[32,128]{1,0:T(8,128)(2,1)S(1)}, u32[]{:S(2)}, u32[]{:S(2)}) collective-permute-start(bf16[32,128]{1,0:T(8,128)(2,1)S(1)} %get-tuple-element.14), channel_id=1, source_target_pairs={{0,4},{1,5},{2,6},{3,7},{4,0},{5,1},{6,2},{7,3},{8,12},{9,13},{10,... | collective-permute-start | bytes 24584 | tf_op jit(solution)/shard_map/ppermute | solution.py:238
  4.6 4.5 %collective-permute-start.2 = (bf16[32,128]{1,0:T(8,128)(2,1)S(1)}, bf16[32,128]{1,0:T(8,128)(2,1)S(1)}, u32[]{:S(2)}, u32[]{:S(2)}) collective-permute-start(bf16[32,128]{1,0:T(8,128)(2,1)S(1)} %get-tuple-element.14), channel_id=1, source_target_pairs={{0,6},{1,7},{2,4},{3,5},{4,2},{5,3},{6,0},{7,1},{8,14},{9,15},{10,... | collective-permute-start | bytes 24584 | tf_op jit(solution)/shard_map/ppermute | solution.py:238
  6.1 3.7 %collective-permute-start.1 = (bf16[32,128]{1,0:T(8,128)(2,1)S(1)}, bf16[32,128]{1,0:T(8,128)(2,1)S(1)}, u32[]{:S(2)}, u32[]{:S(2)}) collective-permute-start(bf16[32,128]{1,0:T(8,128)(2,1)S(1)} %get-tuple-element.14), channel_id=1, source_target_pairs={{0,2},{1,3},{2,0},{3,1},{4,6},{5,7},{6,4},{7,5},{8,10},{9,11},{10,... | collective-permute-start | bytes 24584 | tf_op jit(solution)/shard_map/ppermute | solution.py:238
  9.7 7.9 %collective-permute-start.4 = (bf16[2,32,128]{2,1,0:T(8,128)(2,1)S(1)}, bf16[2,32,128]{2,1,0:T(8,128)(2,1)S(1)}, u32[]{:S(2)}, u32[]{:S(2)}) collective-permute-start(bf16[2,32,128]{2,1,0:T(8,128)(2,1)S(1)} %pad_maximum_fusion), channel_id=1, source_target_pairs={{0,16},{1,17},{2,18},{3,19},{4,20},{5,21},{6,22},{7,23},{8,24},{9,... | collective-permute-start | bytes 49160 | tf_op jit(solution)/shard_map/ppermute | solution.py:238
  10.1 7.5 %collective-permute-start.3 = (bf16[2,32,128]{2,1,0:T(8,128)(2,1)S(1)}, bf16[2,32,128]{2,1,0:T(8,128)(2,1)S(1)}, u32[]{:S(2)}, u32[]{:S(2)}) collective-permute-start(bf16[2,32,128]{2,1,0:T(8,128)(2,1)S(1)} %pad_maximum_fusion), channel_id=1, source_target_pairs={{0,8},{1,9},{2,10},{3,11},{4,12},{5,13},{6,14},{7,15},{8,0},{9,1},... | collective-permute-start | bytes 49160 | tf_op jit(solution)/shard_map/ppermute | solution.py:238
  10.6 7.1 %collective-permute-start.5 = (bf16[2,32,128]{2,1,0:T(8,128)(2,1)S(1)}, bf16[2,32,128]{2,1,0:T(8,128)(2,1)S(1)}, u32[]{:S(2)}, u32[]{:S(2)}) collective-permute-start(bf16[2,32,128]{2,1,0:T(8,128)(2,1)S(1)} %pad_maximum_fusion), channel_id=1, source_target_pairs={{0,24},{1,25},{2,26},{3,27},{4,28},{5,29},{6,30},{7,31},{8,16},{9,... | collective-permute-start | bytes 49160 | tf_op jit(solution)/shard_map/ppermute | solution.py:238
  14.2 7.4 %collective-permute-start.7 = (bf16[11,64,128]{2,1,0:T(8,128)(2,1)S(1)}, bf16[11,64,128]{2,1,0:T(8,128)(2,1)S(1)}, u32[]{:S(2)}, u32[]{:S(2)}) collective-permute-start(bf16[11,64,128]{2,1,0:T(8,128)(2,1)S(1)} %get-tuple-element.18), channel_id=1, source_target_pairs={{0,4},{4,0},{8,12},{12,8},{16,20},{20,16},{24,28},{28,24},{1,5},{5... | collective-permute-start | bytes 540680 | tf_op jit(solution)/shard_map/ppermute | solution.py:243
  15.7 8.3 %collective-permute-start.8 = (bf16[11,64,128]{2,1,0:T(8,128)(2,1)S(1)}, bf16[11,64,128]{2,1,0:T(8,128)(2,1)S(1)}, u32[]{:S(2)}, u32[]{:S(2)}) collective-permute-start(bf16[11,64,128]{2,1,0:T(8,128)(2,1)S(1)} %get-tuple-element.19), channel_id=1, source_target_pairs={{4,8},{8,4},{12,16},{16,12},{20,24},{24,20},{5,9},{9,5},{13,17},{1... | collective-permute-start | bytes 540680 | tf_op jit(solution)/shard_map/ppermute | solution.py:244
  17.7 11.7 %collective-permute-start.6 = (bf16[2,32,128]{2,1,0:T(8,128)(2,1)S(1)}, bf16[2,32,128]{2,1,0:T(8,128)(2,1)S(1)}, u32[]{:S(2)}, u32[]{:S(2)}) collective-permute-start(bf16[2,32,128]{2,1,0:T(8,128)(2,1)S(1)} %add_convert_fusion.own_ref), channel_id=1, source_target_pairs={{0,1},{1,0},{2,3},{3,2},{4,5},{5,4},{6,7},{7,6},{8,9},{9,8},{10,11... | collective-permute-start | bytes 49160 | tf_op jit(solution)/shard_map/ppermute | solution.py:238
  24.0 5.4 %copy-start = (bf16[1,24,64,64]{3,2,1,0:T(8,128)(2,1)S(1)}, bf16[1,24,64,64]{3,2,1,0:T(8,128)(2,1)}, u32[]{:S(2)}) copy-start(bf16[1,24,64,64]{3,2,1,0:T(8,128)(2,1)} %param.26) | copy-start | bytes 589828
  24.0 5.4 %copy-start.1 = (bf16[1,24,64,64]{3,2,1,0:T(8,128)(2,1)S(1)}, bf16[1,24,64,64]{3,2,1,0:T(8,128)(2,1)}, u32[]{:S(2)}) copy-start(bf16[1,24,64,64]{3,2,1,0:T(8,128)(2,1)} %param.19) | copy-start | bytes 589828
  24.0 5.4 %copy-start.2 = (bf16[1,6,64,64]{3,2,1,0:T(8,128)(2,1)S(1)}, bf16[1,6,64,64]{3,2,1,0:T(8,128)(2,1)}, u32[]{:S(2)}) copy-start(bf16[1,6,64,64]{3,2,1,0:T(8,128)(2,1)} %param.30) | copy-start | bytes 147460
  24.0 5.4 %copy-start.3 = (bf16[1,4,64,64]{3,2,1,0:T(8,128)(2,1)S(1)}, bf16[1,4,64,64]{3,2,1,0:T(8,128)(2,1)}, u32[]{:S(2)}) copy-start(bf16[1,4,64,64]{3,2,1,0:T(8,128)(2,1)} %param.33) | copy-start | bytes 98308
  24.0 5.5 %copy-start.4 = (bf16[1,1,64,64]{3,2,1,0:T(8,128)(2,1)S(1)}, bf16[1,1,64,64]{3,2,1,0:T(8,128)(2,1)}, u32[]{:S(2)}) copy-start(bf16[1,1,64,64]{3,2,1,0:T(8,128)(2,1)} %param.32) | copy-start | bytes 24580

commit v3 on v2

v3 whole, which is shorter than its diff:
```python
import jax
import jax.numpy as jnp
from jax import lax
from jax.experimental import pallas as pl
from jax.experimental.pallas import tpu as pltpu
from jax.sharding import PartitionSpec as P


REACH = 8
MREACH = 6
F32 = jnp.float32
BF16 = jnp.bfloat16
NN = (((1,), (0,)), ((), ()))
NT = (((1,), (1,)), ((), ()))


def nn(a, b):
    return lax.dot_general(a, b, NN, preferred_element_type=F32)


def nt(a, b):
    return lax.dot_general(a, b, NT, preferred_element_type=F32)


def beside(*parts):
    return jnp.concatenate(parts, axis=1)


def rows(ref, *at):
    x = ref[at]
    return x.reshape(-1, x.shape[-1])


def in_hbm(x):
    return pltpu.with_memory_space_constraint(x, pltpu.HBM)


def up_kernel(c_hbm, r_hbm, ul_hbm, um_hbm, ut_hbm, nb_hbm, lc_hbm, mc_hbm,
              cp_ref, sp_ref, mp_ref, e0_ref, e1_ref, dt_ref, nbi_ref, lci_ref, lcl_ref, mc_ref,
              c_ref, r_ref, ul_ref, um_ref, ut_ref, sems):
    n, w = c_ref.shape[:2]
    mids = um_ref.shape[0]
    copies = [
        pltpu.make_async_copy(src, dst, sems.at[j])
        for j, (src, dst) in enumerate(
            ((ut_hbm, ut_ref), (um_hbm, um_ref), (c_hbm, c_ref), (r_hbm, r_ref), (ul_hbm, ul_ref)))
    ]
    inside = pl.ds(REACH, nbi_ref.shape[0])
    later = [
        pltpu.make_async_copy(nb_hbm.at[inside], nbi_ref, sems.at[5]),
        pltpu.make_async_copy(lc_hbm.at[inside], lci_ref, sems.at[6]),
        pltpu.make_async_copy(mc_hbm, mc_ref, sems.at[7]),
        pltpu.make_async_copy(lc_hbm.at[pl.ds(0, REACH)], lcl_ref, sems.at[8]),
    ]
    for copy in copies + later:
        copy.start()
    eye = (
        lax.broadcasted_iota(jnp.int32, (w, w), 0) == lax.broadcasted_iota(jnp.int32, (w, w), 1)
    ).astype(F32).astype(BF16)
    zero = jnp.zeros((w, w), BF16)
    zeros = jnp.zeros((w, 2 * w), BF16)
    odd = lax.axis_index("wide") % 2
    for copy in copies:
        copy.wait()
    top = nn(rows(um_ref, pl.ds(0, mids)), ut_ref[0]).astype(BF16)
    cts = [nt(eye, rows(c_ref, pl.ds(4 * m, 4))).astype(BF16) for m in range(mids)]
    sts = []
    for m in range(mids):
        i = 4 * m
        blocks = jnp.concatenate([
            beside(beside(r_ref[i], zero), zeros),
            beside(beside(zero, r_ref[i + 1]), zeros),
            beside(zeros, beside(r_ref[i + 2], zero)),
            beside(zeros, beside(zero, r_ref[i + 3])),
        ], axis=0)
        sts.append(nn(cts[m], blocks).astype(BF16))
    for m in range(mids):
        cp_ref[2 * m] = cts[m][:, : 2 * w]
        cp_ref[2 * m + 1] = cts[m][:, 2 * w :]
        sp_ref[2 * m] = sts[m][:, : 2 * w]
        sp_ref[2 * m + 1] = sts[m][:, 2 * w :]
    mid = [nn(sts[m], rows(ul_ref, pl.ds(4 * m, 4))) for m in range(mids)]
    pairs = [beside(mid[2 * m], mid[2 * m + 1]).astype(BF16) for m in range(mids // 2)]
    for m in range(mids // 2):
        mp_ref[m] = pairs[m]
    term = nn(beside(*pairs), top)
    h = term.shape[0] // 2
    dt_ref[...] = beside(term[:h], term[h:]).astype(BF16)
    half, mhalf = REACH // 2, MREACH // 2
    for e_ref, right in ((e0_ref, 1 - odd), (e1_ref, odd)):
        at = right * (n // 2 - half)
        mat = right * (mids // 2 - mhalf)
        for k in range(half):
            e_ref[k] = cp_ref[at + k]
            e_ref[half + k] = sp_ref[at + k]
        for k in range(mhalf):
            e_ref[2 * half + k] = mp_ref[mat + k]
    for copy in later:
        copy.wait()


def double(pair, lo, tab, at):
    w = pair.shape[1] // 2
    turned = beside(pair[:, w:], pair[:, :w])
    tab[at] = jnp.where(lo, pair, turned)
    tab[at + 1] = jnp.where(lo, turned, pair)


def low(w):
    return lax.broadcasted_iota(jnp.int32, (w, 2 * w), 1) < w


def side(lo, tab, idx):
    return beside(*[jnp.where(lo, tab[idx[k]], tab[idx[k + 1]]) for k in range(0, len(idx), 2)])


def lists_in(near_hbm, count_hbm, far_hbm, ni_ref, nc_ref, fi_ref, sems):
    return [
        pltpu.make_async_copy(src, dst, sems.at[j])
        for j, (src, dst) in enumerate(((near_hbm, ni_ref), (count_hbm, nc_ref), (far_hbm, fi_ref)))
    ]


def inner_kernel(near_hbm, count_hbm, far_hbm, cp_ref, sp_ref, nb_ref, lc_ref, nb_hbm, lc_hbm,
                 near_ref, lf_ref, c2_ref, s2_ref, nbo_ref, lcr_ref, ni_ref, nc_ref, fi_ref, small, big):
    slots, fars = nb_ref.shape[1], lc_ref.shape[1]
    n = s2_ref.shape[0]
    inside = near_ref.shape[0]
    right = pl.ds(n - REACH, REACH)
    later = [
        pltpu.make_async_copy(nb_hbm.at[pl.ds(0, REACH)], nbo_ref.at[pl.ds(0, REACH)], big.at[0]),
        pltpu.make_async_copy(nb_hbm.at[right], nbo_ref.at[pl.ds(REACH, REACH)], big.at[1]),
        pltpu.make_async_copy(lc_hbm.at[right], lcr_ref, big.at[2]),
    ]
    w = c2_ref.shape[1]
    lists = lists_in(near_hbm, count_hbm, far_hbm, ni_ref, nc_ref, fi_ref, small)
    for copy in lists + later:
        copy.start()
    lo = low(w)

    @pl.loop(0, n // 8)
    def _(g):
        for q in range(4):
            k = 4 * g + q
            double(cp_ref[k], lo, c2_ref, 2 * k)
            double(sp_ref[k], lo, s2_ref, 2 * k)

    c2_ref[n] = jnp.zeros(c2_ref.shape[1:], BF16)
    base = lax.axis_index("wide") * n
    for copy in lists:
        copy.wait()

    @pl.loop(0, inside // 4)
    def _(g):
        for r in range(4):
            q = 4 * g + r
            i = REACH + q
            live = nc_ref[0, i]
            idx = [jnp.where(k < live, ni_ref[k, i] - base, n) for k in range(slots)]
            near_ref[q] = jnp.transpose(nn(side(lo, c2_ref, idx), rows(nb_ref, q)))
            idx = [fi_ref[k, 0, i] - base for k in range(fars)]
            lf_ref[q] = jnp.transpose(nn(side(lo, s2_ref, idx), rows(lc_ref, q)))

    for copy in later:
        copy.wait()


def outer_kernel(near_hbm, count_hbm, far_hbm, c2_ref, s2_ref, f0_ref, f1_ref, nb_ref, lcl_ref, lcr_ref,
                 near_ref, lf_ref, lc_ref, ctab, stab, ni_ref, nc_ref, fi_ref, small, big):
    slots, fars = nb_ref.shape[1], lcl_ref.shape[1]
    n = c2_ref.shape[0] - 1
    w = c2_ref.shape[1]
    copies = lists_in(near_hbm, count_hbm, far_hbm, ni_ref, nc_ref, fi_ref, small) + [
        pltpu.make_async_copy(c2_ref.at[pl.ds(0, n)], ctab.at[pl.ds(REACH, n)], big.at[0]),
        pltpu.make_async_copy(s2_ref, stab.at[pl.ds(REACH, n)], big.at[1]),
        pltpu.make_async_copy(lcl_ref, lc_ref.at[pl.ds(0, REACH)], big.at[2]),
        pltpu.make_async_copy(lcr_ref, lc_ref.at[pl.ds(REACH, REACH)], big.at[3]),
    ]
    for copy in copies:
        copy.start()
    lo = low(w)
    pos = lax.axis_index("wide")
    odd = pos % 2
    half = REACH // 2
    for f_ref, right in ((f0_ref, 1 - odd), (f1_ref, odd)):
        at = right * (n + REACH)
        for k in range(half):
            double(f_ref[k], lo, ctab, at + 2 * k)
            double(f_ref[half + k], lo, stab, at + 2 * k)
    ctab[n + 2 * REACH] = jnp.zeros(ctab.shape[1:], BF16)
    base = pos * n - REACH
    for copy in copies:
        copy.wait()

    @pl.loop(0, 2)
    def _(g):
        for q in range(REACH):
            j = g * REACH + q
            i = g * (n - REACH) + q
            live = nc_ref[0, i]
            idx = [jnp.where(k < live, ni_ref[k, i] - base, n + 2 * REACH) for k in range(slots)]
            near_ref[j] = jnp.transpose(nn(side(lo, ctab, idx), rows(nb_ref, j)))
            idx = [fi_ref[k, 0, i] - base for k in range(fars)]
            lf_ref[j] = jnp.transpose(nn(side(lo, stab, idx), rows(lc_ref, j)))


def middle_kernel(mid_hbm, mp_ref, f0_ref, f1_ref, mc_ref, mf_ref, mtab, mi_ref, small):
    mids, mfars = mc_ref.shape[:2]
    w = mtab.shape[1]
    copy = pltpu.make_async_copy(mid_hbm, mi_ref, small.at[0])
    copy.start()
    lo = low(w)
    pos = lax.axis_index("wide")
    odd = pos % 2
    for k in range(mids // 2):
        double(mp_ref[k], lo, mtab, MREACH + 2 * k)
    for f_ref, right in ((f0_ref, 1 - odd), (f1_ref, odd)):
        for k in range(MREACH // 2):
            double(f_ref[REACH + k], lo, mtab, right * (mids + MREACH) + 2 * k)
    base = pos * mids - MREACH
    copy.wait()
    for j in range(mids):
        idx = [mi_ref[j, 0, k] - base for k in range(mfars)]
        mf_ref[j] = jnp.transpose(nn(side(lo, mtab, idx), rows(mc_ref, j)))


def down_kernel(own_ref, over_ref, tc_ref, dtop_ref, dm_ref, tl_ref, cb_ref, neari_ref, lfi_ref, nearo_ref, lfo_ref, mf_ref,
                out_hbm, out_ref, sems):
    mids = dm_ref.shape[0]
    n = tl_ref.shape[0]
    me = lax.axis_index("narrow")
    acc = None
    for ref, k, h in ((own_ref, 1, me ^ 2), (over_ref, 0, me ^ 1), (over_ref, 1, me ^ 3)):
        g = ref[k]
        c = g.shape[1] // 2
        gt = jnp.concatenate([g[:, :c], g[:, c:]], axis=0)
        part = nn(gt, tc_ref[h])
        acc = part if acc is None else acc + part
    dd = nt(dtop_ref[0], acc.astype(BF16)).astype(BF16)
    down = nn(rows(dm_ref, pl.ds(0, mids)), dd)
    r = dd.shape[0]
    copies = []
    for m in range(mids):
        md = (mf_ref[m] + down[m * r : (m + 1) * r]).astype(BF16)
        ld = nn(rows(tl_ref, pl.ds(4 * m, 4)), md)
        for q in range(4):
            i = 4 * m + q
            if REACH <= i < n - REACH:
                near, lf = neari_ref[i - REACH], lfi_ref[i - REACH]
            else:
                j = i if i < REACH else i - (n - 2 * REACH)
                near, lf = nearo_ref[j], lfo_ref[j]
            lq = (lf + ld[q * r : (q + 1) * r]).astype(BF16)
            out_ref[i] = (near + nn(cb_ref[i], lq)).astype(BF16)
        if m % 2 == 1:
            part = pl.ds(4 * (m - 1), 8)
            copy = pltpu.make_async_copy(out_ref.at[part], out_hbm.at[part], sems.at[m // 2])
            copy.start()
            copies.append(copy)
    for copy in copies:
        copy.wait()


def apply(
    charges, leaf_row_basis, leaf_column_basis, near_blocks, near_src, near_count, leaf_coupling, far_src,
    up_leaf, column_transfer_leaf, mid_coupling, mid_src, up_mid, down_mid, up_top, down_top, top_coupling,
):
    n, w, v = charges.shape[1:]
    mids = up_mid.shape[1]
    wide, narrow = lax.axis_size("wide"), lax.axis_size("narrow")
    both = ("wide", "narrow")
    pairs = REACH + MREACH // 2
    slots, fars, mfars = near_src.shape[2], far_src.shape[2], mid_src.shape[2]
    hbm = pl.BlockSpec(memory_space=pltpu.HBM)
    vm = pl.BlockSpec(memory_space=pltpu.VMEM)
    dma = pltpu.SemaphoreType.DMA

    def shp(*s, t=BF16):
        return jax.ShapeDtypeStruct(s, t)

    inside = n - 2 * REACH
    cp, sp, mp, e0, e1, term, nbi, lci, lcl, mc = pl.pallas_call(
        up_kernel,
        in_specs=[hbm] * 8,
        out_specs=[vm] * 10,
        out_shape=[shp(n // 2, v, 2 * w), shp(n // 2, v, 2 * w), shp(mids // 2, v, 2 * w),
                   shp(pairs, v, 2 * w), shp(pairs, v, 2 * w), shp(v // 2, 2 * w),
                   shp(inside, slots, w, v), shp(inside, fars, w, v), shp(REACH, fars, w, v), shp(mids, mfars, w, v)],
        scratch_shapes=[
            pltpu.VMEM((n, w, v), BF16), pltpu.VMEM((n, w, v), BF16), pltpu.VMEM((n, w, v), BF16),
            pltpu.VMEM((mids, w, v), BF16), pltpu.VMEM((1, w, v), BF16), dma((9,)),
        ],
        compiler_params=pltpu.CompilerParams(vmem_limit_bytes=16 << 20),
        cost_estimate=pl.CostEstimate(flops=30_000_000, bytes_accessed=4_000_000, transcendentals=0),
        name="up",
    )(*map(in_hbm, (charges[0], leaf_row_basis[0], up_leaf[0], up_mid[0], up_top[0],
                  near_blocks[0], leaf_coupling[0], mid_coupling[0])))

    def xor(x, dw, dn):
        return lax.ppermute(x, both, [(i * narrow + j, (i ^ dw) * narrow + (j ^ dn)) for i in range(wide) for j in range(narrow)])

    f0 = lax.ppermute(e0, "wide", [(i, i ^ 1) for i in range(wide)])
    f1 = lax.ppermute(e1, "wide", [(i, (((i + 1) ^ 1) - 1) % wide) for i in range(wide)])
    f = term.astype(F32)
    own = (f + xor(term, 1, 0).astype(F32)).astype(BF16)
    have = jnp.stack([own, xor(own, 0, 2)])
    bit = 2
    while bit < wide:
        got = have.astype(F32) + xor(have, bit, 0).astype(F32)
        if 2 * bit < wide:
            got = got + xor(have, 2 * bit, 0).astype(F32) + xor(have, 3 * bit, 0).astype(F32)
        have = got.astype(BF16)
        bit *= 4
    over = xor(have, 0, 1)

    near_list = jnp.transpose(near_src, (0, 2, 1))[0]
    far_list = jnp.transpose(far_src, (2, 0, 1))
    mid_list = jnp.transpose(mid_src, (1, 0, 2))
    raw = tuple(map(in_hbm, (near_list, near_count, far_list)))
    near_i, lf_i, c2, s2, nbo, lcr = pl.pallas_call(
        inner_kernel,
        in_specs=[hbm] * 3 + [vm] * 4 + [hbm] * 2,
        out_specs=[vm] * 6,
        out_shape=[shp(inside, w, v, t=F32), shp(inside, w, v, t=F32), shp(n + 1, v, 2 * w), shp(n, v, 2 * w),
                   shp(2 * REACH, slots, w, v), shp(REACH, fars, w, v)],
        scratch_shapes=[
            pltpu.SMEM((slots, n), jnp.int32), pltpu.SMEM((1, n), jnp.int32), pltpu.SMEM((fars, 1, n), jnp.int32),
            dma((3,)), dma((3,)),
        ],
        compiler_params=pltpu.CompilerParams(vmem_limit_bytes=12 << 20),
        cost_estimate=pl.CostEstimate(flops=60_000_000, bytes_accessed=6_000_000, transcendentals=0),
        name="inner",
    )(*raw, cp, sp, nbi, lci, in_hbm(near_blocks[0]), in_hbm(leaf_coupling[0]))
    near_o, lf_o = pl.pallas_call(
        outer_kernel,
        in_specs=[hbm] * 3 + [vm] * 7,
        out_specs=[vm] * 2,
        out_shape=[shp(2 * REACH, w, v, t=F32), shp(2 * REACH, w, v, t=F32)],
        scratch_shapes=[
            pltpu.VMEM((2 * REACH, fars, w, v), BF16),
            pltpu.VMEM((n + 2 * REACH + 1, v, 2 * w), BF16),
            pltpu.VMEM((n + 2 * REACH, v, 2 * w), BF16),
            pltpu.SMEM((slots, n), jnp.int32), pltpu.SMEM((1, n), jnp.int32), pltpu.SMEM((fars, 1, n), jnp.int32),
            dma((3,)), dma((4,)),
        ],
        compiler_params=pltpu.CompilerParams(vmem_limit_bytes=16 << 20),
        cost_estimate=pl.CostEstimate(flops=140_000_000, bytes_accessed=8_000_000, transcendentals=0),
        name="outer",
    )(*raw, c2, s2, f0, f1, nbo, lcl, lcr)
    mf = pl.pallas_call(
        middle_kernel,
        in_specs=[hbm] + [vm] * 4,
        out_specs=vm,
        out_shape=shp(mids, w, v, t=F32),
        scratch_shapes=[
            pltpu.VMEM((mids + 2 * MREACH, v, 2 * w), BF16), pltpu.SMEM((mids, 1, mfars), jnp.int32), dma((1,)),
        ],
        compiler_params=pltpu.CompilerParams(vmem_limit_bytes=8 << 20),
        cost_estimate=pl.CostEstimate(flops=20_000_000, bytes_accessed=3_000_000, transcendentals=0),
        name="middle",
    )(in_hbm(mid_list), mp, f0, f1, mc)

    out = pl.pallas_call(
        down_kernel,
        in_specs=[vm] * 12,
        out_specs=hbm,
        out_shape=shp(n, w, v),
        scratch_shapes=[pltpu.VMEM((n, w, v), BF16), dma((mids // 2,))],
        compiler_params=pltpu.CompilerParams(vmem_limit_bytes=16 << 20),
        cost_estimate=pl.CostEstimate(flops=30_000_000, bytes_accessed=4_000_000, transcendentals=0),
        name="down",
    )(have, over, top_coupling[0], down_top[0], down_mid[0], column_transfer_leaf[0], leaf_column_basis[0],
      near_i, lf_i, near_o, lf_o, mf)
    return out[None]


def solution(mesh):
    leaf = P("narrow", "wide", None, None)
    block = P("narrow", "wide", None, None, None)
    lists = P("narrow", "wide", None)
    return jax.shard_map(
        apply,
        mesh=mesh,
        in_specs=(
            leaf, leaf, leaf, block, lists, P("narrow", "wide"), block, lists,
            leaf, leaf, block, lists, leaf, leaf, leaf, leaf, P("narrow", None, None, None),
        ),
        out_specs=leaf,
        check_vma=False,
    )
```

time: 31.4 us -> 30.7 us (0.978)
  the two profiles are of different devices: /device:TPU:24 before, /device:TPU:0 now
where the time goes in v3:
time: 30.7 us; the launch traced here: 30.4 us
  starting transfers between devices  15.1 us (49%)
  Pallas kernels  9.15 us (30%)
  waiting for transfers between devices  6 us (20%)
    ppermute x6, starting transfers between devices, xor(): lax.ppermute(x, both, [(i * narrow + j, (i ^ dw) * narrow + (j ^ dn)) for...  9.79 us
    ppermute x6, waiting for transfers between devices, xor(): lax.ppermute(x, both, [(i * narrow + j, (i ^ dw) * narrow + (j ^ dn)) for...  3.64 us
    ppermute x1, starting transfers between devices, apply(): lax.ppermute(e1, 'wide', [(i, ((i + 1 ^ 1) - 1) % wide) for i in range(wi...  3.54 us
    pallas_call x1, Pallas kernels, apply(): pl.pallas_call(up_kernel, in_specs=[hbm] * 8, out_specs=[vm] * 10, out_sh...  2.37 us
    ppermute x1, waiting for transfers between devices, apply(): lax.ppermute(e1, 'wide', [(i, ((i + 1 ^ 1) - 1) % wide) for i in range(wi...  2.35 us
    pallas_call x1, Pallas kernels, apply(): pl.pallas_call(outer_kernel, in_specs=[hbm] * 3 + [vm] * 7, out_specs=[vm...  2.16 us
    pallas_call x1, Pallas kernels, apply(): pl.pallas_call(inner_kernel, in_specs=[hbm] * 3 + [vm] * 4 + [hbm] * 2, o...  1.83 us
    ppermute x1, starting transfers between devices, apply(): f0 = lax.ppermute(e0, 'wide', [(i, i ^ 1) for i in range(wide)])  1.74 us
  transfers between devices with their start and end apart: 8, of which 4 were waited for; matrix products, arithmetic and copies ran while one was open for 0% of the time, Pallas kernels for 17%

profile of v3, /device:TPU:0, one launch (start us, length us, event | category | flops | bytes accessed | tf_op | source)
XLA Modules:
  0.0 30.4 jit_solution(393938839853261991)
XLA Ops:
  0.0 2.4 %up.1 = (bf16[12,64,128]{2,1,0:T(8,128)(2,1)S(1)}, bf16[12,64,128]{2,1,0:T(8,128)(2,1)S(1)}, bf16[3,64,128]{2,1,0:T(8,128)(2,1)S(1)}, bf16[11,64,128]{2,1,0:T(8,...) custom-call(bf16[24,64,64]{2,1,0:T(8,128)(2,1)} %bitcast.31, ...), custom_call_target="tpu_custom_call" | custom-call | flops 30000000 | bytes 4000000 | tf_op jit(solution)/shard_map/up/pallas_call | solution.py:282
  2.4 3.1 %collective-permute-start = (bf16[32,128]{1,0:T(8,128)(2,1)S(1)}, bf16[32,128]{1,0:T(8,128)(2,1)S(1)}, u32[]{:S(2)}, u32[]{:S(2)}) collective-permute-start(bf16[32,128]{1,0:T(8,128)(2,1)S(1)} %get-tuple-element.23), channel_id=1, source_target_pairs={{0,4},{1,5},{2,6},{3,7},{4,0},{5,1},{6,2},{7,3},{8,12},{9,13},{10,... | collective-permute-start | bytes 24584 | tf_op jit(solution)/shard_map/ppermute | solution.py:300
  5.4 1.6 %collective-permute-done = bf16[32,128]{1,0:T(8,128)(2,1)S(1)} collective-permute-done((bf16[32,128]{1,0:T(8,128)(2,1)S(1)}, bf16[32,128]{1,0:T(8,128)(2,1)S(1)}, u32[]{:S(2)}, u32[]{:S(2)}) %collective-permute-start) | collective-permute-done | bytes 8224 | tf_op jit(solution)/shard_map/ppermute | solution.py:300
  7.1 2.0 %collective-permute-start.1 = (bf16[32,128]{1,0:T(8,128)(2,1)S(1)}, bf16[32,128]{1,0:T(8,128)(2,1)S(1)}, u32[]{:S(2)}, u32[]{:S(2)}) collective-permute-start(bf16[32,128]{1,0:T(8,128)(2,1)S(1)} %add_convert_fusion.1), channel_id=1, source_target_pairs={{0,2},{1,3},{2,0},{3,1},{4,6},{5,7},{6,4},{7,5},{8,10},{9,11},{10,... | collective-permute-start | bytes 24584 | tf_op jit(solution)/shard_map/ppermute | solution.py:300
  9.1 1.7 %collective-permute-done.1 = bf16[32,128]{1,0:T(8,128)(2,1)S(1)} collective-permute-done((bf16[32,128]{1,0:T(8,128)(2,1)S(1)}, bf16[32,128]{1,0:T(8,128)(2,1)S(1)}, u32[]{:S(2)}, u32[]{:S(2)}) %collective-permute-start.1) | collective-permute-done | bytes 8224 | tf_op jit(solution)/shard_map/ppermute | solution.py:300
  10.7 3.1 %collective-permute-start.3 = (bf16[2,32,128]{2,1,0:T(8,128)(2,1)S(1)}, bf16[2,32,128]{2,1,0:T(8,128)(2,1)S(1)}, u32[]{:S(2)}, u32[]{:S(2)}) collective-permute-start(bf16[2,32,128]{2,1,0:T(8,128)(2,1)S(1)} %pad_maximum_fusion), channel_id=1, source_target_pairs={{0,16},{1,17},{2,18},{3,19},{4,20},{5,21},{6,22},{7,23},{8,24},{9,... | collective-permute-start | bytes 49160 | tf_op jit(solution)/shard_map/ppermute | solution.py:300
  13.8 1.6 %collective-permute-start.2 = (bf16[2,32,128]{2,1,0:T(8,128)(2,1)S(1)}, bf16[2,32,128]{2,1,0:T(8,128)(2,1)S(1)}, u32[]{:S(2)}, u32[]{:S(2)}) collective-permute-start(bf16[2,32,128]{2,1,0:T(8,128)(2,1)S(1)} %pad_maximum_fusion), channel_id=1, source_target_pairs={{0,8},{1,9},{2,10},{3,11},{4,12},{5,13},{6,14},{7,15},{8,0},{9,1},... | collective-permute-start | bytes 49160 | tf_op jit(solution)/shard_map/ppermute | solution.py:300
  15.4 0.0 collective-permute-start.4
  15.4 1.7 %collective-permute-start.6 = (bf16[11,64,128]{2,1,0:T(8,128)(2,1)S(1)}, bf16[11,64,128]{2,1,0:T(8,128)(2,1)S(1)}, u32[]{:S(2)}, u32[]{:S(2)}) collective-permute-start(bf16[11,64,128]{2,1,0:T(8,128)(2,1)S(1)} %get-tuple-element.32), channel_id=1, source_target_pairs={{0,4},{4,0},{8,12},{12,8},{16,20},{20,16},{24,28},{28,24},{1,5},{5... | collective-permute-start | bytes 540680 | tf_op jit(solution)/shard_map/ppermute | solution.py:302
  17.1 3.5 %collective-permute-start.7 = (bf16[11,64,128]{2,1,0:T(8,128)(2,1)S(1)}, bf16[11,64,128]{2,1,0:T(8,128)(2,1)S(1)}, u32[]{:S(2)}, u32[]{:S(2)}) collective-permute-start(bf16[11,64,128]{2,1,0:T(8,128)(2,1)S(1)} %get-tuple-element.33), channel_id=1, source_target_pairs={{0,28},{4,8},{8,4},{12,16},{16,12},{20,24},{24,20},{28,0},{1,29},{... | collective-permute-start | bytes 540680 | tf_op jit(solution)/shard_map/ppermute | solution.py:303
  20.7 0.0 collective-permute-done.3
  20.7 0.3 %collective-permute-done.4 = bf16[2,32,128]{2,1,0:T(8,128)(2,1)S(1)} collective-permute-done((bf16[2,32,128]{2,1,0:T(8,128)(2,1)S(1)}, bf16[2,32,128]{2,1,0:T(8,128)(2,1)S(1)}, u32[]{:S(2)}, u32[]{:S(2)}) %collective-permute-start.4) | collective-permute-done | bytes 16416 | tf_op jit(solution)/shard_map/ppermute | solution.py:300
  21.1 0.1 collective-permute-start.5
  21.1 1.8 %inner.1 = (f32[8,64,64]{2,1,0:T(8,128)S(1)}, f32[8,64,64]{2,1,0:T(8,128)S(1)}, bf16[25,64,128]{2,1,0:T(8,128)(2,1)S(1)}, bf16[24,64,128]{2,1,0:T(8,128)(2,1)S(1...) custom-call(s32[8,24]{1,0:T(8,128)} %bitcast.40, s32[1,24]{1,0:T(1,128)} %count_hbm.3, ...), custom_call_target="tpu_custom_call" | custom-call | flops 60000000 | bytes 6000000 | tf_op jit(solution)/shard_map/inner/pallas_call | solution.py:320
  23.0 2.4 %collective-permute-done.7.f1_ref = bf16[11,64,128]{2,1,0:T(8,128)(2,1)S(1)} collective-permute-done((bf16[11,64,128]{2,1,0:T(8,128)(2,1)S(1)}, bf16[11,64,128]{2,1,0:T(8,128)(2,1)S(1)}, u32[]{:S(2)}, u32[]{:S(2)}) %collective-permute-start.7) | collective-permute-done | bytes 180256 | tf_op jit(solution)/shard_map/ppermute | solution.py:303
  25.3 1.1 %middle.1.mf_ref = f32[6,64,64]{2,1,0:T(8,128)S(1)} custom-call(s32[6,1,6]{2,1,0:T(1,128)} %bitcast.44, bf16[3,64,128]{2,1,0:T(8,128)(2,1)S(1)} %get-tuple-element.39.mp_ref, bf16[11,64,128]{2,1,0:T(8,128)(2,1)S(1)} %collective-permute-done.6.f0_ref, bf16[11,64,128]{2,1,0:T(8,128)(2,1)S(1)} %collective-permute-done.7.f1_ref, ...), custom_call_target="tpu_custom_call" | custom-call | flops 20000000 | bytes 3000000 | tf_op jit(solution)/shard_map/middle/pallas_call | solution.py:350
  26.4 0.0 copy-start
  26.4 0.0 copy-start.1
  26.5 0.0 copy-start.2
  26.5 0.0 copy-start.3
  26.5 0.0 copy-start.4
  26.5 2.2 %outer.1 = (f32[16,64,64]{2,1,0:T(8,128)S(1)}, f32[16,64,64]{2,1,0:T(8,128)S(1)}) custom-call(s32[8,24]{1,0:T(8,128)} %bitcast.41, s32[1,24]{1,0:T(1,128)} %count_hbm.3, s32[6,1,24]{2,1,0:T(1,128)} %bitcast.43, bf16[25,64,128]{2,1,0:T(8,128)(2,1)S(1)} %get-tuple-element.30.c2_ref, bf16[24,64,128]{2,1,0:T(8,128)(2,1)S(1)} %get-tuple-element.31.s2_ref, ...), custom_call_target="tpu_custom_call" | custom-call | flops 140000000 | bytes 8000000 | tf_op jit(solution)/shard_map/outer/pallas_call | solution.py:334
  28.7 0.0 collective-permute-done.5.over_ref
  28.7 1.7 %down.1 = bf16[24,64,64]{2,1,0:T(8,128)(2,1)} custom-call(bf16[2,32,128]{2,1,0:T(8,128)(2,1)S(1)} %add_convert_fusion.own_ref, bf16[2,32,128]{2,1,0:T(8,128)(2,1)S(1)} %collective-permute-done.5.over_ref, bf16[4,64,64]{2,1,0:T(8,128)(2,1)S(1)} %bitcast.24, bf16[1,64,64]{2,1,0:T(8,128)(2,1)S(1)} %bitcast.25, bf16[6,64,64]{2,1,0:T(8,128)(2,1)S(1)} %bitcast.23, ...), custom_call_target="tpu_custom_call" | custom-call | flops 30000000 | bytes 4000000 | tf_op jit(solution)/shard_map/down/pallas_call | solution.py:363
  (10 shorter events, 0.0 us)
Async XLA Ops:
  2.4 4.7 %collective-permute-start = (bf16[32,128]{1,0:T(8,128)(2,1)S(1)}, bf16[32,128]{1,0:T(8,128)(2,1)S(1)}, u32[]{:S(2)}, u32[]{:S(2)}) collective-permute-start(bf16[32,128]{1,0:T(8,128)(2,1)S(1)} %get-tuple-element.23), channel_id=1, source_target_pairs={{0,4},{1,5},{2,6},{3,7},{4,0},{5,1},{6,2},{7,3},{8,12},{9,13},{10,... | collective-permute-start | bytes 24584 | tf_op jit(solution)/shard_map/ppermute | solution.py:300
  7.1 3.7 %collective-permute-start.1 = (bf16[32,128]{1,0:T(8,128)(2,1)S(1)}, bf16[32,128]{1,0:T(8,128)(2,1)S(1)}, u32[]{:S(2)}, u32[]{:S(2)}) collective-permute-start(bf16[32,128]{1,0:T(8,128)(2,1)S(1)} %add_convert_fusion.1), channel_id=1, source_target_pairs={{0,2},{1,3},{2,0},{3,1},{4,6},{5,7},{6,4},{7,5},{8,10},{9,11},{10,... | collective-permute-start | bytes 24584 | tf_op jit(solution)/shard_map/ppermute | solution.py:300
  10.7 10.0 %collective-permute-start.3 = (bf16[2,32,128]{2,1,0:T(8,128)(2,1)S(1)}, bf16[2,32,128]{2,1,0:T(8,128)(2,1)S(1)}, u32[]{:S(2)}, u32[]{:S(2)}) collective-permute-start(bf16[2,32,128]{2,1,0:T(8,128)(2,1)S(1)} %pad_maximum_fusion), channel_id=1, source_target_pairs={{0,16},{1,17},{2,18},{3,19},{4,20},{5,21},{6,22},{7,23},{8,24},{9,... | collective-permute-start | bytes 49160 | tf_op jit(solution)/shard_map/ppermute | solution.py:300
  13.8 6.9 %collective-permute-start.2 = (bf16[2,32,128]{2,1,0:T(8,128)(2,1)S(1)}, bf16[2,32,128]{2,1,0:T(8,128)(2,1)S(1)}, u32[]{:S(2)}, u32[]{:S(2)}) collective-permute-start(bf16[2,32,128]{2,1,0:T(8,128)(2,1)S(1)} %pad_maximum_fusion), channel_id=1, source_target_pairs={{0,8},{1,9},{2,10},{3,11},{4,12},{5,13},{6,14},{7,15},{8,0},{9,1},... | collective-permute-start | bytes 49160 | tf_op jit(solution)/shard_map/ppermute | solution.py:300
  15.4 5.6 %collective-permute-start.4 = (bf16[2,32,128]{2,1,0:T(8,128)(2,1)S(1)}, bf16[2,32,128]{2,1,0:T(8,128)(2,1)S(1)}, u32[]{:S(2)}, u32[]{:S(2)}) collective-permute-start(bf16[2,32,128]{2,1,0:T(8,128)(2,1)S(1)} %pad_maximum_fusion), channel_id=1, source_target_pairs={{0,24},{1,25},{2,26},{3,27},{4,28},{5,29},{6,30},{7,31},{8,16},{9,... | collective-permute-start | bytes 49160 | tf_op jit(solution)/shard_map/ppermute | solution.py:300
  15.4 7.6 %collective-permute-start.6 = (bf16[11,64,128]{2,1,0:T(8,128)(2,1)S(1)}, bf16[11,64,128]{2,1,0:T(8,128)(2,1)S(1)}, u32[]{:S(2)}, u32[]{:S(2)}) collective-permute-start(bf16[11,64,128]{2,1,0:T(8,128)(2,1)S(1)} %get-tuple-element.32), channel_id=1, source_target_pairs={{0,4},{4,0},{8,12},{12,8},{16,20},{20,16},{24,28},{28,24},{1,5},{5... | collective-permute-start | bytes 540680 | tf_op jit(solution)/shard_map/ppermute | solution.py:302
  17.1 8.2 %collective-permute-start.7 = (bf16[11,64,128]{2,1,0:T(8,128)(2,1)S(1)}, bf16[11,64,128]{2,1,0:T(8,128)(2,1)S(1)}, u32[]{:S(2)}, u32[]{:S(2)}) collective-permute-start(bf16[11,64,128]{2,1,0:T(8,128)(2,1)S(1)} %get-tuple-element.33), channel_id=1, source_target_pairs={{0,28},{4,8},{8,4},{12,16},{16,12},{20,24},{24,20},{28,0},{1,29},{... | collective-permute-start | bytes 540680 | tf_op jit(solution)/shard_map/ppermute | solution.py:303
  21.1 7.6 %collective-permute-start.5 = (bf16[2,32,128]{2,1,0:T(8,128)(2,1)S(1)}, bf16[2,32,128]{2,1,0:T(8,128)(2,1)S(1)}, u32[]{:S(2)}, u32[]{:S(2)}) collective-permute-start(bf16[2,32,128]{2,1,0:T(8,128)(2,1)S(1)} %add_convert_fusion.own_ref), channel_id=1, source_target_pairs={{0,1},{1,0},{2,3},{3,2},{4,5},{5,4},{6,7},{7,6},{8,9},{9,8},{10,11... | collective-permute-start | bytes 49160 | tf_op jit(solution)/shard_map/ppermute | solution.py:300
  26.4 2.2 %copy-start = (bf16[1,24,64,64]{3,2,1,0:T(8,128)(2,1)S(1)}, bf16[1,24,64,64]{3,2,1,0:T(8,128)(2,1)}, u32[]{:S(2)}) copy-start(bf16[1,24,64,64]{3,2,1,0:T(8,128)(2,1)} %param.26) | copy-start | bytes 589828
  26.4 2.2 %copy-start.1 = (bf16[1,24,64,64]{3,2,1,0:T(8,128)(2,1)S(1)}, bf16[1,24,64,64]{3,2,1,0:T(8,128)(2,1)}, u32[]{:S(2)}) copy-start(bf16[1,24,64,64]{3,2,1,0:T(8,128)(2,1)} %param.19) | copy-start | bytes 589828
  26.5 2.2 %copy-start.2 = (bf16[1,6,64,64]{3,2,1,0:T(8,128)(2,1)S(1)}, bf16[1,6,64,64]{3,2,1,0:T(8,128)(2,1)}, u32[]{:S(2)}) copy-start(bf16[1,6,64,64]{3,2,1,0:T(8,128)(2,1)} %param.30) | copy-start | bytes 147460
  26.5 2.2 %copy-start.3 = (bf16[1,4,64,64]{3,2,1,0:T(8,128)(2,1)S(1)}, bf16[1,4,64,64]{3,2,1,0:T(8,128)(2,1)}, u32[]{:S(2)}) copy-start(bf16[1,4,64,64]{3,2,1,0:T(8,128)(2,1)} %param.33) | copy-start | bytes 98308
  26.5 2.2 %copy-start.4 = (bf16[1,1,64,64]{3,2,1,0:T(8,128)(2,1)S(1)}, bf16[1,1,64,64]{3,2,1,0:T(8,128)(2,1)}, u32[]{:S(2)}) copy-start(bf16[1,1,64,64]{3,2,1,0:T(8,128)(2,1)} %param.32) | copy-start | bytes 24580

commit v4 on v3

--- a/solution.py
+++ b/solution.py
@@ -35,22 +35,20 @@
     return pltpu.with_memory_space_constraint(x, pltpu.HBM)
 
 
-def up_kernel(c_hbm, r_hbm, ul_hbm, um_hbm, ut_hbm, nb_hbm, lc_hbm, mc_hbm,
-              cp_ref, sp_ref, mp_ref, e0_ref, e1_ref, dt_ref, nbi_ref, lci_ref, lcl_ref, mc_ref,
+def up_kernel(c_hbm, r_hbm, ul_hbm, um_hbm, ut_hbm, nb_hbm, lc_hbm,
+              cp_ref, sp_ref, mp_ref, e0_ref, e1_ref, dt_ref, nbi_ref, lci_ref,
               c_ref, r_ref, ul_ref, um_ref, ut_ref, sems):
     n, w = c_ref.shape[:2]
     mids = um_ref.shape[0]
     copies = [
         pltpu.make_async_copy(src, dst, sems.at[j])
         for j, (src, dst) in enumerate(
-            ((ut_hbm, ut_ref), (um_hbm, um_ref), (c_hbm, c_ref), (r_hbm, r_ref), (ul_hbm, ul_ref)))
+            ((c_hbm, c_ref), (r_hbm, r_ref), (ul_hbm, ul_ref), (um_hbm, um_ref), (ut_hbm, ut_ref)))
     ]
     inside = pl.ds(REACH, nbi_ref.shape[0])
     later = [
         pltpu.make_async_copy(nb_hbm.at[inside], nbi_ref, sems.at[5]),
         pltpu.make_async_copy(lc_hbm.at[inside], lci_ref, sems.at[6]),
-        pltpu.make_async_copy(mc_hbm, mc_ref, sems.at[7]),
-        pltpu.make_async_copy(lc_hbm.at[pl.ds(0, REACH)], lcl_ref, sems.at[8]),
     ]
     for copy in copies + later:
         copy.start()
@@ -60,10 +58,11 @@
     zero = jnp.zeros((w, w), BF16)
     zeros = jnp.zeros((w, 2 * w), BF16)
     odd = lax.axis_index("wide") % 2
-    for copy in copies:
+    copies[0].wait()
+    cts = [nt(eye, rows(c_ref, pl.ds(4 * m, 4))).astype(BF16) for m in range(mids)]
+    for copy in copies[1:]:
         copy.wait()
     top = nn(rows(um_ref, pl.ds(0, mids)), ut_ref[0]).astype(BF16)
-    cts = [nt(eye, rows(c_ref, pl.ds(4 * m, 4))).astype(BF16) for m in range(mids)]
     sts = []
     for m in range(mids):
         i = 4 * m
@@ -99,11 +98,10 @@
         copy.wait()
 
 
-def double(pair, lo, tab, at):
+def both_ways(pair, tab, at):
     w = pair.shape[1] // 2
-    turned = beside(pair[:, w:], pair[:, :w])
-    tab[at] = jnp.where(lo, pair, turned)
-    tab[at + 1] = jnp.where(lo, turned, pair)
+    tab[at] = pair
+    tab[at + 1] = beside(pair[:, w:], pair[:, :w])
 
 
 def low(w):
@@ -111,7 +109,7 @@
 
 
 def side(lo, tab, idx):
-    return beside(*[jnp.where(lo, tab[idx[k]], tab[idx[k + 1]]) for k in range(0, len(idx), 2)])
+    return beside(*[jnp.where(lo, tab[idx[k]], tab[idx[k + 1] ^ 1]) for k in range(0, len(idx), 2)])
 
 
 def lists_in(near_hbm, count_hbm, far_hbm, ni_ref, nc_ref, fi_ref, sems):
@@ -122,7 +120,7 @@
 
 
 def inner_kernel(near_hbm, count_hbm, far_hbm, cp_ref, sp_ref, nb_ref, lc_ref, nb_hbm, lc_hbm,
-                 near_ref, lf_ref, c2_ref, s2_ref, nbo_ref, lcr_ref, ni_ref, nc_ref, fi_ref, small, big):
+                 near_ref, lf_ref, c2_ref, s2_ref, nbo_ref, lco_ref, ni_ref, nc_ref, fi_ref, small, big):
     slots, fars = nb_ref.shape[1], lc_ref.shape[1]
     n = s2_ref.shape[0]
     inside = near_ref.shape[0]
@@ -130,7 +128,8 @@
     later = [
         pltpu.make_async_copy(nb_hbm.at[pl.ds(0, REACH)], nbo_ref.at[pl.ds(0, REACH)], big.at[0]),
         pltpu.make_async_copy(nb_hbm.at[right], nbo_ref.at[pl.ds(REACH, REACH)], big.at[1]),
-        pltpu.make_async_copy(lc_hbm.at[right], lcr_ref, big.at[2]),
+        pltpu.make_async_copy(lc_hbm.at[pl.ds(0, REACH)], lco_ref.at[pl.ds(0, REACH)], big.at[2]),
+        pltpu.make_async_copy(lc_hbm.at[right], lco_ref.at[pl.ds(REACH, REACH)], big.at[3]),
     ]
     w = c2_ref.shape[1]
     lists = lists_in(near_hbm, count_hbm, far_hbm, ni_ref, nc_ref, fi_ref, small)
@@ -142,10 +141,11 @@
     def _(g):
         for q in range(4):
             k = 4 * g + q
-            double(cp_ref[k], lo, c2_ref, 2 * k)
-            double(sp_ref[k], lo, s2_ref, 2 * k)
-
-    c2_ref[n] = jnp.zeros(c2_ref.shape[1:], BF16)
+            both_ways(cp_ref[k], c2_ref, 2 * k)
+            both_ways(sp_ref[k], s2_ref, 2 * k)
+
+    for k in range(2):
+        c2_ref[n + k] = jnp.zeros(c2_ref.shape[1:], BF16)
     base = lax.axis_index("wide") * n
     for copy in lists:
         copy.wait()
@@ -165,16 +165,14 @@
         copy.wait()
 
 
-def outer_kernel(near_hbm, count_hbm, far_hbm, c2_ref, s2_ref, f0_ref, f1_ref, nb_ref, lcl_ref, lcr_ref,
-                 near_ref, lf_ref, lc_ref, ctab, stab, ni_ref, nc_ref, fi_ref, small, big):
-    slots, fars = nb_ref.shape[1], lcl_ref.shape[1]
-    n = c2_ref.shape[0] - 1
+def outer_kernel(near_hbm, count_hbm, far_hbm, c2_ref, s2_ref, f0_ref, f1_ref, nb_ref, lc_ref,
+                 near_ref, lf_ref, ctab, stab, ni_ref, nc_ref, fi_ref, small, big):
+    slots, fars = nb_ref.shape[1], lc_ref.shape[1]
+    n = c2_ref.shape[0] - 2
     w = c2_ref.shape[1]
     copies = lists_in(near_hbm, count_hbm, far_hbm, ni_ref, nc_ref, fi_ref, small) + [
         pltpu.make_async_copy(c2_ref.at[pl.ds(0, n)], ctab.at[pl.ds(REACH, n)], big.at[0]),
         pltpu.make_async_copy(s2_ref, stab.at[pl.ds(REACH, n)], big.at[1]),
-        pltpu.make_async_copy(lcl_ref, lc_ref.at[pl.ds(0, REACH)], big.at[2]),
-        pltpu.make_async_copy(lcr_ref, lc_ref.at[pl.ds(REACH, REACH)], big.at[3]),
     ]
     for copy in copies:
         copy.start()
@@ -185,9 +183,10 @@
     for f_ref, right in ((f0_ref, 1 - odd), (f1_ref, odd)):
         at = right * (n + REACH)
         for k in range(half):
-            double(f_ref[k], lo, ctab, at + 2 * k)
-            double(f_ref[half + k], lo, stab, at + 2 * k)
-    ctab[n + 2 * REACH] = jnp.zeros(ctab.shape[1:], BF16)
+            both_ways(f_ref[k], ctab, at + 2 * k)
+            both_ways(f_ref[half + k], stab, at + 2 * k)
+    for k in range(2):
+        ctab[n + 2 * REACH + k] = jnp.zeros(ctab.shape[1:], BF16)
     base = pos * n - REACH
     for copy in copies:
         copy.wait()
@@ -204,7 +203,7 @@
             lf_ref[j] = jnp.transpose(nn(side(lo, stab, idx), rows(lc_ref, j)))
 
 
-def middle_kernel(mid_hbm, mp_ref, f0_ref, f1_ref, mc_ref, mf_ref, mtab, mi_ref, small):
+def middle_kernel(mid_hbm, mp_ref, f0_ref, f1_ref, mc_ref, dm_ref, dtop_ref, mf_ref, both_ref, mtab, mi_ref, small):
     mids, mfars = mc_ref.shape[:2]
     w = mtab.shape[1]
     copy = pltpu.make_async_copy(mid_hbm, mi_ref, small.at[0])
@@ -213,10 +212,11 @@
     pos = lax.axis_index("wide")
     odd = pos % 2
     for k in range(mids // 2):
-        double(mp_ref[k], lo, mtab, MREACH + 2 * k)
+        both_ways(mp_ref[k], mtab, MREACH + 2 * k)
     for f_ref, right in ((f0_ref, 1 - odd), (f1_ref, odd)):
         for k in range(MREACH // 2):
-            double(f_ref[REACH + k], lo, mtab, right * (mids + MREACH) + 2 * k)
+            both_ways(f_ref[REACH + k], mtab, right * (mids + MREACH) + 2 * k)
+    both_ref[...] = nn(rows(dm_ref, pl.ds(0, mids)), dtop_ref[0]).astype(BF16)
     base = pos * mids - MREACH
     copy.wait()
     for j in range(mids):
@@ -224,9 +224,9 @@
         mf_ref[j] = jnp.transpose(nn(side(lo, mtab, idx), rows(mc_ref, j)))
 
 
-def down_kernel(own_ref, over_ref, tc_ref, dtop_ref, dm_ref, tl_ref, cb_ref, neari_ref, lfi_ref, nearo_ref, lfo_ref, mf_ref,
+def down_kernel(own_ref, over_ref, tc_ref, both_ref, tl_ref, cb_ref, neari_ref, lfi_ref, nearo_ref, lfo_ref, mf_ref,
                 out_hbm, out_ref, sems):
-    mids = dm_ref.shape[0]
+    mids = mf_ref.shape[0]
     n = tl_ref.shape[0]
     me = lax.axis_index("narrow")
     acc = None
@@ -236,9 +236,8 @@
         gt = jnp.concatenate([g[:, :c], g[:, c:]], axis=0)
         part = nn(gt, tc_ref[h])
         acc = part if acc is None else acc + part
-    dd = nt(dtop_ref[0], acc.astype(BF16)).astype(BF16)
-    down = nn(rows(dm_ref, pl.ds(0, mids)), dd)
-    r = dd.shape[0]
+    down = nt(both_ref[...], acc.astype(BF16))
+    r = tl_ref.shape[1]
     copies = []
     for m in range(mids):
         md = (mf_ref[m] + down[m * r : (m + 1) * r]).astype(BF16)
@@ -279,22 +278,22 @@
         return jax.ShapeDtypeStruct(s, t)
 
     inside = n - 2 * REACH
-    cp, sp, mp, e0, e1, term, nbi, lci, lcl, mc = pl.pallas_call(
+    cp, sp, mp, e0, e1, term, nbi, lci = pl.pallas_call(
         up_kernel,
-        in_specs=[hbm] * 8,
-        out_specs=[vm] * 10,
+        in_specs=[hbm] * 7,
+        out_specs=[vm] * 8,
         out_shape=[shp(n // 2, v, 2 * w), shp(n // 2, v, 2 * w), shp(mids // 2, v, 2 * w),
                    shp(pairs, v, 2 * w), shp(pairs, v, 2 * w), shp(v // 2, 2 * w),
-                   shp(inside, slots, w, v), shp(inside, fars, w, v), shp(REACH, fars, w, v), shp(mids, mfars, w, v)],
+                   shp(inside, slots, w, v), shp(inside, fars, w, v)],
         scratch_shapes=[
             pltpu.VMEM((n, w, v), BF16), pltpu.VMEM((n, w, v), BF16), pltpu.VMEM((n, w, v), BF16),
-            pltpu.VMEM((mids, w, v), BF16), pltpu.VMEM((1, w, v), BF16), dma((9,)),
+            pltpu.VMEM((mids, w, v), BF16), pltpu.VMEM((1, w, v), BF16), dma((7,)),
         ],
         compiler_params=pltpu.CompilerParams(vmem_limit_bytes=16 << 20),
         cost_estimate=pl.CostEstimate(flops=30_000_000, bytes_accessed=4_000_000, transcendentals=0),
         name="up",
     )(*map(in_hbm, (charges[0], leaf_row_basis[0], up_leaf[0], up_mid[0], up_top[0],
-                  near_blocks[0], leaf_coupling[0], mid_coupling[0])))
+                  near_blocks[0], leaf_coupling[0])))
 
     def xor(x, dw, dn):
         return lax.ppermute(x, both, [(i * narrow + j, (i ^ dw) * narrow + (j ^ dn)) for i in range(wide) for j in range(narrow)])
@@ -317,15 +316,15 @@
     far_list = jnp.transpose(far_src, (2, 0, 1))
     mid_list = jnp.transpose(mid_src, (1, 0, 2))
     raw = tuple(map(in_hbm, (near_list, near_count, far_list)))
-    near_i, lf_i, c2, s2, nbo, lcr = pl.pallas_call(
+    near_i, lf_i, c2, s2, nbo, lco = pl.pallas_call(
         inner_kernel,
         in_specs=[hbm] * 3 + [vm] * 4 + [hbm] * 2,
         out_specs=[vm] * 6,
-        out_shape=[shp(inside, w, v, t=F32), shp(inside, w, v, t=F32), shp(n + 1, v, 2 * w), shp(n, v, 2 * w),
-                   shp(2 * REACH, slots, w, v), shp(REACH, fars, w, v)],
+        out_shape=[shp(inside, w, v, t=F32), shp(inside, w, v, t=F32), shp(n + 2, v, 2 * w), shp(n, v, 2 * w),
+                   shp(2 * REACH, slots, w, v), shp(2 * REACH, fars, w, v)],
         scratch_shapes=[
             pltpu.SMEM((slots, n), jnp.int32), pltpu.SMEM((1, n), jnp.int32), pltpu.SMEM((fars, 1, n), jnp.int32),
-            dma((3,)), dma((3,)),
+            dma((3,)), dma((4,)),
         ],
         compiler_params=pltpu.CompilerParams(vmem_limit_bytes=12 << 20),
         cost_estimate=pl.CostEstimate(flops=60_000_000, bytes_accessed=6_000_000, transcendentals=0),
@@ -333,12 +332,11 @@
     )(*raw, cp, sp, nbi, lci, in_hbm(near_blocks[0]), in_hbm(leaf_coupling[0]))
     near_o, lf_o = pl.pallas_call(
         outer_kernel,
-        in_specs=[hbm] * 3 + [vm] * 7,
+        in_specs=[hbm] * 3 + [vm] * 6,
         out_specs=[vm] * 2,
         out_shape=[shp(2 * REACH, w, v, t=F32), shp(2 * REACH, w, v, t=F32)],
         scratch_shapes=[
-            pltpu.VMEM((2 * REACH, fars, w, v), BF16),
-            pltpu.VMEM((n + 2 * REACH + 1, v, 2 * w), BF16),
+            pltpu.VMEM((n + 2 * REACH + 2, v, 2 * w), BF16),
             pltpu.VMEM((n + 2 * REACH, v, 2 * w), BF16),
             pltpu.SMEM((slots, n), jnp.int32), pltpu.SMEM((1, n), jnp.int32), pltpu.SMEM((fars, 1, n), jnp.int32),
             dma((3,)), dma((4,)),
@@ -346,30 +344,30 @@
         compiler_params=pltpu.CompilerParams(vmem_limit_bytes=16 << 20),
         cost_estimate=pl.CostEstimate(flops=140_000_000, bytes_accessed=8_000_000, transcendentals=0),
         name="outer",
-    )(*raw, c2, s2, f0, f1, nbo, lcl, lcr)
-    mf = pl.pallas_call(
+    )(*raw, c2, s2, f0, f1, nbo, lco)
+    mf, down_both = pl.pallas_call(
         middle_kernel,
-        in_specs=[hbm] + [vm] * 4,
-        out_specs=vm,
-        out_shape=shp(mids, w, v, t=F32),
+        in_specs=[hbm] + [vm] * 6,
+        out_specs=[vm] * 2,
+        out_shape=[shp(mids, w, v, t=F32), shp(mids * w, w)],
         scratch_shapes=[
             pltpu.VMEM((mids + 2 * MREACH, v, 2 * w), BF16), pltpu.SMEM((mids, 1, mfars), jnp.int32), dma((1,)),
         ],
         compiler_params=pltpu.CompilerParams(vmem_limit_bytes=8 << 20),
         cost_estimate=pl.CostEstimate(flops=20_000_000, bytes_accessed=3_000_000, transcendentals=0),
         name="middle",
-    )(in_hbm(mid_list), mp, f0, f1, mc)
+    )(in_hbm(mid_list), mp, f0, f1, mid_coupling[0], down_mid[0], down_top[0])
 
     out = pl.pallas_call(
         down_kernel,
-        in_specs=[vm] * 12,
+        in_specs=[vm] * 11,
         out_specs=hbm,
         out_shape=shp(n, w, v),
         scratch_shapes=[pltpu.VMEM((n, w, v), BF16), dma((mids // 2,))],
         compiler_params=pltpu.CompilerParams(vmem_limit_bytes=16 << 20),
         cost_estimate=pl.CostEstimate(flops=30_000_000, bytes_accessed=4_000_000, transcendentals=0),
         name="down",
-    )(have, over, top_coupling[0], down_top[0], down_mid[0], column_transfer_leaf[0], leaf_column_basis[0],
+    )(have, over, top_coupling[0], down_both, column_transfer_leaf[0], leaf_column_basis[0],
       near_i, lf_i, near_o, lf_o, mf)
     return out[None]
 

time: 30.7 us -> 30.1 us (0.980)
  waiting for transfers between devices: 6 us -> 5.64 us
    pallas_call x4, Pallas kernels: 7.33 us -> 6.9 us  [the longest x1 2.2 us: apply(): pl.pallas_call(outer_kernel, in_specs=[hbm] * 3 + [vm] * 6, out_specs=[vm...]
    ppermute x1, waiting for transfers between devices: 2.35 us -> 2 us  [apply(): lax.ppermute(e1, 'wide', [(i, ((i + 1 ^ 1) - 1) % wide) for i in range(wi...]
  transfers between devices with their start and end apart: 8 -> 8, of which waited for: 4 -> 4; matrix products, arithmetic and copies ran while one was open for 0% -> 0% of each run, Pallas kernels for 17% -> 18%
where the time goes in v4:
time: 30.1 us; the launch traced here: 30 us
  starting transfers between devices  15.1 us (50%)
  Pallas kernels  9.03 us (30%)
  waiting for transfers between devices  5.64 us (19%)
    ppermute x6, starting transfers between devices, xor(): lax.ppermute(x, both, [(i * narrow + j, (i ^ dw) * narrow + (j ^ dn)) for...  9.8 us
    ppermute x6, waiting for transfers between devices, xor(): lax.ppermute(x, both, [(i * narrow + j, (i ^ dw) * narrow + (j ^ dn)) for...  3.64 us
    ppermute x1, starting transfers between devices, apply(): lax.ppermute(e1, 'wide', [(i, ((i + 1 ^ 1) - 1) % wide) for i in range(wi...  3.56 us
    pallas_call x1, Pallas kernels, apply(): pl.pallas_call(outer_kernel, in_specs=[hbm] * 3 + [vm] * 6, out_specs=[vm...  2.2 us
    pallas_call x1, Pallas kernels, apply(): pl.pallas_call(inner_kernel, in_specs=[hbm] * 3 + [vm] * 4 + [hbm] * 2, o...  2.13 us
    pallas_call x1, Pallas kernels, apply(): pl.pallas_call(up_kernel, in_specs=[hbm] * 7, out_specs=[vm] * 8, out_sha...  2.03 us
    ppermute x1, waiting for transfers between devices, apply(): lax.ppermute(e1, 'wide', [(i, ((i + 1 ^ 1) - 1) % wide) for i in range(wi...  2 us
    ppermute x1, starting transfers between devices, apply(): f0 = lax.ppermute(e0, 'wide', [(i, i ^ 1) for i in range(wide)])  1.73 us
  transfers between devices with their start and end apart: 8, of which 4 were waited for; matrix products, arithmetic and copies ran while one was open for 0% of the time, Pallas kernels for 18%

profile of v4, /device:TPU:0, one launch (start us, length us, event | category | flops | bytes accessed | tf_op | source)
XLA Modules:
  0.0 30.0 jit_solution(12679468461212167001)
XLA Ops:
  0.0 2.0 %up.1 = (bf16[12,64,128]{2,1,0:T(8,128)(2,1)S(1)}, bf16[12,64,128]{2,1,0:T(8,128)(2,1)S(1)}, bf16[3,64,128]{2,1,0:T(8,128)(2,1)S(1)}, bf16[11,64,128]{2,1,0:T(8,...) custom-call(bf16[24,64,64]{2,1,0:T(8,128)(2,1)} %bitcast.31, ...), custom_call_target="tpu_custom_call" | custom-call | flops 30000000 | bytes 4000000 | tf_op jit(solution)/shard_map/up/pallas_call | solution.py:281
  2.0 3.0 %collective-permute-start = (bf16[32,128]{1,0:T(8,128)(2,1)S(1)}, bf16[32,128]{1,0:T(8,128)(2,1)S(1)}, u32[]{:S(2)}, u32[]{:S(2)}) collective-permute-start(bf16[32,128]{1,0:T(8,128)(2,1)S(1)} %get-tuple-element.23), channel_id=1, source_target_pairs={{0,4},{1,5},{2,6},{3,7},{4,0},{5,1},{6,2},{7,3},{8,12},{9,13},{10,... | collective-permute-start | bytes 24584 | tf_op jit(solution)/shard_map/ppermute | solution.py:299
  5.1 1.6 %collective-permute-done = bf16[32,128]{1,0:T(8,128)(2,1)S(1)} collective-permute-done((bf16[32,128]{1,0:T(8,128)(2,1)S(1)}, bf16[32,128]{1,0:T(8,128)(2,1)S(1)}, u32[]{:S(2)}, u32[]{:S(2)}) %collective-permute-start) | collective-permute-done | bytes 8224 | tf_op jit(solution)/shard_map/ppermute | solution.py:299
  6.7 2.0 %collective-permute-start.1 = (bf16[32,128]{1,0:T(8,128)(2,1)S(1)}, bf16[32,128]{1,0:T(8,128)(2,1)S(1)}, u32[]{:S(2)}, u32[]{:S(2)}) collective-permute-start(bf16[32,128]{1,0:T(8,128)(2,1)S(1)} %add_convert_fusion.1), channel_id=1, source_target_pairs={{0,2},{1,3},{2,0},{3,1},{4,6},{5,7},{6,4},{7,5},{8,10},{9,11},{10,... | collective-permute-start | bytes 24584 | tf_op jit(solution)/shard_map/ppermute | solution.py:299
  8.7 1.7 %collective-permute-done.1 = bf16[32,128]{1,0:T(8,128)(2,1)S(1)} collective-permute-done((bf16[32,128]{1,0:T(8,128)(2,1)S(1)}, bf16[32,128]{1,0:T(8,128)(2,1)S(1)}, u32[]{:S(2)}, u32[]{:S(2)}) %collective-permute-start.1) | collective-permute-done | bytes 8224 | tf_op jit(solution)/shard_map/ppermute | solution.py:299
  10.4 2.1 %collective-permute-start.2 = (bf16[2,32,128]{2,1,0:T(8,128)(2,1)S(1)}, bf16[2,32,128]{2,1,0:T(8,128)(2,1)S(1)}, u32[]{:S(2)}, u32[]{:S(2)}) collective-permute-start(bf16[2,32,128]{2,1,0:T(8,128)(2,1)S(1)} %pad_maximum_fusion), channel_id=1, source_target_pairs={{0,8},{1,9},{2,10},{3,11},{4,12},{5,13},{6,14},{7,15},{8,0},{9,1},... | collective-permute-start | bytes 49160 | tf_op jit(solution)/shard_map/ppermute | solution.py:299
  12.5 2.6 %collective-permute-start.3 = (bf16[2,32,128]{2,1,0:T(8,128)(2,1)S(1)}, bf16[2,32,128]{2,1,0:T(8,128)(2,1)S(1)}, u32[]{:S(2)}, u32[]{:S(2)}) collective-permute-start(bf16[2,32,128]{2,1,0:T(8,128)(2,1)S(1)} %pad_maximum_fusion), channel_id=1, source_target_pairs={{0,16},{1,17},{2,18},{3,19},{4,20},{5,21},{6,22},{7,23},{8,24},{9,... | collective-permute-start | bytes 49160 | tf_op jit(solution)/shard_map/ppermute | solution.py:299
  15.1 1.7 %collective-permute-start.6 = (bf16[11,64,128]{2,1,0:T(8,128)(2,1)S(1)}, bf16[11,64,128]{2,1,0:T(8,128)(2,1)S(1)}, u32[]{:S(2)}, u32[]{:S(2)}) collective-permute-start(bf16[11,64,128]{2,1,0:T(8,128)(2,1)S(1)} %get-tuple-element.25), channel_id=1, source_target_pairs={{0,4},{4,0},{8,12},{12,8},{16,20},{20,16},{24,28},{28,24},{1,5},{5... | collective-permute-start | bytes 540680 | tf_op jit(solution)/shard_map/ppermute | solution.py:301
  16.8 3.6 %collective-permute-start.7 = (bf16[11,64,128]{2,1,0:T(8,128)(2,1)S(1)}, bf16[11,64,128]{2,1,0:T(8,128)(2,1)S(1)}, u32[]{:S(2)}, u32[]{:S(2)}) collective-permute-start(bf16[11,64,128]{2,1,0:T(8,128)(2,1)S(1)} %get-tuple-element.26), channel_id=1, source_target_pairs={{0,28},{4,8},{8,4},{12,16},{16,12},{20,24},{24,20},{28,0},{1,29},{... | collective-permute-start | bytes 540680 | tf_op jit(solution)/shard_map/ppermute | solution.py:302
  20.3 0.0 collective-permute-done.2
  20.4 0.0 collective-permute-done.3
  20.4 0.3 %collective-permute-done.4 = bf16[2,32,128]{2,1,0:T(8,128)(2,1)S(1)} collective-permute-done((bf16[2,32,128]{2,1,0:T(8,128)(2,1)S(1)}, bf16[2,32,128]{2,1,0:T(8,128)(2,1)S(1)}, u32[]{:S(2)}, u32[]{:S(2)}) %collective-permute-start.4) | collective-permute-done | bytes 16416 | tf_op jit(solution)/shard_map/ppermute | solution.py:299
  20.7 0.1 collective-permute-start.5
  20.8 0.0 copy-start
  20.8 0.0 copy-start.3
  20.8 0.0 copy-start.5
  20.8 2.1 %inner.1 = (f32[8,64,64]{2,1,0:T(8,128)S(1)}, f32[8,64,64]{2,1,0:T(8,128)S(1)}, bf16[26,64,128]{2,1,0:T(8,128)(2,1)S(1)}, bf16[24,64,128]{2,1,0:T(8,128)(2,1)S(1...) custom-call(s32[8,24]{1,0:T(8,128)} %bitcast.40, s32[1,24]{1,0:T(1,128)} %count_hbm.3, ...), custom_call_target="tpu_custom_call" | custom-call | flops 60000000 | bytes 6000000 | tf_op jit(solution)/shard_map/inner/pallas_call | solution.py:319
  23.0 2.0 %collective-permute-done.7.f1_ref = bf16[11,64,128]{2,1,0:T(8,128)(2,1)S(1)} collective-permute-done((bf16[11,64,128]{2,1,0:T(8,128)(2,1)S(1)}, bf16[11,64,128]{2,1,0:T(8,128)(2,1)S(1)}, u32[]{:S(2)}, u32[]{:S(2)}) %collective-permute-start.7) | collective-permute-done | bytes 180256 | tf_op jit(solution)/shard_map/ppermute | solution.py:302
  25.0 1.1 %middle.1 = (f32[6,64,64]{2,1,0:T(8,128)S(1)}, bf16[384,64]{1,0:T(8,128)(2,1)S(1)}) custom-call(s32[6,1,6]{2,1,0:T(1,128)} %bitcast.44, bf16[3,64,128]{2,1,0:T(8,128)(2,1)S(1)} %get-tuple-element.24.mp_ref, bf16[11,64,128]{2,1,0:T(8,128)(2,1)S(1)} %collective-permute-done.6.f0_ref, bf16[11,64,128]{2,1,0:T(8,128)(2,1)S(1)} %collective-permute-done.7.f1_ref, ...), custom_call_target="tpu_custom_call" | custom-call | flops 20000000 | bytes 3000000 | tf_op jit(solution)/shard_map/middle/pallas_call | solution.py:348
  26.1 0.0 copy-start.1
  26.1 0.0 copy-start.2
  26.1 0.0 copy-start.4
  26.1 2.2 %outer.1 = (f32[16,64,64]{2,1,0:T(8,128)S(1)}, f32[16,64,64]{2,1,0:T(8,128)S(1)}) custom-call(s32[8,24]{1,0:T(8,128)} %bitcast.41, s32[1,24]{1,0:T(1,128)} %count_hbm.3, s32[6,1,24]{2,1,0:T(1,128)} %bitcast.43, bf16[26,64,128]{2,1,0:T(8,128)(2,1)S(1)} %get-tuple-element.34.c2_ref, bf16[24,64,128]{2,1,0:T(8,128)(2,1)S(1)} %get-tuple-element.35.s2_ref, ...), custom_call_target="tpu_custom_call" | custom-call | flops 140000000 | bytes 8000000 | tf_op jit(solution)/shard_map/outer/pallas_call | solution.py:333
  28.4 1.6 %down.1 = bf16[24,64,64]{2,1,0:T(8,128)(2,1)} custom-call(bf16[2,32,128]{2,1,0:T(8,128)(2,1)S(1)} %add_convert_fusion.own_ref, bf16[2,32,128]{2,1,0:T(8,128)(2,1)S(1)} %collective-permute-done.5.over_ref, bf16[4,64,64]{2,1,0:T(8,128)(2,1)S(1)} %bitcast.25, bf16[384,64]{1,0:T(8,128)(2,1)S(1)} %get-tuple-element.27.both_ref, bf16[24,64,64]{2,1,0:T(8,128)(2,1)S(1)} %bitcast.22, ...), custom_call_target="tpu_custom_call" | custom-call | flops 30000000 | bytes 4000000 | tf_op jit(solution)/shard_map/down/pallas_call | solution.py:361
  (12 shorter events, 0.0 us)
Async XLA Ops:
  2.0 4.7 %collective-permute-start = (bf16[32,128]{1,0:T(8,128)(2,1)S(1)}, bf16[32,128]{1,0:T(8,128)(2,1)S(1)}, u32[]{:S(2)}, u32[]{:S(2)}) collective-permute-start(bf16[32,128]{1,0:T(8,128)(2,1)S(1)} %get-tuple-element.23), channel_id=1, source_target_pairs={{0,4},{1,5},{2,6},{3,7},{4,0},{5,1},{6,2},{7,3},{8,12},{9,13},{10,... | collective-permute-start | bytes 24584 | tf_op jit(solution)/shard_map/ppermute | solution.py:299
  6.7 3.7 %collective-permute-start.1 = (bf16[32,128]{1,0:T(8,128)(2,1)S(1)}, bf16[32,128]{1,0:T(8,128)(2,1)S(1)}, u32[]{:S(2)}, u32[]{:S(2)}) collective-permute-start(bf16[32,128]{1,0:T(8,128)(2,1)S(1)} %add_convert_fusion.1), channel_id=1, source_target_pairs={{0,2},{1,3},{2,0},{3,1},{4,6},{5,7},{6,4},{7,5},{8,10},{9,11},{10,... | collective-permute-start | bytes 24584 | tf_op jit(solution)/shard_map/ppermute | solution.py:299
  10.4 10.0 %collective-permute-start.2 = (bf16[2,32,128]{2,1,0:T(8,128)(2,1)S(1)}, bf16[2,32,128]{2,1,0:T(8,128)(2,1)S(1)}, u32[]{:S(2)}, u32[]{:S(2)}) collective-permute-start(bf16[2,32,128]{2,1,0:T(8,128)(2,1)S(1)} %pad_maximum_fusion), channel_id=1, source_target_pairs={{0,8},{1,9},{2,10},{3,11},{4,12},{5,13},{6,14},{7,15},{8,0},{9,1},... | collective-permute-start | bytes 49160 | tf_op jit(solution)/shard_map/ppermute | solution.py:299
  12.5 7.9 %collective-permute-start.3 = (bf16[2,32,128]{2,1,0:T(8,128)(2,1)S(1)}, bf16[2,32,128]{2,1,0:T(8,128)(2,1)S(1)}, u32[]{:S(2)}, u32[]{:S(2)}) collective-permute-start(bf16[2,32,128]{2,1,0:T(8,128)(2,1)S(1)} %pad_maximum_fusion), channel_id=1, source_target_pairs={{0,16},{1,17},{2,18},{3,19},{4,20},{5,21},{6,22},{7,23},{8,24},{9,... | collective-permute-start | bytes 49160 | tf_op jit(solution)/shard_map/ppermute | solution.py:299
  15.1 5.6 %collective-permute-start.4 = (bf16[2,32,128]{2,1,0:T(8,128)(2,1)S(1)}, bf16[2,32,128]{2,1,0:T(8,128)(2,1)S(1)}, u32[]{:S(2)}, u32[]{:S(2)}) collective-permute-start(bf16[2,32,128]{2,1,0:T(8,128)(2,1)S(1)} %pad_maximum_fusion), channel_id=1, source_target_pairs={{0,24},{1,25},{2,26},{3,27},{4,28},{5,29},{6,30},{7,31},{8,16},{9,... | collective-permute-start | bytes 49160 | tf_op jit(solution)/shard_map/ppermute | solution.py:299
  15.1 7.9 %collective-permute-start.6 = (bf16[11,64,128]{2,1,0:T(8,128)(2,1)S(1)}, bf16[11,64,128]{2,1,0:T(8,128)(2,1)S(1)}, u32[]{:S(2)}, u32[]{:S(2)}) collective-permute-start(bf16[11,64,128]{2,1,0:T(8,128)(2,1)S(1)} %get-tuple-element.25), channel_id=1, source_target_pairs={{0,4},{4,0},{8,12},{12,8},{16,20},{20,16},{24,28},{28,24},{1,5},{5... | collective-permute-start | bytes 540680 | tf_op jit(solution)/shard_map/ppermute | solution.py:301
  16.8 8.2 %collective-permute-start.7 = (bf16[11,64,128]{2,1,0:T(8,128)(2,1)S(1)}, bf16[11,64,128]{2,1,0:T(8,128)(2,1)S(1)}, u32[]{:S(2)}, u32[]{:S(2)}) collective-permute-start(bf16[11,64,128]{2,1,0:T(8,128)(2,1)S(1)} %get-tuple-element.26), channel_id=1, source_target_pairs={{0,28},{4,8},{8,4},{12,16},{16,12},{20,24},{24,20},{28,0},{1,29},{... | collective-permute-start | bytes 540680 | tf_op jit(solution)/shard_map/ppermute | solution.py:302
  20.7 7.6 %collective-permute-start.5 = (bf16[2,32,128]{2,1,0:T(8,128)(2,1)S(1)}, bf16[2,32,128]{2,1,0:T(8,128)(2,1)S(1)}, u32[]{:S(2)}, u32[]{:S(2)}) collective-permute-start(bf16[2,32,128]{2,1,0:T(8,128)(2,1)S(1)} %add_convert_fusion.own_ref), channel_id=1, source_target_pairs={{0,1},{1,0},{2,3},{3,2},{4,5},{5,4},{6,7},{7,6},{8,9},{9,8},{10,11... | collective-permute-start | bytes 49160 | tf_op jit(solution)/shard_map/ppermute | solution.py:299
  20.8 4.2 %copy-start = (bf16[1,6,6,64,64]{4,3,2,1,0:T(8,128)(2,1)S(1)}, bf16[1,6,6,64,64]{4,3,2,1,0:T(8,128)(2,1)}, u32[]{:S(2)}) copy-start(bf16[1,6,6,64,64]{4,3,2,1,0:T(8,128)(2,1)} %param.27) | copy-start | bytes 884740
  20.8 4.2 %copy-start.3 = (bf16[1,6,64,64]{3,2,1,0:T(8,128)(2,1)S(1)}, bf16[1,6,64,64]{3,2,1,0:T(8,128)(2,1)}, u32[]{:S(2)}) copy-start(bf16[1,6,64,64]{3,2,1,0:T(8,128)(2,1)} %param.30) | copy-start | bytes 147460
  20.8 4.2 %copy-start.5 = (bf16[1,1,64,64]{3,2,1,0:T(8,128)(2,1)S(1)}, bf16[1,1,64,64]{3,2,1,0:T(8,128)(2,1)}, u32[]{:S(2)}) copy-start(bf16[1,1,64,64]{3,2,1,0:T(8,128)(2,1)} %param.32) | copy-start | bytes 24580
  26.1 2.3 %copy-start.1 = (bf16[1,24,64,64]{3,2,1,0:T(8,128)(2,1)S(1)}, bf16[1,24,64,64]{3,2,1,0:T(8,128)(2,1)}, u32[]{:S(2)}) copy-start(bf16[1,24,64,64]{3,2,1,0:T(8,128)(2,1)} %param.26) | copy-start | bytes 589828
  26.1 2.3 %copy-start.2 = (bf16[1,24,64,64]{3,2,1,0:T(8,128)(2,1)S(1)}, bf16[1,24,64,64]{3,2,1,0:T(8,128)(2,1)}, u32[]{:S(2)}) copy-start(bf16[1,24,64,64]{3,2,1,0:T(8,128)(2,1)} %param.19) | copy-start | bytes 589828
  26.1 2.2 %copy-start.4 = (bf16[1,4,64,64]{3,2,1,0:T(8,128)(2,1)S(1)}, bf16[1,4,64,64]{3,2,1,0:T(8,128)(2,1)}, u32[]{:S(2)}) copy-start(bf16[1,4,64,64]{3,2,1,0:T(8,128)(2,1)} %param.33) | copy-start | bytes 98308

commit v5 on v4

--- a/solution.py
+++ b/solution.py
@@ -251,11 +251,10 @@
                 near, lf = nearo_ref[j], lfo_ref[j]
             lq = (lf + ld[q * r : (q + 1) * r]).astype(BF16)
             out_ref[i] = (near + nn(cb_ref[i], lq)).astype(BF16)
-        if m % 2 == 1:
-            part = pl.ds(4 * (m - 1), 8)
-            copy = pltpu.make_async_copy(out_ref.at[part], out_hbm.at[part], sems.at[m // 2])
-            copy.start()
-            copies.append(copy)
+        part = pl.ds(4 * m, 4)
+        copy = pltpu.make_async_copy(out_ref.at[part], out_hbm.at[part], sems.at[m])
+        copy.start()
+        copies.append(copy)
     for copy in copies:
         copy.wait()
 
@@ -299,7 +298,11 @@
         return lax.ppermute(x, both, [(i * narrow + j, (i ^ dw) * narrow + (j ^ dn)) for i in range(wide) for j in range(narrow)])
 
     f0 = lax.ppermute(e0, "wide", [(i, i ^ 1) for i in range(wide)])
-    f1 = lax.ppermute(e1, "wide", [(i, (((i + 1) ^ 1) - 1) % wide) for i in range(wide)])
+    ends = (0, wide - 1)
+    f1 = lax.ppermute(e1, both, [
+        (i * narrow + j, i * narrow + (j ^ 1) if i in ends else (((i + 1) ^ 1) - 1) * narrow + j)
+        for i in range(wide) for j in range(narrow)
+    ])
     f = term.astype(F32)
     own = (f + xor(term, 1, 0).astype(F32)).astype(BF16)
     have = jnp.stack([own, xor(own, 0, 2)])
@@ -363,7 +366,7 @@
         in_specs=[vm] * 11,
         out_specs=hbm,
         out_shape=shp(n, w, v),
-        scratch_shapes=[pltpu.VMEM((n, w, v), BF16), dma((mids // 2,))],
+        scratch_shapes=[pltpu.VMEM((n, w, v), BF16), dma((mids,))],
         compiler_params=pltpu.CompilerParams(vmem_limit_bytes=16 << 20),
         cost_estimate=pl.CostEstimate(flops=30_000_000, bytes_accessed=4_000_000, transcendentals=0),
         name="down",

time: 30.1 us -> 28.2 us (0.937)
  starting transfers between devices: 15.1 us -> 11.5 us
  waiting for transfers between devices: 5.64 us -> 7.2 us
    ppermute x1, starting transfers between devices: 3.56 us -> 0.01 us  [apply(): lax.ppermute(e1, both, [(i * narrow + j, i * narrow + (j ^ 1) if i in end...]
    ppermute x6, waiting for transfers between devices: 3.64 us -> 7.19 us  [xor(): lax.ppermute(x, both, [(i * narrow + j, (i ^ dw) * narrow + (j ^ dn)) for...]
    ppermute x1, waiting for transfers between devices: 2 us -> 0.01 us  [apply(): lax.ppermute(e1, both, [(i * narrow + j, i * narrow + (j ^ 1) if i in end...]
  transfers between devices with their start and end apart: 8 -> 8, of which waited for: 4 -> 4; matrix products, arithmetic and copies ran while one was open for 0% -> 0% of each run, Pallas kernels for 18% -> 19%
where the time goes in v5:
time: 28.2 us; the launch traced here: 28 us
  starting transfers between devices  11.5 us (41%)
  Pallas kernels  9.04 us (32%)
  waiting for transfers between devices  7.2 us (26%)
    ppermute x6, starting transfers between devices, xor(): lax.ppermute(x, both, [(i * narrow + j, (i ^ dw) * narrow + (j ^ dn)) for...  9.8 us
    ppermute x6, waiting for transfers between devices, xor(): lax.ppermute(x, both, [(i * narrow + j, (i ^ dw) * narrow + (j ^ dn)) for...  7.19 us
    pallas_call x1, Pallas kernels, apply(): pl.pallas_call(outer_kernel, in_specs=[hbm] * 3 + [vm] * 6, out_specs=[vm...  2.2 us
    pallas_call x1, Pallas kernels, apply(): pl.pallas_call(inner_kernel, in_specs=[hbm] * 3 + [vm] * 4 + [hbm] * 2, o...  2.13 us
    pallas_call x1, Pallas kernels, apply(): pl.pallas_call(up_kernel, in_specs=[hbm] * 7, out_specs=[vm] * 8, out_sha...  2.03 us
    ppermute x1, starting transfers between devices, apply(): f0 = lax.ppermute(e0, 'wide', [(i, i ^ 1) for i in range(wide)])  1.73 us
    pallas_call x1, Pallas kernels, apply(): pl.pallas_call(down_kernel, in_specs=[vm] * 11, out_specs=hbm, out_shape=...  1.6 us
    pallas_call x1, Pallas kernels, apply(): pl.pallas_call(middle_kernel, in_specs=[hbm] + [vm] * 6, out_specs=[vm] *...  1.08 us
  transfers between devices with their start and end apart: 8, of which 4 were waited for; matrix products, arithmetic and copies ran while one was open for 0% of the time, Pallas kernels for 19%

profile of v5, /device:TPU:0, one launch (start us, length us, event | category | flops | bytes accessed | tf_op | source)
XLA Modules:
  0.0 28.0 jit_solution(5060103629300644920)
XLA Ops:
  0.0 2.0 %up.1 = (bf16[12,64,128]{2,1,0:T(8,128)(2,1)S(1)}, bf16[12,64,128]{2,1,0:T(8,128)(2,1)S(1)}, bf16[3,64,128]{2,1,0:T(8,128)(2,1)S(1)}, bf16[11,64,128]{2,1,0:T(8,...) custom-call(bf16[24,64,64]{2,1,0:T(8,128)(2,1)} %bitcast.31, ...), custom_call_target="tpu_custom_call" | custom-call | flops 30000000 | bytes 4000000 | tf_op jit(solution)/shard_map/up/pallas_call | solution.py:280
  2.0 3.0 %collective-permute-start = (bf16[32,128]{1,0:T(8,128)(2,1)S(1)}, bf16[32,128]{1,0:T(8,128)(2,1)S(1)}, u32[]{:S(2)}, u32[]{:S(2)}) collective-permute-start(bf16[32,128]{1,0:T(8,128)(2,1)S(1)} %get-tuple-element.23), channel_id=1, source_target_pairs={{0,4},{1,5},{2,6},{3,7},{4,0},{5,1},{6,2},{7,3},{8,12},{9,13},{10,... | collective-permute-start | bytes 24584 | tf_op jit(solution)/shard_map/ppermute | solution.py:298
  5.1 1.6 %collective-permute-done = bf16[32,128]{1,0:T(8,128)(2,1)S(1)} collective-permute-done((bf16[32,128]{1,0:T(8,128)(2,1)S(1)}, bf16[32,128]{1,0:T(8,128)(2,1)S(1)}, u32[]{:S(2)}, u32[]{:S(2)}) %collective-permute-start) | collective-permute-done | bytes 8224 | tf_op jit(solution)/shard_map/ppermute | solution.py:298
  6.7 2.0 %collective-permute-start.1 = (bf16[32,128]{1,0:T(8,128)(2,1)S(1)}, bf16[32,128]{1,0:T(8,128)(2,1)S(1)}, u32[]{:S(2)}, u32[]{:S(2)}) collective-permute-start(bf16[32,128]{1,0:T(8,128)(2,1)S(1)} %add_convert_fusion.1), channel_id=1, source_target_pairs={{0,2},{1,3},{2,0},{3,1},{4,6},{5,7},{6,4},{7,5},{8,10},{9,11},{10,... | collective-permute-start | bytes 24584 | tf_op jit(solution)/shard_map/ppermute | solution.py:298
  8.7 1.7 %collective-permute-done.1 = bf16[32,128]{1,0:T(8,128)(2,1)S(1)} collective-permute-done((bf16[32,128]{1,0:T(8,128)(2,1)S(1)}, bf16[32,128]{1,0:T(8,128)(2,1)S(1)}, u32[]{:S(2)}, u32[]{:S(2)}) %collective-permute-start.1) | collective-permute-done | bytes 8224 | tf_op jit(solution)/shard_map/ppermute | solution.py:298
  10.4 2.1 %collective-permute-start.2 = (bf16[2,32,128]{2,1,0:T(8,128)(2,1)S(1)}, bf16[2,32,128]{2,1,0:T(8,128)(2,1)S(1)}, u32[]{:S(2)}, u32[]{:S(2)}) collective-permute-start(bf16[2,32,128]{2,1,0:T(8,128)(2,1)S(1)} %pad_maximum_fusion), channel_id=1, source_target_pairs={{0,8},{1,9},{2,10},{3,11},{4,12},{5,13},{6,14},{7,15},{8,0},{9,1},... | collective-permute-start | bytes 49160 | tf_op jit(solution)/shard_map/ppermute | solution.py:298
  12.5 2.6 %collective-permute-start.3 = (bf16[2,32,128]{2,1,0:T(8,128)(2,1)S(1)}, bf16[2,32,128]{2,1,0:T(8,128)(2,1)S(1)}, u32[]{:S(2)}, u32[]{:S(2)}) collective-permute-start(bf16[2,32,128]{2,1,0:T(8,128)(2,1)S(1)} %pad_maximum_fusion), channel_id=1, source_target_pairs={{0,16},{1,17},{2,18},{3,19},{4,20},{5,21},{6,22},{7,23},{8,24},{9,... | collective-permute-start | bytes 49160 | tf_op jit(solution)/shard_map/ppermute | solution.py:298
  15.1 1.7 %collective-permute-start.6 = (bf16[11,64,128]{2,1,0:T(8,128)(2,1)S(1)}, bf16[11,64,128]{2,1,0:T(8,128)(2,1)S(1)}, u32[]{:S(2)}, u32[]{:S(2)}) collective-permute-start(bf16[11,64,128]{2,1,0:T(8,128)(2,1)S(1)} %get-tuple-element.25), channel_id=1, source_target_pairs={{0,4},{4,0},{8,12},{12,8},{16,20},{20,16},{24,28},{28,24},{1,5},{5... | collective-permute-start | bytes 540680 | tf_op jit(solution)/shard_map/ppermute | solution.py:300
  16.8 0.0 collective-permute-start.7
  16.8 0.0 collective-permute-done.2
  16.8 0.5 %collective-permute-done.3 = bf16[2,32,128]{2,1,0:T(8,128)(2,1)S(1)} collective-permute-done((bf16[2,32,128]{2,1,0:T(8,128)(2,1)S(1)}, bf16[2,32,128]{2,1,0:T(8,128)(2,1)S(1)}, u32[]{:S(2)}, u32[]{:S(2)}) %collective-permute-start.3) | collective-permute-done | bytes 16416 | tf_op jit(solution)/shard_map/ppermute | solution.py:298
  17.3 3.4 %collective-permute-done.4 = bf16[2,32,128]{2,1,0:T(8,128)(2,1)S(1)} collective-permute-done((bf16[2,32,128]{2,1,0:T(8,128)(2,1)S(1)}, bf16[2,32,128]{2,1,0:T(8,128)(2,1)S(1)}, u32[]{:S(2)}, u32[]{:S(2)}) %collective-permute-start.4) | collective-permute-done | bytes 16416 | tf_op jit(solution)/shard_map/ppermute | solution.py:298
  20.7 0.1 collective-permute-start.5
  20.8 0.0 copy-start
  20.8 0.0 copy-start.3
  20.8 0.0 copy-start.5
  20.8 2.1 %inner.1 = (f32[8,64,64]{2,1,0:T(8,128)S(1)}, f32[8,64,64]{2,1,0:T(8,128)S(1)}, bf16[26,64,128]{2,1,0:T(8,128)(2,1)S(1)}, bf16[24,64,128]{2,1,0:T(8,128)(2,1)S(1...) custom-call(s32[8,24]{1,0:T(8,128)} %bitcast.40, s32[1,24]{1,0:T(1,128)} %count_hbm.3, ...), custom_call_target="tpu_custom_call" | custom-call | flops 60000000 | bytes 6000000 | tf_op jit(solution)/shard_map/inner/pallas_call | solution.py:322
  23.0 0.0 collective-permute-done.7.f1_ref
  23.0 1.1 %middle.1 = (f32[6,64,64]{2,1,0:T(8,128)S(1)}, bf16[384,64]{1,0:T(8,128)(2,1)S(1)}) custom-call(s32[6,1,6]{2,1,0:T(1,128)} %bitcast.44, bf16[3,64,128]{2,1,0:T(8,128)(2,1)S(1)} %get-tuple-element.24.mp_ref, bf16[11,64,128]{2,1,0:T(8,128)(2,1)S(1)} %collective-permute-done.6.f0_ref, bf16[11,64,128]{2,1,0:T(8,128)(2,1)S(1)} %collective-permute-done.7.f1_ref, ...), custom_call_target="tpu_custom_call" | custom-call | flops 20000000 | bytes 3000000 | tf_op jit(solution)/shard_map/middle/pallas_call | solution.py:351
  24.1 0.0 copy-start.1
  24.1 0.0 copy-start.2
  24.1 0.0 copy-start.4
  24.2 2.2 %outer.1 = (f32[16,64,64]{2,1,0:T(8,128)S(1)}, f32[16,64,64]{2,1,0:T(8,128)S(1)}) custom-call(s32[8,24]{1,0:T(8,128)} %bitcast.41, s32[1,24]{1,0:T(1,128)} %count_hbm.3, s32[6,1,24]{2,1,0:T(1,128)} %bitcast.43, bf16[26,64,128]{2,1,0:T(8,128)(2,1)S(1)} %get-tuple-element.34.c2_ref, bf16[24,64,128]{2,1,0:T(8,128)(2,1)S(1)} %get-tuple-element.35.s2_ref, ...), custom_call_target="tpu_custom_call" | custom-call | flops 140000000 | bytes 8000000 | tf_op jit(solution)/shard_map/outer/pallas_call | solution.py:336
  26.4 1.6 %down.1 = bf16[24,64,64]{2,1,0:T(8,128)(2,1)} custom-call(bf16[2,32,128]{2,1,0:T(8,128)(2,1)S(1)} %add_convert_fusion.own_ref, bf16[2,32,128]{2,1,0:T(8,128)(2,1)S(1)} %collective-permute-done.5.over_ref, bf16[4,64,64]{2,1,0:T(8,128)(2,1)S(1)} %bitcast.25, bf16[384,64]{1,0:T(8,128)(2,1)S(1)} %get-tuple-element.27.both_ref, bf16[24,64,64]{2,1,0:T(8,128)(2,1)S(1)} %bitcast.22, ...), custom_call_target="tpu_custom_call" | custom-call | flops 30000000 | bytes 4000000 | tf_op jit(solution)/shard_map/down/pallas_call | solution.py:364
  (12 shorter events, 0.0 us)
Async XLA Ops:
  2.0 4.7 %collective-permute-start = (bf16[32,128]{1,0:T(8,128)(2,1)S(1)}, bf16[32,128]{1,0:T(8,128)(2,1)S(1)}, u32[]{:S(2)}, u32[]{:S(2)}) collective-permute-start(bf16[32,128]{1,0:T(8,128)(2,1)S(1)} %get-tuple-element.23), channel_id=1, source_target_pairs={{0,4},{1,5},{2,6},{3,7},{4,0},{5,1},{6,2},{7,3},{8,12},{9,13},{10,... | collective-permute-start | bytes 24584 | tf_op jit(solution)/shard_map/ppermute | solution.py:298
  6.7 3.7 %collective-permute-start.1 = (bf16[32,128]{1,0:T(8,128)(2,1)S(1)}, bf16[32,128]{1,0:T(8,128)(2,1)S(1)}, u32[]{:S(2)}, u32[]{:S(2)}) collective-permute-start(bf16[32,128]{1,0:T(8,128)(2,1)S(1)} %add_convert_fusion.1), channel_id=1, source_target_pairs={{0,2},{1,3},{2,0},{3,1},{4,6},{5,7},{6,4},{7,5},{8,10},{9,11},{10,... | collective-permute-start | bytes 24584 | tf_op jit(solution)/shard_map/ppermute | solution.py:298
  10.4 6.4 %collective-permute-start.2 = (bf16[2,32,128]{2,1,0:T(8,128)(2,1)S(1)}, bf16[2,32,128]{2,1,0:T(8,128)(2,1)S(1)}, u32[]{:S(2)}, u32[]{:S(2)}) collective-permute-start(bf16[2,32,128]{2,1,0:T(8,128)(2,1)S(1)} %pad_maximum_fusion), channel_id=1, source_target_pairs={{0,8},{1,9},{2,10},{3,11},{4,12},{5,13},{6,14},{7,15},{8,0},{9,1},... | collective-permute-start | bytes 49160 | tf_op jit(solution)/shard_map/ppermute | solution.py:298
  12.5 4.8 %collective-permute-start.3 = (bf16[2,32,128]{2,1,0:T(8,128)(2,1)S(1)}, bf16[2,32,128]{2,1,0:T(8,128)(2,1)S(1)}, u32[]{:S(2)}, u32[]{:S(2)}) collective-permute-start(bf16[2,32,128]{2,1,0:T(8,128)(2,1)S(1)} %pad_maximum_fusion), channel_id=1, source_target_pairs={{0,16},{1,17},{2,18},{3,19},{4,20},{5,21},{6,22},{7,23},{8,24},{9,... | collective-permute-start | bytes 49160 | tf_op jit(solution)/shard_map/ppermute | solution.py:298
  15.1 5.6 %collective-permute-start.4 = (bf16[2,32,128]{2,1,0:T(8,128)(2,1)S(1)}, bf16[2,32,128]{2,1,0:T(8,128)(2,1)S(1)}, u32[]{:S(2)}, u32[]{:S(2)}) collective-permute-start(bf16[2,32,128]{2,1,0:T(8,128)(2,1)S(1)} %pad_maximum_fusion), channel_id=1, source_target_pairs={{0,24},{1,25},{2,26},{3,27},{4,28},{5,29},{6,30},{7,31},{8,16},{9,... | collective-permute-start | bytes 49160 | tf_op jit(solution)/shard_map/ppermute | solution.py:298
  15.1 7.9 %collective-permute-start.6 = (bf16[11,64,128]{2,1,0:T(8,128)(2,1)S(1)}, bf16[11,64,128]{2,1,0:T(8,128)(2,1)S(1)}, u32[]{:S(2)}, u32[]{:S(2)}) collective-permute-start(bf16[11,64,128]{2,1,0:T(8,128)(2,1)S(1)} %get-tuple-element.25), channel_id=1, source_target_pairs={{0,4},{4,0},{8,12},{12,8},{16,20},{20,16},{24,28},{28,24},{1,5},{5... | collective-permute-start | bytes 540680 | tf_op jit(solution)/shard_map/ppermute | solution.py:300
  16.8 6.2 %collective-permute-start.7 = (bf16[11,64,128]{2,1,0:T(8,128)(2,1)S(1)}, bf16[11,64,128]{2,1,0:T(8,128)(2,1)S(1)}, u32[]{:S(2)}, u32[]{:S(2)}) collective-permute-start(bf16[11,64,128]{2,1,0:T(8,128)(2,1)S(1)} %get-tuple-element.26), channel_id=1, source_target_pairs={{0,1},{1,0},{2,3},{3,2},{4,8},{5,9},{6,10},{7,11},{8,4},{9,5},{10,... | collective-permute-start | bytes 540680 | tf_op jit(solution)/shard_map/ppermute | solution.py:302
  20.7 5.6 %collective-permute-start.5 = (bf16[2,32,128]{2,1,0:T(8,128)(2,1)S(1)}, bf16[2,32,128]{2,1,0:T(8,128)(2,1)S(1)}, u32[]{:S(2)}, u32[]{:S(2)}) collective-permute-start(bf16[2,32,128]{2,1,0:T(8,128)(2,1)S(1)} %add_convert_fusion.own_ref), channel_id=1, source_target_pairs={{0,1},{1,0},{2,3},{3,2},{4,5},{5,4},{6,7},{7,6},{8,9},{9,8},{10,11... | collective-permute-start | bytes 49160 | tf_op jit(solution)/shard_map/ppermute | solution.py:298
  20.8 2.2 %copy-start = (bf16[1,6,6,64,64]{4,3,2,1,0:T(8,128)(2,1)S(1)}, bf16[1,6,6,64,64]{4,3,2,1,0:T(8,128)(2,1)}, u32[]{:S(2)}) copy-start(bf16[1,6,6,64,64]{4,3,2,1,0:T(8,128)(2,1)} %param.27) | copy-start | bytes 884740
  20.8 2.2 %copy-start.3 = (bf16[1,6,64,64]{3,2,1,0:T(8,128)(2,1)S(1)}, bf16[1,6,64,64]{3,2,1,0:T(8,128)(2,1)}, u32[]{:S(2)}) copy-start(bf16[1,6,64,64]{3,2,1,0:T(8,128)(2,1)} %param.30) | copy-start | bytes 147460
  20.8 2.2 %copy-start.5 = (bf16[1,1,64,64]{3,2,1,0:T(8,128)(2,1)S(1)}, bf16[1,1,64,64]{3,2,1,0:T(8,128)(2,1)}, u32[]{:S(2)}) copy-start(bf16[1,1,64,64]{3,2,1,0:T(8,128)(2,1)} %param.32) | copy-start | bytes 24580
  24.1 2.3 %copy-start.1 = (bf16[1,24,64,64]{3,2,1,0:T(8,128)(2,1)S(1)}, bf16[1,24,64,64]{3,2,1,0:T(8,128)(2,1)}, u32[]{:S(2)}) copy-start(bf16[1,24,64,64]{3,2,1,0:T(8,128)(2,1)} %param.26) | copy-start | bytes 589828
  24.1 2.2 %copy-start.2 = (bf16[1,24,64,64]{3,2,1,0:T(8,128)(2,1)S(1)}, bf16[1,24,64,64]{3,2,1,0:T(8,128)(2,1)}, u32[]{:S(2)}) copy-start(bf16[1,24,64,64]{3,2,1,0:T(8,128)(2,1)} %param.19) | copy-start | bytes 589828
  24.1 2.2 %copy-start.4 = (bf16[1,4,64,64]{3,2,1,0:T(8,128)(2,1)S(1)}, bf16[1,4,64,64]{3,2,1,0:T(8,128)(2,1)}, u32[]{:S(2)}) copy-start(bf16[1,4,64,64]{3,2,1,0:T(8,128)(2,1)} %param.33) | copy-start | bytes 98308

commit v6 on v5

--- a/solution.py
+++ b/solution.py
@@ -83,8 +83,7 @@
     for m in range(mids // 2):
         mp_ref[m] = pairs[m]
     term = nn(beside(*pairs), top)
-    h = term.shape[0] // 2
-    dt_ref[...] = beside(term[:h], term[h:]).astype(BF16)
+    dt_ref[...] = term.astype(BF16)
     half, mhalf = REACH // 2, MREACH // 2
     for e_ref, right in ((e0_ref, 1 - odd), (e1_ref, odd)):
         at = right * (n // 2 - half)
@@ -231,10 +230,7 @@
     me = lax.axis_index("narrow")
     acc = None
     for ref, k, h in ((own_ref, 1, me ^ 2), (over_ref, 0, me ^ 1), (over_ref, 1, me ^ 3)):
-        g = ref[k]
-        c = g.shape[1] // 2
-        gt = jnp.concatenate([g[:, :c], g[:, c:]], axis=0)
-        part = nn(gt, tc_ref[h])
+        part = nn(ref[k], tc_ref[h])
         acc = part if acc is None else acc + part
     down = nt(both_ref[...], acc.astype(BF16))
     r = tl_ref.shape[1]
@@ -282,7 +278,7 @@
         in_specs=[hbm] * 7,
         out_specs=[vm] * 8,
         out_shape=[shp(n // 2, v, 2 * w), shp(n // 2, v, 2 * w), shp(mids // 2, v, 2 * w),
-                   shp(pairs, v, 2 * w), shp(pairs, v, 2 * w), shp(v // 2, 2 * w),
+                   shp(pairs, v, 2 * w), shp(pairs, v, 2 * w), shp(v, w),
                    shp(inside, slots, w, v), shp(inside, fars, w, v)],
         scratch_shapes=[
             pltpu.VMEM((n, w, v), BF16), pltpu.VMEM((n, w, v), BF16), pltpu.VMEM((n, w, v), BF16),

time: 28.2 us -> 28.6 us (1.014)
  waiting for transfers between devices: 7.2 us -> 7.55 us
    ppermute x6, waiting for transfers between devices: 7.19 us -> 7.54 us  [xor(): lax.ppermute(x, both, [(i * narrow + j, (i ^ dw) * narrow + (j ^ dn)) for...]
where the time goes in v6:
time: 28.6 us; the launch traced here: 28.4 us
  starting transfers between devices  11.7 us (41%)
  Pallas kernels  8.91 us (31%)
  waiting for transfers between devices  7.55 us (26%)
    ppermute x6, starting transfers between devices, xor(): lax.ppermute(x, both, [(i * narrow + j, (i ^ dw) * narrow + (j ^ dn)) for...  9.93 us
    ppermute x6, waiting for transfers between devices, xor(): lax.ppermute(x, both, [(i * narrow + j, (i ^ dw) * narrow + (j ^ dn)) for...  7.54 us
    pallas_call x1, Pallas kernels, apply(): pl.pallas_call(outer_kernel, in_specs=[hbm] * 3 + [vm] * 6, out_specs=[vm...  2.2 us
    pallas_call x1, Pallas kernels, apply(): pl.pallas_call(inner_kernel, in_specs=[hbm] * 3 + [vm] * 4 + [hbm] * 2, o...  2.13 us
    pallas_call x1, Pallas kernels, apply(): pl.pallas_call(up_kernel, in_specs=[hbm] * 7, out_specs=[vm] * 8, out_sha...  1.96 us
    ppermute x1, starting transfers between devices, apply(): f0 = lax.ppermute(e0, 'wide', [(i, i ^ 1) for i in range(wide)])  1.73 us
    pallas_call x1, Pallas kernels, apply(): pl.pallas_call(down_kernel, in_specs=[vm] * 11, out_specs=hbm, out_shape=...  1.55 us
    pallas_call x1, Pallas kernels, apply(): pl.pallas_call(middle_kernel, in_specs=[hbm] + [vm] * 6, out_specs=[vm] *...  1.08 us
  transfers between devices with their start and end apart: 8, of which 4 were waited for; matrix products, arithmetic and copies ran while one was open for 0% of the time, Pallas kernels for 19%

profile of v6, /device:TPU:0, one launch (start us, length us, event | category | flops | bytes accessed | tf_op | source)
XLA Modules:
  0.0 28.4 jit_solution(16146365299525860681)
XLA Ops:
  0.0 2.0 %up.1 = (bf16[12,64,128]{2,1,0:T(8,128)(2,1)S(1)}, bf16[12,64,128]{2,1,0:T(8,128)(2,1)S(1)}, bf16[3,64,128]{2,1,0:T(8,128)(2,1)S(1)}, bf16[11,64,128]{2,1,0:T(8,...) custom-call(bf16[24,64,64]{2,1,0:T(8,128)(2,1)} %bitcast.31, ...), custom_call_target="tpu_custom_call" | custom-call | flops 30000000 | bytes 4000000 | tf_op jit(solution)/shard_map/up/pallas_call | solution.py:276
  2.0 3.0 %collective-permute-start = (bf16[64,64]{1,0:T(8,128)(2,1)S(1)}, bf16[64,64]{1,0:T(8,128)(2,1)S(1)}, u32[]{:S(2)}, u32[]{:S(2)}) collective-permute-start(bf16[64,64]{1,0:T(8,128)(2,1)S(1)} %get-tuple-element.23), channel_id=1, source_target_pairs={{0,4},{1,5},{2,6},{3,7},{4,0},{5,1},{6,2},{7,3},{8,12},{9,13},{10,... | collective-permute-start | bytes 24584 | tf_op jit(solution)/shard_map/ppermute | solution.py:294
  5.0 1.7 %collective-permute-done = bf16[64,64]{1,0:T(8,128)(2,1)S(1)} collective-permute-done((bf16[64,64]{1,0:T(8,128)(2,1)S(1)}, bf16[64,64]{1,0:T(8,128)(2,1)S(1)}, u32[]{:S(2)}, u32[]{:S(2)}) %collective-permute-start) | collective-permute-done | bytes 8224 | tf_op jit(solution)/shard_map/ppermute | solution.py:294
  6.7 2.1 %collective-permute-start.1 = (bf16[64,64]{1,0:T(8,128)(2,1)S(1)}, bf16[64,64]{1,0:T(8,128)(2,1)S(1)}, u32[]{:S(2)}, u32[]{:S(2)}) collective-permute-start(bf16[64,64]{1,0:T(8,128)(2,1)S(1)} %add_convert_fusion.1), channel_id=1, source_target_pairs={{0,2},{1,3},{2,0},{3,1},{4,6},{5,7},{6,4},{7,5},{8,10},{9,11},{10,... | collective-permute-start | bytes 24584 | tf_op jit(solution)/shard_map/ppermute | solution.py:294
  8.8 1.7 %collective-permute-done.1 = bf16[64,64]{1,0:T(8,128)(2,1)S(1)} collective-permute-done((bf16[64,64]{1,0:T(8,128)(2,1)S(1)}, bf16[64,64]{1,0:T(8,128)(2,1)S(1)}, u32[]{:S(2)}, u32[]{:S(2)}) %collective-permute-start.1) | collective-permute-done | bytes 8224 | tf_op jit(solution)/shard_map/ppermute | solution.py:294
  10.6 2.1 %collective-permute-start.2 = (bf16[2,64,64]{2,1,0:T(8,128)(2,1)S(1)}, bf16[2,64,64]{2,1,0:T(8,128)(2,1)S(1)}, u32[]{:S(2)}, u32[]{:S(2)}) collective-permute-start(bf16[2,64,64]{2,1,0:T(8,128)(2,1)S(1)} %pad_maximum_fusion), channel_id=1, source_target_pairs={{0,8},{1,9},{2,10},{3,11},{4,12},{5,13},{6,14},{7,15},{8,0},{9,1},... | collective-permute-start | bytes 49160 | tf_op jit(solution)/shard_map/ppermute | solution.py:294
  12.7 2.6 %collective-permute-start.3 = (bf16[2,64,64]{2,1,0:T(8,128)(2,1)S(1)}, bf16[2,64,64]{2,1,0:T(8,128)(2,1)S(1)}, u32[]{:S(2)}, u32[]{:S(2)}) collective-permute-start(bf16[2,64,64]{2,1,0:T(8,128)(2,1)S(1)} %pad_maximum_fusion), channel_id=1, source_target_pairs={{0,16},{1,17},{2,18},{3,19},{4,20},{5,21},{6,22},{7,23},{8,24},{9,... | collective-permute-start | bytes 49160 | tf_op jit(solution)/shard_map/ppermute | solution.py:294
  15.3 0.0 collective-permute-start.4
  15.3 1.7 %collective-permute-start.6 = (bf16[11,64,128]{2,1,0:T(8,128)(2,1)S(1)}, bf16[11,64,128]{2,1,0:T(8,128)(2,1)S(1)}, u32[]{:S(2)}, u32[]{:S(2)}) collective-permute-start(bf16[11,64,128]{2,1,0:T(8,128)(2,1)S(1)} %get-tuple-element.25), channel_id=1, source_target_pairs={{0,4},{4,0},{8,12},{12,8},{16,20},{20,16},{24,28},{28,24},{1,5},{5... | collective-permute-start | bytes 540680 | tf_op jit(solution)/shard_map/ppermute | solution.py:296
  17.0 0.0 collective-permute-start.7
  17.0 0.0 collective-permute-done.2
  17.0 1.3 %collective-permute-done.3 = bf16[2,64,64]{2,1,0:T(8,128)(2,1)S(1)} collective-permute-done((bf16[2,64,64]{2,1,0:T(8,128)(2,1)S(1)}, bf16[2,64,64]{2,1,0:T(8,128)(2,1)S(1)}, u32[]{:S(2)}, u32[]{:S(2)}) %collective-permute-start.3) | collective-permute-done | bytes 16416 | tf_op jit(solution)/shard_map/ppermute | solution.py:294
  18.3 2.8 %collective-permute-done.4 = bf16[2,64,64]{2,1,0:T(8,128)(2,1)S(1)} collective-permute-done((bf16[2,64,64]{2,1,0:T(8,128)(2,1)S(1)}, bf16[2,64,64]{2,1,0:T(8,128)(2,1)S(1)}, u32[]{:S(2)}, u32[]{:S(2)}) %collective-permute-start.4) | collective-permute-done | bytes 16416 | tf_op jit(solution)/shard_map/ppermute | solution.py:294
  21.2 0.1 collective-permute-start.5
  21.2 0.0 copy-start
  21.2 0.0 copy-start.3
  21.3 0.0 copy-start.5
  21.3 2.1 %inner.1 = (f32[8,64,64]{2,1,0:T(8,128)S(1)}, f32[8,64,64]{2,1,0:T(8,128)S(1)}, bf16[26,64,128]{2,1,0:T(8,128)(2,1)S(1)}, bf16[24,64,128]{2,1,0:T(8,128)(2,1)S(1...) custom-call(s32[8,24]{1,0:T(8,128)} %bitcast.40, s32[1,24]{1,0:T(1,128)} %count_hbm.3, ...), custom_call_target="tpu_custom_call" | custom-call | flops 60000000 | bytes 6000000 | tf_op jit(solution)/shard_map/inner/pallas_call | solution.py:318
  23.5 1.1 %middle.1 = (f32[6,64,64]{2,1,0:T(8,128)S(1)}, bf16[384,64]{1,0:T(8,128)(2,1)S(1)}) custom-call(s32[6,1,6]{2,1,0:T(1,128)} %bitcast.44, bf16[3,64,128]{2,1,0:T(8,128)(2,1)S(1)} %get-tuple-element.24.mp_ref, bf16[11,64,128]{2,1,0:T(8,128)(2,1)S(1)} %collective-permute-done.6.f0_ref, bf16[11,64,128]{2,1,0:T(8,128)(2,1)S(1)} %collective-permute-done.7.f1_ref, ...), custom_call_target="tpu_custom_call" | custom-call | flops 20000000 | bytes 3000000 | tf_op jit(solution)/shard_map/middle/pallas_call | solution.py:347
  24.6 0.0 copy-start.1
  24.6 0.0 copy-start.2
  24.6 0.0 copy-start.4
  24.6 2.2 %outer.1 = (f32[16,64,64]{2,1,0:T(8,128)S(1)}, f32[16,64,64]{2,1,0:T(8,128)S(1)}) custom-call(s32[8,24]{1,0:T(8,128)} %bitcast.41, s32[1,24]{1,0:T(1,128)} %count_hbm.3, s32[6,1,24]{2,1,0:T(1,128)} %bitcast.43, bf16[26,64,128]{2,1,0:T(8,128)(2,1)S(1)} %get-tuple-element.34.c2_ref, bf16[24,64,128]{2,1,0:T(8,128)(2,1)S(1)} %get-tuple-element.35.s2_ref, ...), custom_call_target="tpu_custom_call" | custom-call | flops 140000000 | bytes 8000000 | tf_op jit(solution)/shard_map/outer/pallas_call | solution.py:332
  26.8 1.5 %down.1 = bf16[24,64,64]{2,1,0:T(8,128)(2,1)} custom-call(bf16[2,64,64]{2,1,0:T(8,128)(2,1)S(1)} %add_convert_fusion.own_ref, bf16[2,64,64]{2,1,0:T(8,128)(2,1)S(1)} %collective-permute-done.5.over_ref, bf16[4,64,64]{2,1,0:T(8,128)(2,1)S(1)} %bitcast.25, bf16[384,64]{1,0:T(8,128)(2,1)S(1)} %get-tuple-element.27.both_ref, bf16[24,64,64]{2,1,0:T(8,128)(2,1)S(1)} %bitcast.22, ...), custom_call_target="tpu_custom_call" | custom-call | flops 30000000 | bytes 4000000 | tf_op jit(solution)/shard_map/down/pallas_call | solution.py:360
  (12 shorter events, 0.1 us)
Async XLA Ops:
  2.0 4.8 %collective-permute-start = (bf16[64,64]{1,0:T(8,128)(2,1)S(1)}, bf16[64,64]{1,0:T(8,128)(2,1)S(1)}, u32[]{:S(2)}, u32[]{:S(2)}) collective-permute-start(bf16[64,64]{1,0:T(8,128)(2,1)S(1)} %get-tuple-element.23), channel_id=1, source_target_pairs={{0,4},{1,5},{2,6},{3,7},{4,0},{5,1},{6,2},{7,3},{8,12},{9,13},{10,... | collective-permute-start | bytes 24584 | tf_op jit(solution)/shard_map/ppermute | solution.py:294
  6.7 3.8 %collective-permute-start.1 = (bf16[64,64]{1,0:T(8,128)(2,1)S(1)}, bf16[64,64]{1,0:T(8,128)(2,1)S(1)}, u32[]{:S(2)}, u32[]{:S(2)}) collective-permute-start(bf16[64,64]{1,0:T(8,128)(2,1)S(1)} %add_convert_fusion.1), channel_id=1, source_target_pairs={{0,2},{1,3},{2,0},{3,1},{4,6},{5,7},{6,4},{7,5},{8,10},{9,11},{10,... | collective-permute-start | bytes 24584 | tf_op jit(solution)/shard_map/ppermute | solution.py:294
  10.6 6.5 %collective-permute-start.2 = (bf16[2,64,64]{2,1,0:T(8,128)(2,1)S(1)}, bf16[2,64,64]{2,1,0:T(8,128)(2,1)S(1)}, u32[]{:S(2)}, u32[]{:S(2)}) collective-permute-start(bf16[2,64,64]{2,1,0:T(8,128)(2,1)S(1)} %pad_maximum_fusion), channel_id=1, source_target_pairs={{0,8},{1,9},{2,10},{3,11},{4,12},{5,13},{6,14},{7,15},{8,0},{9,1},... | collective-permute-start | bytes 49160 | tf_op jit(solution)/shard_map/ppermute | solution.py:294
  12.7 5.6 %collective-permute-start.3 = (bf16[2,64,64]{2,1,0:T(8,128)(2,1)S(1)}, bf16[2,64,64]{2,1,0:T(8,128)(2,1)S(1)}, u32[]{:S(2)}, u32[]{:S(2)}) collective-permute-start(bf16[2,64,64]{2,1,0:T(8,128)(2,1)S(1)} %pad_maximum_fusion), channel_id=1, source_target_pairs={{0,16},{1,17},{2,18},{3,19},{4,20},{5,21},{6,22},{7,23},{8,24},{9,... | collective-permute-start | bytes 49160 | tf_op jit(solution)/shard_map/ppermute | solution.py:294
  15.3 5.8 %collective-permute-start.4 = (bf16[2,64,64]{2,1,0:T(8,128)(2,1)S(1)}, bf16[2,64,64]{2,1,0:T(8,128)(2,1)S(1)}, u32[]{:S(2)}, u32[]{:S(2)}) collective-permute-start(bf16[2,64,64]{2,1,0:T(8,128)(2,1)S(1)} %pad_maximum_fusion), channel_id=1, source_target_pairs={{0,24},{1,25},{2,26},{3,27},{4,28},{5,29},{6,30},{7,31},{8,16},{9,... | collective-permute-start | bytes 49160 | tf_op jit(solution)/shard_map/ppermute | solution.py:294
  15.3 8.1 %collective-permute-start.6 = (bf16[11,64,128]{2,1,0:T(8,128)(2,1)S(1)}, bf16[11,64,128]{2,1,0:T(8,128)(2,1)S(1)}, u32[]{:S(2)}, u32[]{:S(2)}) collective-permute-start(bf16[11,64,128]{2,1,0:T(8,128)(2,1)S(1)} %get-tuple-element.25), channel_id=1, source_target_pairs={{0,4},{4,0},{8,12},{12,8},{16,20},{20,16},{24,28},{28,24},{1,5},{5... | collective-permute-start | bytes 540680 | tf_op jit(solution)/shard_map/ppermute | solution.py:296
  17.0 6.4 %collective-permute-start.7 = (bf16[11,64,128]{2,1,0:T(8,128)(2,1)S(1)}, bf16[11,64,128]{2,1,0:T(8,128)(2,1)S(1)}, u32[]{:S(2)}, u32[]{:S(2)}) collective-permute-start(bf16[11,64,128]{2,1,0:T(8,128)(2,1)S(1)} %get-tuple-element.26), channel_id=1, source_target_pairs={{0,1},{1,0},{2,3},{3,2},{4,8},{5,9},{6,10},{7,11},{8,4},{9,5},{10,... | collective-permute-start | bytes 540680 | tf_op jit(solution)/shard_map/ppermute | solution.py:298
  21.2 5.6 %collective-permute-start.5 = (bf16[2,64,64]{2,1,0:T(8,128)(2,1)S(1)}, bf16[2,64,64]{2,1,0:T(8,128)(2,1)S(1)}, u32[]{:S(2)}, u32[]{:S(2)}) collective-permute-start(bf16[2,64,64]{2,1,0:T(8,128)(2,1)S(1)} %add_convert_fusion.own_ref), channel_id=1, source_target_pairs={{0,1},{1,0},{2,3},{3,2},{4,5},{5,4},{6,7},{7,6},{8,9},{9,8},{10,11... | collective-permute-start | bytes 49160 | tf_op jit(solution)/shard_map/ppermute | solution.py:294
  21.2 2.2 %copy-start = (bf16[1,6,6,64,64]{4,3,2,1,0:T(8,128)(2,1)S(1)}, bf16[1,6,6,64,64]{4,3,2,1,0:T(8,128)(2,1)}, u32[]{:S(2)}) copy-start(bf16[1,6,6,64,64]{4,3,2,1,0:T(8,128)(2,1)} %param.27) | copy-start | bytes 884740
  21.2 2.2 %copy-start.3 = (bf16[1,6,64,64]{3,2,1,0:T(8,128)(2,1)S(1)}, bf16[1,6,64,64]{3,2,1,0:T(8,128)(2,1)}, u32[]{:S(2)}) copy-start(bf16[1,6,64,64]{3,2,1,0:T(8,128)(2,1)} %param.30) | copy-start | bytes 147460
  21.3 2.2 %copy-start.5 = (bf16[1,1,64,64]{3,2,1,0:T(8,128)(2,1)S(1)}, bf16[1,1,64,64]{3,2,1,0:T(8,128)(2,1)}, u32[]{:S(2)}) copy-start(bf16[1,1,64,64]{3,2,1,0:T(8,128)(2,1)} %param.32) | copy-start | bytes 24580
  24.6 2.3 %copy-start.1 = (bf16[1,24,64,64]{3,2,1,0:T(8,128)(2,1)S(1)}, bf16[1,24,64,64]{3,2,1,0:T(8,128)(2,1)}, u32[]{:S(2)}) copy-start(bf16[1,24,64,64]{3,2,1,0:T(8,128)(2,1)} %param.26) | copy-start | bytes 589828
  24.6 2.3 %copy-start.2 = (bf16[1,24,64,64]{3,2,1,0:T(8,128)(2,1)S(1)}, bf16[1,24,64,64]{3,2,1,0:T(8,128)(2,1)}, u32[]{:S(2)}) copy-start(bf16[1,24,64,64]{3,2,1,0:T(8,128)(2,1)} %param.19) | copy-start | bytes 589828
  24.6 2.2 %copy-start.4 = (bf16[1,4,64,64]{3,2,1,0:T(8,128)(2,1)S(1)}, bf16[1,4,64,64]{3,2,1,0:T(8,128)(2,1)}, u32[]{:S(2)}) copy-start(bf16[1,4,64,64]{3,2,1,0:T(8,128)(2,1)} %param.33) | copy-start | bytes 98308
